TPU v7x, 256 devices: a whole 4x4x8 slice. The times are simulated.
256 devices in a mesh: outer: 2 (over core), inner: 32 (over z, x), head: 4 (over y).
Axes of the slice: x: 4, y: 4, z: 8, core: 2. Of those that a mesh axis runs over, the one named last changes fastest.
Arguments:
- queries: bfloat16 [512, 64, 128], P('inner', 'head'), may hold values from -20 to 20
- keys: bfloat16 [131072, 8, 128], P(('outer', 'inner'), 'head'), may hold values from -15 to 15
- values: bfloat16 [131072, 8, 128], P(('outer', 'inner'), 'head'), may hold values from -6 to 6
- doc_lengths: int32 [32], replicated, may hold values from 1 to 256, 1024 in all
Outputs:
- attended: bfloat16 [512, 64, 128], P('inner', 'head')
All inputs are finite; a program needn't handle non-finite values.
Results may differ from a plain program's by a relative error of at most 0.003.
Values may be sent and summed in bfloat16 or wider, within the bound.
No kernel may reach another device: no remote copies, remote signals or barrier semaphores. Data moves between devices by JAX's collectives and lax.ppermute only.
A program may use at most 256 MiB of HBM per device.

v0:
```python
import jax
import jax.numpy as jnp
from jax import lax
from jax.sharding import PartitionSpec as P

BLOCK = 128


NEGATIVE = -1e30


def from_behind(shard, axis, by):
    size = lax.axis_size(axis)
    return lax.ppermute(shard, axis, [(i, (i + by) % size) for i in range(size)])


def merged_2(shard, axis, combine):
    everything = jax.tree.map(lambda part: lax.all_gather(part, axis), shard)
    leading = jax.tree.map(lambda part: part[0], everything)

    def step(k, so_far):
        return combine(so_far, jax.tree.map(lambda part: part[k], everything))

    return lax.fori_loop(1, lax.axis_size(axis), step, leading)


def document_of(positions, doc_lengths):
    boundary = BLOCK * jnp.cumsum(doc_lengths)
    return jnp.sum((boundary[None, :] <= positions[:, None]).astype(jnp.int32), axis=1)


def absorb(running, partial_value):
    row_peak = jnp.maximum(running[0], partial_value[0])
    old_factor = jnp.exp(running[0] - row_peak)
    new_factor = jnp.exp(partial_value[0] - row_peak)
    row_total = running[1] * old_factor + partial_value[1] * new_factor
    output = running[2] * old_factor[..., None] + partial_value[2] * new_factor[..., None]
    return (row_peak, row_total, output)


def attend_tile(query_tile, key_tile, value_tile, alive_mask, score_scale):
    scores = (
        jnp.einsum("rhgd,shd->rhgs", query_tile, key_tile, preferred_element_type=jnp.float32)
        * score_scale
    )
    scores = jnp.where(alive_mask[:, None, None, :], scores, NEGATIVE)
    row_peak = jnp.max(scores, axis=3)
    weights = jnp.where(alive_mask[:, None, None, :], jnp.exp(scores - row_peak[..., None]), 0.0)
    row_total = jnp.sum(weights, axis=3)
    output = jnp.einsum(
        "rhgs,shd->rhgd",
        weights.astype(jnp.bfloat16),
        value_tile,
        preferred_element_type=jnp.float32,
    )
    return (row_peak, row_total, output)


def body(queries, keys, values, doc_lengths):
    cycle_size = lax.axis_size("inner")
    group_count = lax.axis_size("outer")
    inner_index = lax.axis_index("inner")
    outer_index = lax.axis_index("outer")
    query_rows, head_count, head_dim = queries.shape
    key_rows = keys.shape[0]
    kv_count = keys.shape[1]
    sharing = head_count // kv_count
    tail_len = query_rows // group_count
    score_scale = head_dim ** (-0.5)
    grouped = queries.reshape(query_rows, kv_count, sharing, head_dim)
    key_offsets = jnp.arange(key_rows, dtype=jnp.int32)
    running = (
        jnp.full((query_rows, kv_count, sharing), NEGATIVE, jnp.float32),
        jnp.zeros((query_rows, kv_count, sharing), jnp.float32),
        jnp.zeros((query_rows, kv_count, sharing, head_dim), jnp.float32),
    )
    own_keys = (outer_index * cycle_size + inner_index) * key_rows + key_offsets
    moving = grouped
    for turn_index in range(cycle_size):
        anchor = (inner_index - turn_index) % cycle_size
        starts = (
            (jnp.arange(group_count, dtype=jnp.int32)[:, None] * cycle_size + anchor) * key_rows
            + key_rows
            - tail_len
        )
        query_pos = (starts + jnp.arange(tail_len, dtype=jnp.int32)[None, :]).reshape(-1)
        query_doc = document_of(query_pos, doc_lengths)
        key_doc = document_of(own_keys, doc_lengths)
        alive_mask = (own_keys[None, :] <= query_pos[:, None]) & (
            key_doc[None, :] == query_doc[:, None]
        )
        running = absorb(running, attend_tile(moving, keys, values, alive_mask, score_scale))
        if turn_index + 1 < cycle_size:
            moving = from_behind(moving, "inner", 1)
            running = from_behind((running[0], running[1], running[2]), "inner", 1)
    running = from_behind((running[0], running[1], running[2]), "inner", 1)
    merged = merged_2((running[0], running[1], running[2]), "outer", absorb)
    result = (merged[2] / merged[1][..., None]).astype(jnp.bfloat16)
    return result.reshape(query_rows, head_count, head_dim)


def solution(mesh):
    placed = (
        P("inner", "head", None),
        P(("outer", "inner"), "head", None),
        P(("outer", "inner"), "head", None),
        P(),
    )
    return jax.shard_map(
        body, mesh=mesh, in_specs=placed, out_specs=P("inner", "head", None), check_vma=False
    )
```

profile of v0, /device:TPU:1, one launch (start us, length us, event | category | flops | bytes accessed | tf_op | source)
XLA Modules:
  0.0 440.3 jit_solution(11502069548374005445)
XLA Ops:
  0.0 0.9 copy.756
  1.0 2.1 collective-permute-start.2
  8.7 0.7 copy.755
  11.0 1.8 fusion.398
  13.3 1.3 collective-permute-start.1
  14.6 0.9 collective-permute-start.95
  16.2 1.6 collective-permute-start
  19.8 1.3 collective-permute-start.5
  21.6 0.8 collective-permute-start.96
  22.3 1.1 collective-permute-start.4
  23.4 2.8 collective-permute-done.5
  28.8 1.1 collective-permute-start.97
  29.9 2.5 collective-permute-start.7
  32.5 4.0 collective-permute-done.8
  38.5 6.2 %collective-permute-done.11 = bf16[16,2,8,128]{3,0,2,1:T(8,128)(2,1)S(1)} collective-permute-done((bf16[16,2,8,128]{3,0,2,1:T(8,128)(2,1)S(1)}, bf16[16,2,8,128]{3,0,2,1:T(8,128)(2,1)S(1)}, u32[]{:S(2)}, u32[]{:S(2)}) %collective-permute-start.11) | collective-permute-done | bytes 65568 | tf_op jit(solution)/shard_map/ppermute | solution.py:14
  47.2 1.1 collective-permute-start.13
  48.3 6.1 %collective-permute-done.14 = bf16[16,2,8,128]{3,0,2,1:T(8,128)(2,1)S(1)} collective-permute-done((bf16[16,2,8,128]{3,0,2,1:T(8,128)(2,1)S(1)}, bf16[16,2,8,128]{3,0,2,1:T(8,128)(2,1)S(1)}, u32[]{:S(2)}, u32[]{:S(2)}) %collective-permute-start.14) | collective-permute-done | bytes 65568 | tf_op jit(solution)/shard_map/ppermute | solution.py:14
  56.7 6.2 %collective-permute-done.17 = bf16[16,2,8,128]{3,0,2,1:T(8,128)(2,1)S(1)} collective-permute-done((bf16[16,2,8,128]{3,0,2,1:T(8,128)(2,1)S(1)}, bf16[16,2,8,128]{3,0,2,1:T(8,128)(2,1)S(1)}, u32[]{:S(2)}, u32[]{:S(2)}) %collective-permute-start.17) | collective-permute-done | bytes 65568 | tf_op jit(solution)/shard_map/ppermute | solution.py:14
  64.9 7.2 %collective-permute-done.20 = bf16[16,2,8,128]{3,0,2,1:T(8,128)(2,1)S(1)} collective-permute-done((bf16[16,2,8,128]{3,0,2,1:T(8,128)(2,1)S(1)}, bf16[16,2,8,128]{3,0,2,1:T(8,128)(2,1)S(1)}, u32[]{:S(2)}, u32[]{:S(2)}) %collective-permute-start.20) | collective-permute-done | bytes 65568 | tf_op jit(solution)/shard_map/ppermute | solution.py:14
  74.2 6.0 %collective-permute-done.23 = bf16[16,2,8,128]{3,0,2,1:T(8,128)(2,1)S(1)} collective-permute-done((bf16[16,2,8,128]{3,0,2,1:T(8,128)(2,1)S(1)}, bf16[16,2,8,128]{3,0,2,1:T(8,128)(2,1)S(1)}, u32[]{:S(2)}, u32[]{:S(2)}) %collective-permute-start.23) | collective-permute-done | bytes 65568 | tf_op jit(solution)/shard_map/ppermute | solution.py:14
  82.5 8.3 %collective-permute-done.26 = bf16[16,2,8,128]{3,0,2,1:T(8,128)(2,1)S(1)} collective-permute-done((bf16[16,2,8,128]{3,0,2,1:T(8,128)(2,1)S(1)}, bf16[16,2,8,128]{3,0,2,1:T(8,128)(2,1)S(1)}, u32[]{:S(2)}, u32[]{:S(2)}) %collective-permute-start.26) | collective-permute-done | bytes 65568 | tf_op jit(solution)/shard_map/ppermute | solution.py:14
  92.8 7.1 %collective-permute-done.29 = bf16[16,2,8,128]{3,0,2,1:T(8,128)(2,1)S(1)} collective-permute-done((bf16[16,2,8,128]{3,0,2,1:T(8,128)(2,1)S(1)}, bf16[16,2,8,128]{3,0,2,1:T(8,128)(2,1)S(1)}, u32[]{:S(2)}, u32[]{:S(2)}) %collective-permute-start.29) | collective-permute-done | bytes 65568 | tf_op jit(solution)/shard_map/ppermute | solution.py:14
  102.5 6.2 %collective-permute-done.32 = bf16[16,2,8,128]{3,0,2,1:T(8,128)(2,1)S(1)} collective-permute-done((bf16[16,2,8,128]{3,0,2,1:T(8,128)(2,1)S(1)}, bf16[16,2,8,128]{3,0,2,1:T(8,128)(2,1)S(1)}, u32[]{:S(2)}, u32[]{:S(2)}) %collective-permute-start.32) | collective-permute-done | bytes 65568 | tf_op jit(solution)/shard_map/ppermute | solution.py:14
  110.7 6.2 %collective-permute-done.35 = bf16[16,2,8,128]{3,0,2,1:T(8,128)(2,1)S(1)} collective-permute-done((bf16[16,2,8,128]{3,0,2,1:T(8,128)(2,1)S(1)}, bf16[16,2,8,128]{3,0,2,1:T(8,128)(2,1)S(1)}, u32[]{:S(2)}, u32[]{:S(2)}) %collective-permute-start.35) | collective-permute-done | bytes 65568 | tf_op jit(solution)/shard_map/ppermute | solution.py:14
  119.2 6.2 %collective-permute-done.38 = bf16[16,2,8,128]{3,0,2,1:T(8,128)(2,1)S(1)} collective-permute-done((bf16[16,2,8,128]{3,0,2,1:T(8,128)(2,1)S(1)}, bf16[16,2,8,128]{3,0,2,1:T(8,128)(2,1)S(1)}, u32[]{:S(2)}, u32[]{:S(2)}) %collective-permute-start.38) | collective-permute-done | bytes 65568 | tf_op jit(solution)/shard_map/ppermute | solution.py:14
  127.5 6.0 %collective-permute-done.41 = bf16[16,2,8,128]{3,0,2,1:T(8,128)(2,1)S(1)} collective-permute-done((bf16[16,2,8,128]{3,0,2,1:T(8,128)(2,1)S(1)}, bf16[16,2,8,128]{3,0,2,1:T(8,128)(2,1)S(1)}, u32[]{:S(2)}, u32[]{:S(2)}) %collective-permute-start.41) | collective-permute-done | bytes 65568 | tf_op jit(solution)/shard_map/ppermute | solution.py:14
  135.8 6.2 %collective-permute-done.44 = bf16[16,2,8,128]{3,0,2,1:T(8,128)(2,1)S(1)} collective-permute-done((bf16[16,2,8,128]{3,0,2,1:T(8,128)(2,1)S(1)}, bf16[16,2,8,128]{3,0,2,1:T(8,128)(2,1)S(1)}, u32[]{:S(2)}, u32[]{:S(2)}) %collective-permute-start.44) | collective-permute-done | bytes 65568 | tf_op jit(solution)/shard_map/ppermute | solution.py:14
  144.0 6.2 %collective-permute-done.47 = bf16[16,2,8,128]{3,0,2,1:T(8,128)(2,1)S(1)} collective-permute-done((bf16[16,2,8,128]{3,0,2,1:T(8,128)(2,1)S(1)}, bf16[16,2,8,128]{3,0,2,1:T(8,128)(2,1)S(1)}, u32[]{:S(2)}, u32[]{:S(2)}) %collective-permute-start.47) | collective-permute-done | bytes 65568 | tf_op jit(solution)/shard_map/ppermute | solution.py:14
  152.9 7.1 %collective-permute-done.50 = bf16[16,2,8,128]{3,0,2,1:T(8,128)(2,1)S(1)} collective-permute-done((bf16[16,2,8,128]{3,0,2,1:T(8,128)(2,1)S(1)}, bf16[16,2,8,128]{3,0,2,1:T(8,128)(2,1)S(1)}, u32[]{:S(2)}, u32[]{:S(2)}) %collective-permute-start.50) | collective-permute-done | bytes 65568 | tf_op jit(solution)/shard_map/ppermute | solution.py:14
  162.7 6.5 %collective-permute-done.53 = bf16[16,2,8,128]{3,0,2,1:T(8,128)(2,1)S(1)} collective-permute-done((bf16[16,2,8,128]{3,0,2,1:T(8,128)(2,1)S(1)}, bf16[16,2,8,128]{3,0,2,1:T(8,128)(2,1)S(1)}, u32[]{:S(2)}, u32[]{:S(2)}) %collective-permute-start.53) | collective-permute-done | bytes 65568 | tf_op jit(solution)/shard_map/ppermute | solution.py:14
  171.2 6.2 %collective-permute-done.56 = bf16[16,2,8,128]{3,0,2,1:T(8,128)(2,1)S(1)} collective-permute-done((bf16[16,2,8,128]{3,0,2,1:T(8,128)(2,1)S(1)}, bf16[16,2,8,128]{3,0,2,1:T(8,128)(2,1)S(1)}, u32[]{:S(2)}, u32[]{:S(2)}) %collective-permute-start.56) | collective-permute-done | bytes 65568 | tf_op jit(solution)/shard_map/ppermute | solution.py:14
  179.8 6.2 %collective-permute-done.59 = bf16[16,2,8,128]{3,0,2,1:T(8,128)(2,1)S(1)} collective-permute-done((bf16[16,2,8,128]{3,0,2,1:T(8,128)(2,1)S(1)}, bf16[16,2,8,128]{3,0,2,1:T(8,128)(2,1)S(1)}, u32[]{:S(2)}, u32[]{:S(2)}) %collective-permute-start.59) | collective-permute-done | bytes 65568 | tf_op jit(solution)/shard_map/ppermute | solution.py:14
  188.0 6.2 %collective-permute-done.62 = bf16[16,2,8,128]{3,0,2,1:T(8,128)(2,1)S(1)} collective-permute-done((bf16[16,2,8,128]{3,0,2,1:T(8,128)(2,1)S(1)}, bf16[16,2,8,128]{3,0,2,1:T(8,128)(2,1)S(1)}, u32[]{:S(2)}, u32[]{:S(2)}) %collective-permute-start.62) | collective-permute-done | bytes 65568 | tf_op jit(solution)/shard_map/ppermute | solution.py:14
  196.5 6.2 %collective-permute-done.65 = bf16[16,2,8,128]{3,0,2,1:T(8,128)(2,1)S(1)} collective-permute-done((bf16[16,2,8,128]{3,0,2,1:T(8,128)(2,1)S(1)}, bf16[16,2,8,128]{3,0,2,1:T(8,128)(2,1)S(1)}, u32[]{:S(2)}, u32[]{:S(2)}) %collective-permute-start.65) | collective-permute-done | bytes 65568 | tf_op jit(solution)/shard_map/ppermute | solution.py:14
  205.1 5.8 %collective-permute-done.68 = bf16[16,2,8,128]{3,0,2,1:T(8,128)(2,1)S(1)} collective-permute-done((bf16[16,2,8,128]{3,0,2,1:T(8,128)(2,1)S(1)}, bf16[16,2,8,128]{3,0,2,1:T(8,128)(2,1)S(1)}, u32[]{:S(2)}, u32[]{:S(2)}) %collective-permute-start.68) | collective-permute-done | bytes 65568 | tf_op jit(solution)/shard_map/ppermute | solution.py:14
  213.0 0.7 collective-permute-start.36
  213.7 5.6 %collective-permute-done.71 = bf16[16,2,8,128]{3,0,2,1:T(8,128)(2,1)S(1)} collective-permute-done((bf16[16,2,8,128]{3,0,2,1:T(8,128)(2,1)S(1)}, bf16[16,2,8,128]{3,0,2,1:T(8,128)(2,1)S(1)}, u32[]{:S(2)}, u32[]{:S(2)}) %collective-permute-start.71) | collective-permute-done | bytes 65568 | tf_op jit(solution)/shard_map/ppermute | solution.py:14
  221.3 7.1 %collective-permute-done.74 = bf16[16,2,8,128]{3,0,2,1:T(8,128)(2,1)S(1)} collective-permute-done((bf16[16,2,8,128]{3,0,2,1:T(8,128)(2,1)S(1)}, bf16[16,2,8,128]{3,0,2,1:T(8,128)(2,1)S(1)}, u32[]{:S(2)}, u32[]{:S(2)}) %collective-permute-start.74) | collective-permute-done | bytes 65568 | tf_op jit(solution)/shard_map/ppermute | solution.py:14
  230.8 7.1 %collective-permute-done.77 = bf16[16,2,8,128]{3,0,2,1:T(8,128)(2,1)S(1)} collective-permute-done((bf16[16,2,8,128]{3,0,2,1:T(8,128)(2,1)S(1)}, bf16[16,2,8,128]{3,0,2,1:T(8,128)(2,1)S(1)}, u32[]{:S(2)}, u32[]{:S(2)}) %collective-permute-start.77) | collective-permute-done | bytes 65568 | tf_op jit(solution)/shard_map/ppermute | solution.py:14
  239.9 6.6 %collective-permute-done.80 = bf16[16,2,8,128]{3,0,2,1:T(8,128)(2,1)S(1)} collective-permute-done((bf16[16,2,8,128]{3,0,2,1:T(8,128)(2,1)S(1)}, bf16[16,2,8,128]{3,0,2,1:T(8,128)(2,1)S(1)}, u32[]{:S(2)}, u32[]{:S(2)}) %collective-permute-start.80) | collective-permute-done | bytes 65568 | tf_op jit(solution)/shard_map/ppermute | solution.py:14
  248.8 6.2 %collective-permute-done.83 = bf16[16,2,8,128]{3,0,2,1:T(8,128)(2,1)S(1)} collective-permute-done((bf16[16,2,8,128]{3,0,2,1:T(8,128)(2,1)S(1)}, bf16[16,2,8,128]{3,0,2,1:T(8,128)(2,1)S(1)}, u32[]{:S(2)}, u32[]{:S(2)}) %collective-permute-start.83) | collective-permute-done | bytes 65568 | tf_op jit(solution)/shard_map/ppermute | solution.py:14
  256.2 1.0 collective-permute-done.42
  258.3 6.6 %collective-permute-done.45 = f32[16,2,8,128]{3,0,2,1:T(8,128)S(1)} collective-permute-done((f32[16,2,8,128]{3,0,2,1:T(8,128)S(1)}, f32[16,2,8,128]{3,0,2,1:T(8,128)S(1)}, u32[]{:S(2)}, u32[]{:S(2)}) %collective-permute-start.45) | collective-permute-done | bytes 131104 | tf_op jit(solution)/shard_map/ppermute | solution.py:14
  265.5 6.8 %collective-permute-done.48 = f32[16,2,8,128]{3,0,2,1:T(8,128)S(1)} collective-permute-done((f32[16,2,8,128]{3,0,2,1:T(8,128)S(1)}, f32[16,2,8,128]{3,0,2,1:T(8,128)S(1)}, u32[]{:S(2)}, u32[]{:S(2)}) %collective-permute-start.48) | collective-permute-done | bytes 131104 | tf_op jit(solution)/shard_map/ppermute | solution.py:14
  272.5 0.7 collective-permute-done.86
  273.8 5.9 %collective-permute-done.51 = f32[16,2,8,128]{3,0,2,1:T(8,128)S(1)} collective-permute-done((f32[16,2,8,128]{3,0,2,1:T(8,128)S(1)}, f32[16,2,8,128]{3,0,2,1:T(8,128)S(1)}, u32[]{:S(2)}, u32[]{:S(2)}) %collective-permute-start.51) | collective-permute-done | bytes 131104 | tf_op jit(solution)/shard_map/ppermute | solution.py:14
  280.5 8.1 %collective-permute-done.54 = f32[16,2,8,128]{3,0,2,1:T(8,128)S(1)} collective-permute-done((f32[16,2,8,128]{3,0,2,1:T(8,128)S(1)}, f32[16,2,8,128]{3,0,2,1:T(8,128)S(1)}, u32[]{:S(2)}, u32[]{:S(2)}) %collective-permute-start.54) | collective-permute-done | bytes 131104 | tf_op jit(solution)/shard_map/ppermute | solution.py:14
  289.4 6.6 %collective-permute-done.57 = f32[16,2,8,128]{3,0,2,1:T(8,128)S(1)} collective-permute-done((f32[16,2,8,128]{3,0,2,1:T(8,128)S(1)}, f32[16,2,8,128]{3,0,2,1:T(8,128)S(1)}, u32[]{:S(2)}, u32[]{:S(2)}) %collective-permute-start.57) | collective-permute-done | bytes 131104 | tf_op jit(solution)/shard_map/ppermute | solution.py:14
  296.5 6.8 %collective-permute-done.60 = f32[16,2,8,128]{3,0,2,1:T(8,128)S(1)} collective-permute-done((f32[16,2,8,128]{3,0,2,1:T(8,128)S(1)}, f32[16,2,8,128]{3,0,2,1:T(8,128)S(1)}, u32[]{:S(2)}, u32[]{:S(2)}) %collective-permute-start.60) | collective-permute-done | bytes 131104 | tf_op jit(solution)/shard_map/ppermute | solution.py:14
  303.6 0.7 collective-permute-done.89
  304.8 5.9 %collective-permute-done.63 = f32[16,2,8,128]{3,0,2,1:T(8,128)S(1)} collective-permute-done((f32[16,2,8,128]{3,0,2,1:T(8,128)S(1)}, f32[16,2,8,128]{3,0,2,1:T(8,128)S(1)}, u32[]{:S(2)}, u32[]{:S(2)}) %collective-permute-start.63) | collective-permute-done | bytes 131104 | tf_op jit(solution)/shard_map/ppermute | solution.py:14
  311.7 6.5 %collective-permute-done.66 = f32[16,2,8,128]{3,0,2,1:T(8,128)S(1)} collective-permute-done((f32[16,2,8,128]{3,0,2,1:T(8,128)S(1)}, f32[16,2,8,128]{3,0,2,1:T(8,128)S(1)}, u32[]{:S(2)}, u32[]{:S(2)}) %collective-permute-start.66) | collective-permute-done | bytes 131104 | tf_op jit(solution)/shard_map/ppermute | solution.py:14
  319.0 6.6 %collective-permute-done.69 = f32[16,2,8,128]{3,0,2,1:T(8,128)S(1)} collective-permute-done((f32[16,2,8,128]{3,0,2,1:T(8,128)S(1)}, f32[16,2,8,128]{3,0,2,1:T(8,128)S(1)}, u32[]{:S(2)}, u32[]{:S(2)}) %collective-permute-start.69) | collective-permute-done | bytes 131104 | tf_op jit(solution)/shard_map/ppermute | solution.py:14
  326.1 6.8 %collective-permute-done.72 = f32[16,2,8,128]{3,0,2,1:T(8,128)S(1)} collective-permute-done((f32[16,2,8,128]{3,0,2,1:T(8,128)S(1)}, f32[16,2,8,128]{3,0,2,1:T(8,128)S(1)}, u32[]{:S(2)}, u32[]{:S(2)}) %collective-permute-start.72) | collective-permute-done | bytes 131104 | tf_op jit(solution)/shard_map/ppermute | solution.py:14
  333.2 0.7 collective-permute-done.92
  334.4 7.6 %collective-permute-done.75 = f32[16,2,8,128]{3,0,2,1:T(8,128)S(1)} collective-permute-done((f32[16,2,8,128]{3,0,2,1:T(8,128)S(1)}, f32[16,2,8,128]{3,0,2,1:T(8,128)S(1)}, u32[]{:S(2)}, u32[]{:S(2)}) %collective-permute-start.75) | collective-permute-done | bytes 131104 | tf_op jit(solution)/shard_map/ppermute | solution.py:14
  342.7 8.1 %collective-permute-done.78 = f32[16,2,8,128]{3,0,2,1:T(8,128)S(1)} collective-permute-done((f32[16,2,8,128]{3,0,2,1:T(8,128)S(1)}, f32[16,2,8,128]{3,0,2,1:T(8,128)S(1)}, u32[]{:S(2)}, u32[]{:S(2)}) %collective-permute-start.78) | collective-permute-done | bytes 131104 | tf_op jit(solution)/shard_map/ppermute | solution.py:14
  351.1 7.4 %collective-permute-done.81 = f32[16,2,8,128]{3,0,2,1:T(8,128)S(1)} collective-permute-done((f32[16,2,8,128]{3,0,2,1:T(8,128)S(1)}, f32[16,2,8,128]{3,0,2,1:T(8,128)S(1)}, u32[]{:S(2)}, u32[]{:S(2)}) %collective-permute-start.81) | collective-permute-done | bytes 131104 | tf_op jit(solution)/shard_map/ppermute | solution.py:14
  359.5 45.8 %all-gather.2 = f32[32,2,8]{2,1,0:T(2,128)S(1)} all-gather(f32[16,2,8]{2,1,0:T(2,128)S(1)} %copy.828), channel_id=4, replica_groups=mesh['outer'=2,'inner'=32,'head'=4] {'outer'}, dimensions={0}, use_global_device_ids=true | all-gather | bytes 3072 | tf_op jit(solution)/shard_map/all_gather | solution.py:18
  405.8 7.5 %all-gather.1 = f32[32,2,8]{2,1,0:T(2,128)S(1)} all-gather(f32[16,2,8]{2,1,0:T(2,128)S(1)} %copy.822), channel_id=3, replica_groups=mesh['outer'=2,'inner'=32,'head'=4] {'outer'}, dimensions={0}, use_global_device_ids=true | all-gather | bytes 3072 | tf_op jit(solution)/shard_map/all_gather | solution.py:18
  413.7 7.2 %collective-permute-done.90 = f32[16,2,8,128]{3,0,2,1:T(8,128)S(1)} collective-permute-done((f32[16,2,8,128]{3,0,2,1:T(8,128)S(1)}, f32[16,2,8,128]{3,0,2,1:T(8,128)S(1)}, u32[]{:S(2)}, u32[]{:S(2)}) %collective-permute-start.90) | collective-permute-done | bytes 131104 | tf_op jit(solution)/shard_map/ppermute | solution.py:14
  421.4 7.7 %collective-permute-done.93 = f32[16,2,8,128]{3,0,2,1:T(8,128)S(1)} collective-permute-done((f32[16,2,8,128]{3,0,2,1:T(8,128)S(1)}, f32[16,2,8,128]{3,0,2,1:T(8,128)S(1)}, u32[]{:S(2)}, u32[]{:S(2)}) %collective-permute-start.93) | collective-permute-done | bytes 131104 | tf_op jit(solution)/shard_map/ppermute | solution.py:14
  429.0 10.2 %all-gather = f32[32,2,8,128]{3,0,2,1:T(8,128)S(1)} all-gather(f32[16,2,8,128]{3,0,2,1:T(8,128)S(1)} %collective-permute-done.93), channel_id=2, replica_groups=mesh['outer'=2,'inner'=32,'head'=4] {'outer'}, dimensions={0}, use_global_device_ids=true | all-gather | bytes 393216 | tf_op jit(solution)/shard_map/all_gather | solution.py:18
  439.3 0.8 fusion.260
  (477 shorter events, 79.4 us)
Async XLA Ops:
  1.0 17.7 %collective-permute-start.2 = (bf16[16,2,8,128]{3,0,2,1:T(8,128)(2,1)S(1)}, bf16[16,2,8,128]{3,0,2,1:T(8,128)(2,1)S(1)}, u32[]{:S(2)}, u32[]{:S(2)}) collective-permute-start(bf16[16,2,8,128]{3,0,2,1:T(8,128)(2,1)S(1)} %bitcast.358), channel_id=1, source_target_pairs={{0,4},{4,8},{8,12},{12,16},{16,20},{20,24},{24,28},{28,32},{32,36}... | collective-permute-start | bytes 196616 | tf_op jit(solution)/shard_map/ppermute | solution.py:14
  16.2 11.3 %collective-permute-start = (f32[16,2,8,128]{3,0,2,1:T(8,128)S(1)}, f32[16,2,8,128]{3,0,2,1:T(8,128)S(1)}, u32[]{:S(2)}, u32[]{:S(2)}) collective-permute-start(f32[16,2,8,128]{3,0,2,1:T(8,128)S(1)} %fusion.129), channel_id=1, source_target_pairs={{0,4},{4,8},{8,12},{12,16},{16,20},{20,24},{24,28},{28,32},{32,36}... | collective-permute-start | bytes 393224 | tf_op jit(solution)/shard_map/ppermute | solution.py:14
  28.6 17.3 %collective-permute-start.3 = (f32[16,2,8,128]{3,0,2,1:T(8,128)S(1)}, f32[16,2,8,128]{3,0,2,1:T(8,128)S(1)}, u32[]{:S(2)}, u32[]{:S(2)}) collective-permute-start(f32[16,2,8,128]{3,0,2,1:T(8,128)S(1)} %multiply_add_fusion.30), channel_id=1, source_target_pairs={{0,4},{4,8},{8,12},{12,16},{16,20},{20,24},{24,28},{28,32},{32,36}... | collective-permute-start | bytes 393224 | tf_op jit(solution)/shard_map/ppermute | solution.py:14
  28.8 9.5 %collective-permute-start.97 = (f32[16,2,8]{0,2,1:T(8,128)S(1)}, f32[16,2,8]{0,2,1:T(8,128)S(1)}, u32[]{:S(2)}, u32[]{:S(2)}) collective-permute-start(f32[16,2,8]{0,2,1:T(8,128)S(1)} %get-tuple-element.180), channel_id=1, source_target_pairs={{0,4},{4,8},{8,12},{12,16},{16,20},{20,24},{24,28},{28,32},{32,36}... | collective-permute-start | bytes 3080 | tf_op jit(solution)/shard_map/ppermute | solution.py:14
  38.3 8.4 %collective-permute-start.98 = (f32[16,2,8]{0,2,1:T(8,128)S(1)}, f32[16,2,8]{0,2,1:T(8,128)S(1)}, u32[]{:S(2)}, u32[]{:S(2)}) collective-permute-start(f32[16,2,8]{0,2,1:T(8,128)S(1)} %get-tuple-element.176), channel_id=1, source_target_pairs={{0,4},{4,8},{8,12},{12,16},{16,20},{20,24},{24,28},{28,32},{32,36}... | collective-permute-start | bytes 3080 | tf_op jit(solution)/shard_map/ppermute | solution.py:14
  46.5 9.9 %collective-permute-start.6 = (f32[16,2,8,128]{3,0,2,1:T(8,128)S(1)}, f32[16,2,8,128]{3,0,2,1:T(8,128)S(1)}, u32[]{:S(2)}, u32[]{:S(2)}) collective-permute-start(f32[16,2,8,128]{3,0,2,1:T(8,128)S(1)} %multiply_add_fusion.29), channel_id=1, source_target_pairs={{0,4},{4,8},{8,12},{12,16},{16,20},{20,24},{24,28},{28,32},{32,36}... | collective-permute-start | bytes 393224 | tf_op jit(solution)/shard_map/ppermute | solution.py:14
  46.7 9.4 %collective-permute-start.99 = (f32[16,2,8]{0,2,1:T(8,128)S(1)}, f32[16,2,8]{0,2,1:T(8,128)S(1)}, u32[]{:S(2)}, u32[]{:S(2)}) collective-permute-start(f32[16,2,8]{0,2,1:T(8,128)S(1)} %get-tuple-element.172), channel_id=1, source_target_pairs={{0,4},{4,8},{8,12},{12,16},{16,20},{20,24},{24,28},{28,32},{32,36}... | collective-permute-start | bytes 3080 | tf_op jit(solution)/shard_map/ppermute | solution.py:14
  47.2 8.9 %collective-permute-start.13 = (f32[16,2,8]{0,2,1:T(8,128)S(1)}, f32[16,2,8]{0,2,1:T(8,128)S(1)}, u32[]{:S(2)}, u32[]{:S(2)}) collective-permute-start(f32[16,2,8]{0,2,1:T(8,128)S(1)} %get-tuple-element.175), channel_id=1, source_target_pairs={{0,4},{4,8},{8,12},{12,16},{16,20},{20,24},{24,28},{28,32},{32,36}... | collective-permute-start | bytes 3080 | tf_op jit(solution)/shard_map/ppermute | solution.py:14
  56.2 8.5 %collective-permute-start.100 = (f32[16,2,8]{0,2,1:T(8,128)S(1)}, f32[16,2,8]{0,2,1:T(8,128)S(1)}, u32[]{:S(2)}, u32[]{:S(2)}) collective-permute-start(f32[16,2,8]{0,2,1:T(8,128)S(1)} %get-tuple-element.168), channel_id=1, source_target_pairs={{0,4},{4,8},{8,12},{12,16},{16,20},{20,24},{24,28},{28,32},{32,36}... | collective-permute-start | bytes 3080 | tf_op jit(solution)/shard_map/ppermute | solution.py:14
  56.3 8.4 %collective-permute-start.16 = (f32[16,2,8]{0,2,1:T(8,128)S(1)}, f32[16,2,8]{0,2,1:T(8,128)S(1)}, u32[]{:S(2)}, u32[]{:S(2)}) collective-permute-start(f32[16,2,8]{0,2,1:T(8,128)S(1)} %get-tuple-element.171), channel_id=1, source_target_pairs={{0,4},{4,8},{8,12},{12,16},{16,20},{20,24},{24,28},{28,32},{32,36}... | collective-permute-start | bytes 3080 | tf_op jit(solution)/shard_map/ppermute | solution.py:14
  56.6 24.9 %collective-permute-start.9 = (f32[16,2,8,128]{3,0,2,1:T(8,128)S(1)}, f32[16,2,8,128]{3,0,2,1:T(8,128)S(1)}, u32[]{:S(2)}, u32[]{:S(2)}) collective-permute-start(f32[16,2,8,128]{3,0,2,1:T(8,128)S(1)} %multiply_add_fusion.28), channel_id=1, source_target_pairs={{0,4},{4,8},{8,12},{12,16},{16,20},{20,24},{24,28},{28,32},{32,36}... | collective-permute-start | bytes 393224 | tf_op jit(solution)/shard_map/ppermute | solution.py:14
  64.7 9.2 %collective-permute-start.101 = (f32[16,2,8]{0,2,1:T(8,128)S(1)}, f32[16,2,8]{0,2,1:T(8,128)S(1)}, u32[]{:S(2)}, u32[]{:S(2)}) collective-permute-start(f32[16,2,8]{0,2,1:T(8,128)S(1)} %get-tuple-element.164), channel_id=1, source_target_pairs={{0,4},{4,8},{8,12},{12,16},{16,20},{20,24},{24,28},{28,32},{32,36}... | collective-permute-start | bytes 3080 | tf_op jit(solution)/shard_map/ppermute | solution.py:14
  64.8 9.1 %collective-permute-start.19 = (f32[16,2,8]{0,2,1:T(8,128)S(1)}, f32[16,2,8]{0,2,1:T(8,128)S(1)}, u32[]{:S(2)}, u32[]{:S(2)}) collective-permute-start(f32[16,2,8]{0,2,1:T(8,128)S(1)} %get-tuple-element.167), channel_id=1, source_target_pairs={{0,4},{4,8},{8,12},{12,16},{16,20},{20,24},{24,28},{28,32},{32,36}... | collective-permute-start | bytes 3080 | tf_op jit(solution)/shard_map/ppermute | solution.py:14
  73.9 8.4 %collective-permute-start.102 = (f32[16,2,8]{0,2,1:T(8,128)S(1)}, f32[16,2,8]{0,2,1:T(8,128)S(1)}, u32[]{:S(2)}, u32[]{:S(2)}) collective-permute-start(f32[16,2,8]{0,2,1:T(8,128)S(1)} %get-tuple-element.160), channel_id=1, source_target_pairs={{0,4},{4,8},{8,12},{12,16},{16,20},{20,24},{24,28},{28,32},{32,36}... | collective-permute-start | bytes 3080 | tf_op jit(solution)/shard_map/ppermute | solution.py:14
  82.1 20.2 %collective-permute-start.12 = (f32[16,2,8,128]{3,0,2,1:T(8,128)S(1)}, f32[16,2,8,128]{3,0,2,1:T(8,128)S(1)}, u32[]{:S(2)}, u32[]{:S(2)}) collective-permute-start(f32[16,2,8,128]{3,0,2,1:T(8,128)S(1)} %multiply_add_fusion.27), channel_id=1, source_target_pairs={{0,4},{4,8},{8,12},{12,16},{16,20},{20,24},{24,28},{28,32},{32,36}... | collective-permute-start | bytes 393224 | tf_op jit(solution)/shard_map/ppermute | solution.py:14
  82.2 8.6 %collective-permute-start.26 = (bf16[16,2,8,128]{3,0,2,1:T(8,128)(2,1)S(1)}, bf16[16,2,8,128]{3,0,2,1:T(8,128)(2,1)S(1)}, u32[]{:S(2)}, u32[]{:S(2)}) collective-permute-start(bf16[16,2,8,128]{3,0,2,1:T(8,128)(2,1)S(1)} %collective-permute-done.23), channel_id=1, source_target_pairs={{0,4},{4,8},{8,12},{12,16},{16,20},{20,24},{24,28},{28,32},{32,36}... | collective-permute-start | bytes 196616 | tf_op jit(solution)/shard_map/ppermute | solution.py:14
  82.3 10.2 %collective-permute-start.103 = (f32[16,2,8]{0,2,1:T(8,128)S(1)}, f32[16,2,8]{0,2,1:T(8,128)S(1)}, u32[]{:S(2)}, u32[]{:S(2)}) collective-permute-start(f32[16,2,8]{0,2,1:T(8,128)S(1)} %get-tuple-element.156), channel_id=1, source_target_pairs={{0,4},{4,8},{8,12},{12,16},{16,20},{20,24},{24,28},{28,32},{32,36}... | collective-permute-start | bytes 3080 | tf_op jit(solution)/shard_map/ppermute | solution.py:14
  82.4 10.1 %collective-permute-start.25 = (f32[16,2,8]{0,2,1:T(8,128)S(1)}, f32[16,2,8]{0,2,1:T(8,128)S(1)}, u32[]{:S(2)}, u32[]{:S(2)}) collective-permute-start(f32[16,2,8]{0,2,1:T(8,128)S(1)} %get-tuple-element.159), channel_id=1, source_target_pairs={{0,4},{4,8},{8,12},{12,16},{16,20},{20,24},{24,28},{28,32},{32,36}... | collective-permute-start | bytes 3080 | tf_op jit(solution)/shard_map/ppermute | solution.py:14
  92.6 9.0 %collective-permute-start.104 = (f32[16,2,8]{0,2,1:T(8,128)S(1)}, f32[16,2,8]{0,2,1:T(8,128)S(1)}, u32[]{:S(2)}, u32[]{:S(2)}) collective-permute-start(f32[16,2,8]{0,2,1:T(8,128)S(1)} %get-tuple-element.152), channel_id=1, source_target_pairs={{0,4},{4,8},{8,12},{12,16},{16,20},{20,24},{24,28},{28,32},{32,36}... | collective-permute-start | bytes 3080 | tf_op jit(solution)/shard_map/ppermute | solution.py:14
  92.7 8.9 %collective-permute-start.28 = (f32[16,2,8]{0,2,1:T(8,128)S(1)}, f32[16,2,8]{0,2,1:T(8,128)S(1)}, u32[]{:S(2)}, u32[]{:S(2)}) collective-permute-start(f32[16,2,8]{0,2,1:T(8,128)S(1)} %get-tuple-element.155), channel_id=1, source_target_pairs={{0,4},{4,8},{8,12},{12,16},{16,20},{20,24},{24,28},{28,32},{32,36}... | collective-permute-start | bytes 3080 | tf_op jit(solution)/shard_map/ppermute | solution.py:14
  101.6 8.9 %collective-permute-start.105 = (f32[16,2,8]{0,2,1:T(8,128)S(1)}, f32[16,2,8]{0,2,1:T(8,128)S(1)}, u32[]{:S(2)}, u32[]{:S(2)}) collective-permute-start(f32[16,2,8]{0,2,1:T(8,128)S(1)} %get-tuple-element.148), channel_id=1, source_target_pairs={{0,4},{4,8},{8,12},{12,16},{16,20},{20,24},{24,28},{28,32},{32,36}... | collective-permute-start | bytes 3080 | tf_op jit(solution)/shard_map/ppermute | solution.py:14
  101.7 8.8 %collective-permute-start.31 = (f32[16,2,8]{0,2,1:T(8,128)S(1)}, f32[16,2,8]{0,2,1:T(8,128)S(1)}, u32[]{:S(2)}, u32[]{:S(2)}) collective-permute-start(f32[16,2,8]{0,2,1:T(8,128)S(1)} %get-tuple-element.151), channel_id=1, source_target_pairs={{0,4},{4,8},{8,12},{12,16},{16,20},{20,24},{24,28},{28,32},{32,36}... | collective-permute-start | bytes 3080 | tf_op jit(solution)/shard_map/ppermute | solution.py:14
  102.4 16.5 %collective-permute-start.15 = (f32[16,2,8,128]{3,0,2,1:T(8,128)S(1)}, f32[16,2,8,128]{3,0,2,1:T(8,128)S(1)}, u32[]{:S(2)}, u32[]{:S(2)}) collective-permute-start(f32[16,2,8,128]{3,0,2,1:T(8,128)S(1)} %multiply_add_fusion.26), channel_id=1, source_target_pairs={{0,4},{4,8},{8,12},{12,16},{16,20},{20,24},{24,28},{28,32},{32,36}... | collective-permute-start | bytes 393224 | tf_op jit(solution)/shard_map/ppermute | solution.py:14
  118.6 8.5 %collective-permute-start.107 = (f32[16,2,8]{0,2,1:T(8,128)S(1)}, f32[16,2,8]{0,2,1:T(8,128)S(1)}, u32[]{:S(2)}, u32[]{:S(2)}) collective-permute-start(f32[16,2,8]{0,2,1:T(8,128)S(1)} %get-tuple-element.140), channel_id=1, source_target_pairs={{0,4},{4,8},{8,12},{12,16},{16,20},{20,24},{24,28},{28,32},{32,36}... | collective-permute-start | bytes 3080 | tf_op jit(solution)/shard_map/ppermute | solution.py:14
  119.1 16.5 %collective-permute-start.18 = (f32[16,2,8,128]{3,0,2,1:T(8,128)S(1)}, f32[16,2,8,128]{3,0,2,1:T(8,128)S(1)}, u32[]{:S(2)}, u32[]{:S(2)}) collective-permute-start(f32[16,2,8,128]{3,0,2,1:T(8,128)S(1)} %multiply_add_fusion.25), channel_id=1, source_target_pairs={{0,4},{4,8},{8,12},{12,16},{16,20},{20,24},{24,28},{28,32},{32,36}... | collective-permute-start | bytes 393224 | tf_op jit(solution)/shard_map/ppermute | solution.py:14
  135.3 8.5 %collective-permute-start.109 = (f32[16,2,8]{0,2,1:T(8,128)S(1)}, f32[16,2,8]{0,2,1:T(8,128)S(1)}, u32[]{:S(2)}, u32[]{:S(2)}) collective-permute-start(f32[16,2,8]{0,2,1:T(8,128)S(1)} %get-tuple-element.132), channel_id=1, source_target_pairs={{0,4},{4,8},{8,12},{12,16},{16,20},{20,24},{24,28},{28,32},{32,36}... | collective-permute-start | bytes 3080 | tf_op jit(solution)/shard_map/ppermute | solution.py:14
  135.4 8.4 %collective-permute-start.43 = (f32[16,2,8]{0,2,1:T(8,128)S(1)}, f32[16,2,8]{0,2,1:T(8,128)S(1)}, u32[]{:S(2)}, u32[]{:S(2)}) collective-permute-start(f32[16,2,8]{0,2,1:T(8,128)S(1)} %get-tuple-element.135), channel_id=1, source_target_pairs={{0,4},{4,8},{8,12},{12,16},{16,20},{20,24},{24,28},{28,32},{32,36}... | collective-permute-start | bytes 3080 | tf_op jit(solution)/shard_map/ppermute | solution.py:14
  135.7 16.9 %collective-permute-start.21 = (f32[16,2,8,128]{3,0,2,1:T(8,128)S(1)}, f32[16,2,8,128]{3,0,2,1:T(8,128)S(1)}, u32[]{:S(2)}, u32[]{:S(2)}) collective-permute-start(f32[16,2,8,128]{3,0,2,1:T(8,128)S(1)} %multiply_add_fusion.24), channel_id=1, source_target_pairs={{0,4},{4,8},{8,12},{12,16},{16,20},{20,24},{24,28},{28,32},{32,36}... | collective-permute-start | bytes 393224 | tf_op jit(solution)/shard_map/ppermute | solution.py:14
  152.0 9.7 %collective-permute-start.111 = (f32[16,2,8]{0,2,1:T(8,128)S(1)}, f32[16,2,8]{0,2,1:T(8,128)S(1)}, u32[]{:S(2)}, u32[]{:S(2)}) collective-permute-start(f32[16,2,8]{0,2,1:T(8,128)S(1)} %get-tuple-element.124), channel_id=1, source_target_pairs={{0,4},{4,8},{8,12},{12,16},{16,20},{20,24},{24,28},{28,32},{32,36}... | collective-permute-start | bytes 3080 | tf_op jit(solution)/shard_map/ppermute | solution.py:14
  152.1 9.7 %collective-permute-start.49 = (f32[16,2,8]{0,2,1:T(8,128)S(1)}, f32[16,2,8]{0,2,1:T(8,128)S(1)}, u32[]{:S(2)}, u32[]{:S(2)}) collective-permute-start(f32[16,2,8]{0,2,1:T(8,128)S(1)} %get-tuple-element.127), channel_id=1, source_target_pairs={{0,4},{4,8},{8,12},{12,16},{16,20},{20,24},{24,28},{28,32},{32,36}... | collective-permute-start | bytes 3080 | tf_op jit(solution)/shard_map/ppermute | solution.py:14
  152.8 9.7 %collective-permute-start.24 = (f32[16,2,8,128]{3,0,2,1:T(8,128)S(1)}, f32[16,2,8,128]{3,0,2,1:T(8,128)S(1)}, u32[]{:S(2)}, u32[]{:S(2)}) collective-permute-start(f32[16,2,8,128]{3,0,2,1:T(8,128)S(1)} %multiply_add_fusion.23), channel_id=1, source_target_pairs={{0,4},{4,8},{8,12},{12,16},{16,20},{20,24},{24,28},{28,32},{32,36}... | collective-permute-start | bytes 393224 | tf_op jit(solution)/shard_map/ppermute | solution.py:14
  161.7 9.2 %collective-permute-start.112 = (f32[16,2,8]{0,2,1:T(8,128)S(1)}, f32[16,2,8]{0,2,1:T(8,128)S(1)}, u32[]{:S(2)}, u32[]{:S(2)}) collective-permute-start(f32[16,2,8]{0,2,1:T(8,128)S(1)} %get-tuple-element.120), channel_id=1, source_target_pairs={{0,4},{4,8},{8,12},{12,16},{16,20},{20,24},{24,28},{28,32},{32,36}... | collective-permute-start | bytes 3080 | tf_op jit(solution)/shard_map/ppermute | solution.py:14
  161.8 9.2 %collective-permute-start.52 = (f32[16,2,8]{0,2,1:T(8,128)S(1)}, f32[16,2,8]{0,2,1:T(8,128)S(1)}, u32[]{:S(2)}, u32[]{:S(2)}) collective-permute-start(f32[16,2,8]{0,2,1:T(8,128)S(1)} %get-tuple-element.123), channel_id=1, source_target_pairs={{0,4},{4,8},{8,12},{12,16},{16,20},{20,24},{24,28},{28,32},{32,36}... | collective-permute-start | bytes 3080 | tf_op jit(solution)/shard_map/ppermute | solution.py:14
  162.6 17.0 %collective-permute-start.27 = (f32[16,2,8,128]{3,0,2,1:T(8,128)S(1)}, f32[16,2,8,128]{3,0,2,1:T(8,128)S(1)}, u32[]{:S(2)}, u32[]{:S(2)}) collective-permute-start(f32[16,2,8,128]{3,0,2,1:T(8,128)S(1)} %multiply_add_fusion.22), channel_id=1, source_target_pairs={{0,4},{4,8},{8,12},{12,16},{16,20},{20,24},{24,28},{28,32},{32,36}... | collective-permute-start | bytes 393224 | tf_op jit(solution)/shard_map/ppermute | solution.py:14
  179.2 8.6 %collective-permute-start.114 = (f32[16,2,8]{0,2,1:T(8,128)S(1)}, f32[16,2,8]{0,2,1:T(8,128)S(1)}, u32[]{:S(2)}, u32[]{:S(2)}) collective-permute-start(f32[16,2,8]{0,2,1:T(8,128)S(1)} %get-tuple-element.112), channel_id=1, source_target_pairs={{0,4},{4,8},{8,12},{12,16},{16,20},{20,24},{24,28},{28,32},{32,36}... | collective-permute-start | bytes 3080 | tf_op jit(solution)/shard_map/ppermute | solution.py:14
  179.2 8.6 %collective-permute-start.58 = (f32[16,2,8]{0,2,1:T(8,128)S(1)}, f32[16,2,8]{0,2,1:T(8,128)S(1)}, u32[]{:S(2)}, u32[]{:S(2)}) collective-permute-start(f32[16,2,8]{0,2,1:T(8,128)S(1)} %get-tuple-element.115), channel_id=1, source_target_pairs={{0,4},{4,8},{8,12},{12,16},{16,20},{20,24},{24,28},{28,32},{32,36}... | collective-permute-start | bytes 3080 | tf_op jit(solution)/shard_map/ppermute | solution.py:14
  179.8 16.5 %collective-permute-start.30 = (f32[16,2,8,128]{3,0,2,1:T(8,128)S(1)}, f32[16,2,8,128]{3,0,2,1:T(8,128)S(1)}, u32[]{:S(2)}, u32[]{:S(2)}) collective-permute-start(f32[16,2,8,128]{3,0,2,1:T(8,128)S(1)} %multiply_add_fusion.21), channel_id=1, source_target_pairs={{0,4},{4,8},{8,12},{12,16},{16,20},{20,24},{24,28},{28,32},{32,36}... | collective-permute-start | bytes 393224 | tf_op jit(solution)/shard_map/ppermute | solution.py:14
  196.0 8.5 %collective-permute-start.116 = (f32[16,2,8]{0,2,1:T(8,128)S(1)}, f32[16,2,8]{0,2,1:T(8,128)S(1)}, u32[]{:S(2)}, u32[]{:S(2)}) collective-permute-start(f32[16,2,8]{0,2,1:T(8,128)S(1)} %get-tuple-element.104), channel_id=1, source_target_pairs={{0,4},{4,8},{8,12},{12,16},{16,20},{20,24},{24,28},{28,32},{32,36}... | collective-permute-start | bytes 3080 | tf_op jit(solution)/shard_map/ppermute | solution.py:14
  196.1 8.4 %collective-permute-start.64 = (f32[16,2,8]{0,2,1:T(8,128)S(1)}, f32[16,2,8]{0,2,1:T(8,128)S(1)}, u32[]{:S(2)}, u32[]{:S(2)}) collective-permute-start(f32[16,2,8]{0,2,1:T(8,128)S(1)} %get-tuple-element.107), channel_id=1, source_target_pairs={{0,4},{4,8},{8,12},{12,16},{16,20},{20,24},{24,28},{28,32},{32,36}... | collective-permute-start | bytes 3080 | tf_op jit(solution)/shard_map/ppermute | solution.py:14
  196.4 16.5 %collective-permute-start.33 = (f32[16,2,8,128]{3,0,2,1:T(8,128)S(1)}, f32[16,2,8,128]{3,0,2,1:T(8,128)S(1)}, u32[]{:S(2)}, u32[]{:S(2)}) collective-permute-start(f32[16,2,8,128]{3,0,2,1:T(8,128)S(1)} %multiply_add_fusion.20), channel_id=1, source_target_pairs={{0,4},{4,8},{8,12},{12,16},{16,20},{20,24},{24,28},{28,32},{32,36}... | collective-permute-start | bytes 393224 | tf_op jit(solution)/shard_map/ppermute | solution.py:14
  212.6 8.5 %collective-permute-start.118 = (f32[16,2,8]{0,2,1:T(8,128)S(1)}, f32[16,2,8]{0,2,1:T(8,128)S(1)}, u32[]{:S(2)}, u32[]{:S(2)}) collective-permute-start(f32[16,2,8]{0,2,1:T(8,128)S(1)} %get-tuple-element.96), channel_id=1, source_target_pairs={{0,4},{4,8},{8,12},{12,16},{16,20},{20,24},{24,28},{28,32},{32,36}... | collective-permute-start | bytes 3080 | tf_op jit(solution)/shard_map/ppermute | solution.py:14
  213.0 17.6 %collective-permute-start.36 = (f32[16,2,8,128]{3,0,2,1:T(8,128)S(1)}, f32[16,2,8,128]{3,0,2,1:T(8,128)S(1)}, u32[]{:S(2)}, u32[]{:S(2)}) collective-permute-start(f32[16,2,8,128]{3,0,2,1:T(8,128)S(1)} %multiply_add_fusion.19), channel_id=1, source_target_pairs={{0,4},{4,8},{8,12},{12,16},{16,20},{20,24},{24,28},{28,32},{32,36}... | collective-permute-start | bytes 393224 | tf_op jit(solution)/shard_map/ppermute | solution.py:14
  221.1 9.0 %collective-permute-start.119 = (f32[16,2,8]{0,2,1:T(8,128)S(1)}, f32[16,2,8]{0,2,1:T(8,128)S(1)}, u32[]{:S(2)}, u32[]{:S(2)}) collective-permute-start(f32[16,2,8]{0,2,1:T(8,128)S(1)} %get-tuple-element.92), channel_id=1, source_target_pairs={{0,4},{4,8},{8,12},{12,16},{16,20},{20,24},{24,28},{28,32},{32,36}... | collective-permute-start | bytes 3080 | tf_op jit(solution)/shard_map/ppermute | solution.py:14
  221.2 8.9 %collective-permute-start.73 = (f32[16,2,8]{0,2,1:T(8,128)S(1)}, f32[16,2,8]{0,2,1:T(8,128)S(1)}, u32[]{:S(2)}, u32[]{:S(2)}) collective-permute-start(f32[16,2,8]{0,2,1:T(8,128)S(1)} %get-tuple-element.95), channel_id=1, source_target_pairs={{0,4},{4,8},{8,12},{12,16},{16,20},{20,24},{24,28},{28,32},{32,36}... | collective-permute-start | bytes 3080 | tf_op jit(solution)/shard_map/ppermute | solution.py:14
  230.1 9.5 %collective-permute-start.120 = (f32[16,2,8]{0,2,1:T(8,128)S(1)}, f32[16,2,8]{0,2,1:T(8,128)S(1)}, u32[]{:S(2)}, u32[]{:S(2)}) collective-permute-start(f32[16,2,8]{0,2,1:T(8,128)S(1)} %get-tuple-element.88), channel_id=1, source_target_pairs={{0,4},{4,8},{8,12},{12,16},{16,20},{20,24},{24,28},{28,32},{32,36}... | collective-permute-start | bytes 3080 | tf_op jit(solution)/shard_map/ppermute | solution.py:14
  230.2 9.5 %collective-permute-start.76 = (f32[16,2,8]{0,2,1:T(8,128)S(1)}, f32[16,2,8]{0,2,1:T(8,128)S(1)}, u32[]{:S(2)}, u32[]{:S(2)}) collective-permute-start(f32[16,2,8]{0,2,1:T(8,128)S(1)} %get-tuple-element.91), channel_id=1, source_target_pairs={{0,4},{4,8},{8,12},{12,16},{16,20},{20,24},{24,28},{28,32},{32,36}... | collective-permute-start | bytes 3080 | tf_op jit(solution)/shard_map/ppermute | solution.py:14
  230.7 17.8 %collective-permute-start.39 = (f32[16,2,8,128]{3,0,2,1:T(8,128)S(1)}, f32[16,2,8,128]{3,0,2,1:T(8,128)S(1)}, u32[]{:S(2)}, u32[]{:S(2)}) collective-permute-start(f32[16,2,8,128]{3,0,2,1:T(8,128)S(1)} %multiply_add_fusion.18), channel_id=1, source_target_pairs={{0,4},{4,8},{8,12},{12,16},{16,20},{20,24},{24,28},{28,32},{32,36}... | collective-permute-start | bytes 393224 | tf_op jit(solution)/shard_map/ppermute | solution.py:14
  239.7 8.5 %collective-permute-start.121 = (f32[16,2,8]{0,2,1:T(8,128)S(1)}, f32[16,2,8]{0,2,1:T(8,128)S(1)}, u32[]{:S(2)}, u32[]{:S(2)}) collective-permute-start(f32[16,2,8]{0,2,1:T(8,128)S(1)} %get-tuple-element.84), channel_id=1, source_target_pairs={{0,4},{4,8},{8,12},{12,16},{16,20},{20,24},{24,28},{28,32},{32,36}... | collective-permute-start | bytes 3080 | tf_op jit(solution)/shard_map/ppermute | solution.py:14
  239.8 8.4 %collective-permute-start.79 = (f32[16,2,8]{0,2,1:T(8,128)S(1)}, f32[16,2,8]{0,2,1:T(8,128)S(1)}, u32[]{:S(2)}, u32[]{:S(2)}) collective-permute-start(f32[16,2,8]{0,2,1:T(8,128)S(1)} %get-tuple-element.87), channel_id=1, source_target_pairs={{0,4},{4,8},{8,12},{12,16},{16,20},{20,24},{24,28},{28,32},{32,36}... | collective-permute-start | bytes 3080 | tf_op jit(solution)/shard_map/ppermute | solution.py:14
  248.3 16.9 %collective-permute-start.122 = (f32[16,2,8]{0,2,1:T(8,128)S(1)}, f32[16,2,8]{0,2,1:T(8,128)S(1)}, u32[]{:S(2)}, u32[]{:S(2)}) collective-permute-start(f32[16,2,8]{0,2,1:T(8,128)S(1)} %get-tuple-element.80), channel_id=1, source_target_pairs={{0,4},{4,8},{8,12},{12,16},{16,20},{20,24},{24,28},{28,32},{32,36}... | collective-permute-start | bytes 3080 | tf_op jit(solution)/shard_map/ppermute | solution.py:14
  248.4 16.8 %collective-permute-start.82 = (f32[16,2,8]{0,2,1:T(8,128)S(1)}, f32[16,2,8]{0,2,1:T(8,128)S(1)}, u32[]{:S(2)}, u32[]{:S(2)}) collective-permute-start(f32[16,2,8]{0,2,1:T(8,128)S(1)} %get-tuple-element.83), channel_id=1, source_target_pairs={{0,4},{4,8},{8,12},{12,16},{16,20},{20,24},{24,28},{28,32},{32,36}... | collective-permute-start | bytes 3080 | tf_op jit(solution)/shard_map/ppermute | solution.py:14
  248.7 8.5 %collective-permute-start.42 = (f32[16,2,8,128]{3,0,2,1:T(8,128)S(1)}, f32[16,2,8,128]{3,0,2,1:T(8,128)S(1)}, u32[]{:S(2)}, u32[]{:S(2)}) collective-permute-start(f32[16,2,8,128]{3,0,2,1:T(8,128)S(1)} %multiply_add_fusion.17), channel_id=1, source_target_pairs={{0,4},{4,8},{8,12},{12,16},{16,20},{20,24},{24,28},{28,32},{32,36}... | collective-permute-start | bytes 393224 | tf_op jit(solution)/shard_map/ppermute | solution.py:14
  265.2 31.0 %collective-permute-start.123 = (f32[16,2,8]{0,2,1:T(8,128)S(1)}, f32[16,2,8]{0,2,1:T(8,128)S(1)}, u32[]{:S(2)}, u32[]{:S(2)}) collective-permute-start(f32[16,2,8]{0,2,1:T(8,128)S(1)} %get-tuple-element.76), channel_id=1, source_target_pairs={{0,4},{4,8},{8,12},{12,16},{16,20},{20,24},{24,28},{28,32},{32,36}... | collective-permute-start | bytes 3080 | tf_op jit(solution)/shard_map/ppermute | solution.py:14
  265.3 30.9 %collective-permute-start.85 = (f32[16,2,8]{0,2,1:T(8,128)S(1)}, f32[16,2,8]{0,2,1:T(8,128)S(1)}, u32[]{:S(2)}, u32[]{:S(2)}) collective-permute-start(f32[16,2,8]{0,2,1:T(8,128)S(1)} %get-tuple-element.79), channel_id=1, source_target_pairs={{0,4},{4,8},{8,12},{12,16},{16,20},{20,24},{24,28},{28,32},{32,36}... | collective-permute-start | bytes 3080 | tf_op jit(solution)/shard_map/ppermute | solution.py:14
  279.8 8.8 %collective-permute-start.54 = (f32[16,2,8,128]{3,0,2,1:T(8,128)S(1)}, f32[16,2,8,128]{3,0,2,1:T(8,128)S(1)}, u32[]{:S(2)}, u32[]{:S(2)}) collective-permute-start(f32[16,2,8,128]{3,0,2,1:T(8,128)S(1)} %multiply_add_fusion.13), channel_id=1, source_target_pairs={{0,4},{4,8},{8,12},{12,16},{16,20},{20,24},{24,28},{28,32},{32,36}... | collective-permute-start | bytes 393224 | tf_op jit(solution)/shard_map/ppermute | solution.py:14
  296.3 29.5 %collective-permute-start.124 = (f32[16,2,8]{0,2,1:T(8,128)S(1)}, f32[16,2,8]{0,2,1:T(8,128)S(1)}, u32[]{:S(2)}, u32[]{:S(2)}) collective-permute-start(f32[16,2,8]{0,2,1:T(8,128)S(1)} %get-tuple-element.72), channel_id=1, source_target_pairs={{0,4},{4,8},{8,12},{12,16},{16,20},{20,24},{24,28},{28,32},{32,36}... | collective-permute-start | bytes 3080 | tf_op jit(solution)/shard_map/ppermute | solution.py:14
  296.4 29.5 %collective-permute-start.88 = (f32[16,2,8]{0,2,1:T(8,128)S(1)}, f32[16,2,8]{0,2,1:T(8,128)S(1)}, u32[]{:S(2)}, u32[]{:S(2)}) collective-permute-start(f32[16,2,8]{0,2,1:T(8,128)S(1)} %get-tuple-element.75), channel_id=1, source_target_pairs={{0,4},{4,8},{8,12},{12,16},{16,20},{20,24},{24,28},{28,32},{32,36}... | collective-permute-start | bytes 3080 | tf_op jit(solution)/shard_map/ppermute | solution.py:14
  325.9 25.1 %collective-permute-start.125 = (f32[16,2,8]{0,2,1:T(8,128)S(1)}, f32[16,2,8]{0,2,1:T(8,128)S(1)}, u32[]{:S(2)}, u32[]{:S(2)}) collective-permute-start(f32[16,2,8]{0,2,1:T(8,128)S(1)} %get-tuple-element.68), channel_id=1, source_target_pairs={{0,4},{4,8},{8,12},{12,16},{16,20},{20,24},{24,28},{28,32},{32,36}... | collective-permute-start | bytes 3080 | tf_op jit(solution)/shard_map/ppermute | solution.py:14
  325.9 25.1 %collective-permute-start.91 = (f32[16,2,8]{0,2,1:T(8,128)S(1)}, f32[16,2,8]{0,2,1:T(8,128)S(1)}, u32[]{:S(2)}, u32[]{:S(2)}) collective-permute-start(f32[16,2,8]{0,2,1:T(8,128)S(1)} %get-tuple-element.71), channel_id=1, source_target_pairs={{0,4},{4,8},{8,12},{12,16},{16,20},{20,24},{24,28},{28,32},{32,36}... | collective-permute-start | bytes 3080 | tf_op jit(solution)/shard_map/ppermute | solution.py:14
  333.1 8.9 %collective-permute-start.75 = (f32[16,2,8,128]{3,0,2,1:T(8,128)S(1)}, f32[16,2,8,128]{3,0,2,1:T(8,128)S(1)}, u32[]{:S(2)}, u32[]{:S(2)}) collective-permute-start(f32[16,2,8,128]{3,0,2,1:T(8,128)S(1)} %multiply_add_fusion.6), channel_id=1, source_target_pairs={{0,4},{4,8},{8,12},{12,16},{16,20},{20,24},{24,28},{28,32},{32,36}... | collective-permute-start | bytes 393224 | tf_op jit(solution)/shard_map/ppermute | solution.py:14
  342.1 8.6 %collective-permute-start.78 = (f32[16,2,8,128]{3,0,2,1:T(8,128)S(1)}, f32[16,2,8,128]{3,0,2,1:T(8,128)S(1)}, u32[]{:S(2)}, u32[]{:S(2)}) collective-permute-start(f32[16,2,8,128]{3,0,2,1:T(8,128)S(1)} %multiply_add_fusion.5), channel_id=1, source_target_pairs={{0,4},{4,8},{8,12},{12,16},{16,20},{20,24},{24,28},{28,32},{32,36}... | collective-permute-start | bytes 393224 | tf_op jit(solution)/shard_map/ppermute | solution.py:14
  351.0 8.4 %collective-permute-start.126 = (f32[16,2,8]{0,2,1:T(8,128)S(1)}, f32[16,2,8]{0,2,1:T(8,128)S(1)}, u32[]{:S(2)}, u32[]{:S(2)}) collective-permute-start(f32[16,2,8]{0,2,1:T(8,128)S(1)} %get-tuple-element.64), channel_id=1, source_target_pairs={{0,4},{4,8},{8,12},{12,16},{16,20},{20,24},{24,28},{28,32},{32,36}... | collective-permute-start | bytes 3080 | tf_op jit(solution)/shard_map/ppermute | solution.py:14
  358.6 46.7 %collective-permute-start.84 = (f32[16,2,8,128]{3,0,2,1:T(8,128)S(1)}, f32[16,2,8,128]{3,0,2,1:T(8,128)S(1)}, u32[]{:S(2)}, u32[]{:S(2)}) collective-permute-start(f32[16,2,8,128]{3,0,2,1:T(8,128)S(1)} %multiply_add_fusion.3), channel_id=1, source_target_pairs={{0,4},{4,8},{8,12},{12,16},{16,20},{20,24},{24,28},{28,32},{32,36}... | collective-permute-start | bytes 393224 | tf_op jit(solution)/shard_map/ppermute | solution.py:14
  359.3 46.4 %collective-permute-start.94 = (f32[16,2,8]{0,2,1:T(8,128)S(1)}, f32[16,2,8]{0,2,1:T(8,128)S(1)}, u32[]{:S(2)}, u32[]{:S(2)}) collective-permute-start(f32[16,2,8]{0,2,1:T(8,128)S(1)} %get-tuple-element.67), channel_id=1, source_target_pairs={{0,4},{4,8},{8,12},{12,16},{16,20},{20,24},{24,28},{28,32},{32,36}... | collective-permute-start | bytes 3080 | tf_op jit(solution)/shard_map/ppermute | solution.py:14
  (65 other events, 483.1 us)
where the time goes:
time: 448 us; the launch traced here: 440 us
  waiting for transfers between devices  277 us (62%)
  blocking collectives  63.5 us (14%)
  matrix products  39.1 us (9%)
  starting transfers between devices  26.7 us (6%)
  other arithmetic  26.1 us (6%)
  local copies, waits for them, and re-layouts  5.07 us (1%)
    ppermute x127, waiting for transfers between devices, from_behind(): lax.ppermute(shard, axis, [(i, (i + by) % size) for i in range(size)])  277 us
    all_gather x3, blocking collectives, merged_2(): everything = jax.tree.map(lambda part: lax.all_gather(part, axis), shard)  63.5 us
    ppermute x127, starting transfers between devices, from_behind(): lax.ppermute(shard, axis, [(i, (i + by) % size) for i in range(size)])  26.7 us
    dot_general x32, matrix products, attend_tile(): jnp.einsum('rhgs,shd->rhgd', weights.astype(jnp.bfloat16), value_tile, pr...  20 us
    dot_general x32, matrix products, attend_tile(): jnp.einsum('rhgd,shd->rhgs', query_tile, key_tile, preferred_element_type...  19.1 us
    reduce_sum x32, other arithmetic, attend_tile(): row_total = jnp.sum(weights, axis=3)  16.1 us
  transfers between devices with their start and end apart: 127, of which 49 were waited for; matrix products, arithmetic and copies ran while one was open for 15% of the time, Pallas kernels for 0%

commit v1 on v0

v1 whole, which is shorter than its diff:
```python
import functools
import math

import jax
import jax.numpy as jnp
from jax import lax
from jax.experimental import pallas as pl
from jax.experimental.pallas import tpu as pltpu
from jax.sharding import Mesh, PartitionSpec as P

BLOCK = 128
NEGATIVE = -1e30
TAIL = 8
EXTRA = 8


def shifted(part, axis, by):
    size = lax.axis_size(axis)
    return lax.ppermute(part, axis, [(i, (i + by) % size) for i in range(size)])


def attend_kernel(own, factor, chunk, live_ref, q_ref, k_ref, v_ref, out_ref, s_ref):
    kv_count, key_rows, dim = k_ref.shape
    blocks, tail, heads, _ = q_ref.shape
    sharing = heads // kv_count
    wide = tail * sharing
    width = blocks * wide
    n_live = live_ref[0]
    first = live_ref[1]
    chunks = key_rows // chunk
    per = chunk // BLOCK

    @pl.when(own >= n_live)
    def _():
        out_ref[:, :dim, :] = jnp.zeros((blocks, dim, kv_count * wide), jnp.float32)
        row = lax.broadcasted_iota(jnp.int32, (blocks, EXTRA, kv_count * wide), 1)
        out_ref[:, dim:, :] = jnp.where(row == 0, NEGATIVE, 0.0)

    @pl.when(own < n_live)
    def _():
        q_all = q_ref[...].astype(jnp.float32)
        rows = [
            q_all[:, :, h * sharing : (h + 1) * sharing, :]
            .reshape(width, dim)
            .astype(jnp.bfloat16)
            for h in range(kv_count)
        ]

        def score(i, peaks):
            base = pl.multiple_of(i * chunk, chunk)
            new = []
            for h in range(kv_count):
                s = lax.dot_general(
                    k_ref[h, pl.ds(base, chunk), :],
                    rows[h],
                    (((1,), (1,)), ((), ())),
                    preferred_element_type=jnp.float32,
                )
                s_ref[h, pl.ds(base, chunk), :] = s
                peak = peaks[h]
                for b in range(per):
                    top = jnp.max(
                        s[b * BLOCK : (b + 1) * BLOCK].reshape(BLOCK // 8, 8, width), axis=0
                    )
                    peak = jnp.maximum(
                        peak, jnp.where(i * per + b >= first, top, NEGATIVE)
                    )
                new.append(peak)
            return tuple(new)

        none = jnp.full((8, width), NEGATIVE, jnp.float32)
        if own == 0:
            peaks = lax.fori_loop(0, chunks - 1, score, (none,) * kv_count)
            base = (chunks - 1) * chunk
            lane = lax.broadcasted_iota(jnp.int32, (8, width), 1)
            late = lax.broadcasted_iota(jnp.int32, (8, width), 0)
            ahead = (lane < wide) & (late > lane // sharing)
            fixed = []
            for h in range(kv_count):
                s = lax.dot_general(
                    k_ref[h, base:, :],
                    rows[h],
                    (((1,), (1,)), ((), ())),
                    preferred_element_type=jnp.float32,
                )
                corner = jnp.where(ahead, NEGATIVE, s[chunk - 8 :])
                s_ref[h, base : base + chunk - 8, :] = s[: chunk - 8]
                s_ref[h, base + chunk - 8 :, :] = corner
                peak = jnp.maximum(peaks[h], corner)
                for b in range(per):
                    hi = BLOCK if b < per - 1 else BLOCK - 8
                    top = jnp.max(
                        s[b * BLOCK : b * BLOCK + hi].reshape(hi // 8, 8, width), axis=0
                    )
                    peak = jnp.maximum(
                        peak,
                        jnp.where((chunks - 1) * per + b >= first, top, NEGATIVE),
                    )
                fixed.append(peak)
            peaks = tuple(fixed)
        else:
            peaks = lax.fori_loop(0, chunks, score, (none,) * kv_count)
        tops = [jnp.max(p, axis=0, keepdims=True) for p in peaks]

        def gather(i, carry):
            base = pl.multiple_of(i * chunk, chunk)
            new = []
            for h in range(kv_count):
                total, acc = carry[h]
                parts = []
                for b in range(per):
                    s = s_ref[h, pl.ds(base + b * BLOCK, BLOCK), :]
                    ref_row = jnp.where(i * per + b >= first, tops[h], -NEGATIVE)
                    w = jnp.exp2((s - ref_row) * factor)
                    total = total + jnp.sum(w.reshape(BLOCK // 8, 8, width), axis=0)
                    parts.append(w.astype(jnp.bfloat16))
                w = jnp.concatenate(parts, axis=0) if per > 1 else parts[0]
                acc = acc + lax.dot_general(
                    v_ref[h, :, pl.ds(base, chunk)],
                    w,
                    (((1,), (0,)), ((), ())),
                    preferred_element_type=jnp.float32,
                )
                new.append((total, acc))
            return tuple(new)

        zero = (jnp.zeros((8, width), jnp.float32), jnp.zeros((dim, width), jnp.float32))
        sums = lax.fori_loop(0, chunks, gather, (zero,) * kv_count)
        row = lax.broadcasted_iota(jnp.int32, (EXTRA, kv_count * wide), 0)
        for j in range(blocks):
            lanes = slice(j * wide, (j + 1) * wide)
            keep = own + blocks * j < n_live
            o = jnp.concatenate([sums[h][1][:, lanes] for h in range(kv_count)], axis=1)
            m = jnp.concatenate([tops[h][:, lanes] for h in range(kv_count)], axis=1)
            l = jnp.concatenate(
                [jnp.sum(sums[h][0][:, lanes], axis=0, keepdims=True) for h in range(kv_count)],
                axis=1,
            )
            out_ref[j, :dim, :] = jnp.where(keep, o, 0.0)
            out_ref[j, dim:, :] = jnp.where(
                row == 0,
                jnp.where(keep, m, NEGATIVE),
                jnp.where((row == 1) & keep, l, 0.0),
            )


def merge(parts, factor, dim):
    top = functools.reduce(jnp.maximum, [m for _, m, _ in parts])
    o = l = None
    for po, pm, pl_ in parts:
        f = jnp.exp2((pm - top) * factor)
        o = po * f if o is None else o + po * f
        l = pl_ * f if l is None else l + pl_ * f
    return o, top, l


def take(ref, j, dim, valid=None):
    o = ref[j, :dim, :]
    m = ref[j, dim : dim + 1, :]
    l = ref[j, dim + 1 : dim + 2, :]
    if valid is not None:
        o = jnp.where(valid, o, 0.0)
        m = jnp.where(valid, m, NEGATIVE)
        l = jnp.where(valid, l, 0.0)
    return o, m, l


def put(ref, j, dim, o, m, l):
    lanes = m.shape[1]
    row = lax.broadcasted_iota(jnp.int32, (EXTRA, lanes), 0)
    ref[j, :dim, :] = o
    ref[j, dim:, :] = jnp.where(row == 0, m, jnp.where(row == 1, l, 0.0))


def column_kernel(factor, x_ref, *refs):
    parts, out_ref = refs[:-1], refs[-1]
    count, dim = parts[0].shape[0], parts[0].shape[1] - EXTRA
    x = x_ref[0]
    for d in range(count + 1):
        found = []
        for u, ref in enumerate(parts):
            if u == 0:
                if d < count:
                    found.append(take(ref, d, dim))
                continue
            j = d - (x < u).astype(jnp.int32)
            valid = (j >= 0) & (j < count)
            found.append(take(ref, jnp.clip(j, 0, count - 1), dim, valid))
        put(out_ref, d, dim, *merge(found, factor, dim))


def row_kernel(factor, place_ref, *refs):
    parts, out_ref = refs[:-1], refs[-1]
    dim = out_ref.shape[1] - EXTRA
    z, o = place_ref[0], place_ref[1]
    for group in range(out_ref.shape[0]):
        found = []
        for d, ref in enumerate(parts):
            mine = jnp.where(d > z, o + 1, o) == group
            found.append(take(ref, 0, dim, mine))
        put(out_ref, group, dim, *merge(found, factor, dim))


def finish_kernel(factor, kv_count, sharing, a_ref, b_ref, out_ref):
    groups = a_ref.shape[0]
    dim = a_ref.shape[1] - EXTRA
    tail = out_ref.shape[0] // groups
    for g in range(groups):
        o, _, l = merge([take(a_ref, g, dim), take(b_ref, g, dim)], factor, dim)
        res = jnp.transpose(o / l)
        res = res.reshape(kv_count, tail, sharing, dim)
        res = jnp.concatenate([res[h] for h in range(kv_count)], axis=1)
        out_ref[g * tail : (g + 1) * tail] = res.astype(out_ref.dtype)


def vmem(count):
    return [pl.BlockSpec(memory_space=pltpu.VMEM)] * count


def smem():
    return [pl.BlockSpec(memory_space=pltpu.SMEM)]


def body(queries, keys, values, doc_lengths):
    rows, columns = lax.axis_size("z"), lax.axis_size("x")
    o, z, x = lax.axis_index("outer"), lax.axis_index("z"), lax.axis_index("x")
    key_rows, kv_count, dim = keys.shape
    query_rows, heads, _ = queries.shape
    sharing = heads // kv_count
    groups = lax.axis_size("outer")
    lanes = kv_count * TAIL * sharing
    reach = 4
    factor = math.log2(math.e) / math.sqrt(dim)

    segment = (o * rows + z) * columns + x
    ends = jnp.cumsum(doc_lengths)
    blocks = key_rows // BLOCK
    last = segment * blocks + blocks - 1
    start = jnp.max(jnp.where(ends <= last, ends, 0))
    end = jnp.min(jnp.where(ends > last, ends, rows * columns * groups * blocks))
    live = jnp.stack([end // blocks - segment, jnp.maximum(start - segment * blocks, 0)])
    live = live.astype(jnp.int32)

    k_heads = jnp.transpose(keys, (1, 0, 2))
    v_heads = jnp.transpose(values, (1, 2, 0))
    tails = queries.reshape(groups, TAIL, heads, dim)

    held = [lax.dynamic_index_in_dim(tails, o, 0)]
    for d in range(1, reach + 1):
        group = jnp.where(z < d, jnp.minimum(o + 1, groups - 1), o)
        held.append(shifted(lax.dynamic_index_in_dim(tails, group, 0), "z", -d))
    stack = jnp.concatenate(held, axis=0)
    asked = [stack[:reach]]
    for u in range(1, columns):
        asked.append(
            shifted(lax.dynamic_slice_in_dim(stack, (x < u).astype(jnp.int32), reach, 0), "x", -u)
        )

    part = jax.ShapeDtypeStruct((reach, dim + EXTRA, lanes), jnp.float32)
    chunk = 256
    partial = []
    for u in range(columns):
        width = reach * TAIL * sharing
        partial.append(
            pl.pallas_call(
                functools.partial(attend_kernel, u, factor, chunk),
                out_shape=part,
                in_specs=smem() + vmem(3),
                out_specs=vmem(1)[0],
                scratch_shapes=[pltpu.VMEM((kv_count, key_rows, width), jnp.float32)],
                cost_estimate=pl.CostEstimate(
                    flops=4 * kv_count * key_rows * width * dim,
                    bytes_accessed=4 * kv_count * key_rows * dim,
                    transcendentals=kv_count * key_rows * width,
                ),
                compiler_params=pltpu.CompilerParams(vmem_limit_bytes=24 << 20),
                name=f"attend_{u}",
            )(live, asked[u], k_heads, v_heads)
        )
    arrived = [partial[0]] + [shifted(partial[u], "x", u) for u in range(1, columns)]
    column = pl.pallas_call(
        functools.partial(column_kernel, factor),
        out_shape=jax.ShapeDtypeStruct((reach + 1, dim + EXTRA, lanes), jnp.float32),
        in_specs=smem() + vmem(columns),
        out_specs=vmem(1)[0],
        name="merge_columns",
    )(x.reshape(1).astype(jnp.int32), *arrived)
    arrived = [column[:1]] + [shifted(column[d : d + 1], "z", d) for d in range(1, reach + 1)]
    mine = pl.pallas_call(
        functools.partial(row_kernel, factor),
        out_shape=jax.ShapeDtypeStruct((groups, dim + EXTRA, lanes), jnp.float32),
        in_specs=smem() + vmem(reach + 1),
        out_specs=vmem(1)[0],
        name="merge_rows",
    )(jnp.stack([z, o]).astype(jnp.int32), *arrived)
    other = shifted(mine, "outer", 1)
    return pl.pallas_call(
        functools.partial(finish_kernel, factor, kv_count, sharing),
        out_shape=jax.ShapeDtypeStruct(queries.shape, queries.dtype),
        in_specs=vmem(2),
        out_specs=vmem(1)[0],
        name="finish",
    )(mine, other)


def solution(mesh):
    outer, inner, head = (mesh.shape[a] for a in ("outer", "inner", "head"))
    columns = 4
    grid = Mesh(
        mesh.devices.reshape(outer, inner // columns, columns, head),
        ("outer", "z", "x", "head"),
    )
    tails = P(("z", "x"), "head", None)
    rows = P(("outer", "z", "x"), "head", None)
    return jax.shard_map(
        body, mesh=grid, in_specs=(tails, rows, rows, P()), out_specs=tails, check_vma=False
    )
```

time: 448 us -> 80.7 us (0.18); the launches traced: 440 us -> 80.6 us
  waiting for transfers between devices: 277 us -> 10.3 us
  blocking collectives: 63.5 us -> 0 us
  matrix products: 39.1 us -> 0 us
  other arithmetic: 26.1 us -> 1.55 us
  starting transfers between devices: 26.7 us -> 42.3 us
  Pallas kernels: 0 us -> 11.9 us
  local copies, waits for them, and re-layouts: 5.07 us -> 11.3 us
    ppermute x127 -> x15, waiting for transfers between devices: 277 us -> 10.3 us  [shifted(): return lax.ppermute(part, axis, [(i, (i + by) % size) for i in range(size)])]
    all_gather x3 -> x0, blocking collectives: 63.5 us -> none  [merged_2(): everything = jax.tree.map(lambda part: lax.all_gather(part, axis), shard)]
    dot_general x64 -> x0, matrix products: 39.1 us -> none  [the longest x32 20 us: attend_tile(): jnp.einsum('rhgs,shd->rhgd', weights.astype(jnp.bfloat16), value_tile, pr...]
    reduce_sum x35 -> x0, other arithmetic: 17.1 us -> none  [the longest x32 16.1 us: attend_tile(): row_total = jnp.sum(weights, axis=3)]
    ppermute x127 -> x15, starting transfers between devices: 26.7 us -> 42.3 us  [shifted(): return lax.ppermute(part, axis, [(i, (i + by) % size) for i in range(size)])]
    pallas_call x0 -> x7, Pallas kernels: none -> 11.9 us  [the longest x4 6.3 us: body(): pl.pallas_call(functools.partial(attend_kernel, u, factor, chunk), out_sh...]
    add x95 -> x0, other arithmetic: 6.63 us -> none  [the longest x30 3.91 us: absorb(): running[2] * old_factor[..., None]]
    unnamed x9 -> x41, local copies, waits for them, and re-layouts: 1.25 us -> 6.52 us
  transfers between devices with their start and end apart: 127 -> 15, of which waited for: 49 -> 5; matrix products, arithmetic and copies ran while one was open for 15% -> 4% of each run, Pallas kernels for 0% -> 8%
where the time goes in v1:
time: 80.7 us; the launch traced here: 80.6 us
  starting transfers between devices  42.3 us (52%)
  Pallas kernels  11.9 us (15%)
  local copies, waits for them, and re-layouts  11.3 us (14%)
  waiting for transfers between devices  10.3 us (13%)
  between operations  3.29 us (4%)
  other arithmetic  1.55 us (2%)
    ppermute x15, starting transfers between devices, shifted(): return lax.ppermute(part, axis, [(i, (i + by) % size) for i in range(size)])  42.3 us
    ppermute x15, waiting for transfers between devices, shifted(): return lax.ppermute(part, axis, [(i, (i + by) % size) for i in range(size)])  10.3 us
    unnamed x41, local copies, waits for them, and re-layouts  6.52 us
    pallas_call x4, Pallas kernels, body(): pl.pallas_call(functools.partial(attend_kernel, u, factor, chunk), out_sh...  6.3 us
    pallas_call x1, Pallas kernels, body(): pl.pallas_call(functools.partial(column_kernel, factor), out_shape=jax.Sh...  2.09 us
    pallas_call x1, Pallas kernels, body(): pl.pallas_call(functools.partial(row_kernel, factor), out_shape=jax.Shape...  1.79 us
    pallas_call x1, Pallas kernels, body(): pl.pallas_call(functools.partial(finish_kernel, factor, kv_count, sharing...  1.73 us
    slice x1, local copies, waits for them, and re-layouts, body(): column[d:d + 1]  1.66 us
  transfers between devices with their start and end apart: 15, of which 5 were waited for; matrix products, arithmetic and copies ran while one was open for 4% of the time, Pallas kernels for 8%

profile of v1, /device:TPU:1, one launch (start us, length us, event | category | flops | bytes accessed | tf_op | source)
XLA Modules:
  0.0 80.6 jit_solution(10859916100697086315)
XLA Ops:
  0.0 1.6 %constant_dynamic-slice_fusion.3 = (bf16[1,8,16,128]{3,2,1,0:T(8,128)(2,1)S(1)}, bf16[1,8,16,128]{3,2,1,0:T(8,128)(2,1)S(1)}, bf16[1,8,16,128]{3,2,1,0:T(8,128)(...) fusion(bf16[2,8,16,128]{3,2,1,0:T(8,128)(2,1)} %bitcast.19, ...), kind=kLoop, calls=%fused_computation.12 | loop fusion | bytes 360468 | tf_op jit(solution)/shard_map/jit(dynamic_index_in_dim)/dynamic_slice | solution.py:251
  1.6 6.4 %collective-permute-start = (bf16[1,8,16,128]{3,2,1,0:T(8,128)(2,1)S(1)}, bf16[1,8,16,128]{3,2,1,0:T(8,128)(2,1)S(1)}, u32[]{:S(2)}, u32[]{:S(2)}) collective-permute-start(bf16[1,8,16,128]{3,2,1,0:T(8,128)(2,1)S(1)} %get-tuple-element.20), channel_id=1, source_target_pairs={{0,112},{16,0},{32,16},{48,32},{64,48},{80,64},{96,80},{112,96},{1... | collective-permute-start | bytes 98312 | tf_op jit(solution)/shard_map/ppermute | solution.py:19
  8.0 1.3 %collective-permute-start.3 = (bf16[1,8,16,128]{3,2,1,0:T(8,128)(2,1)S(1)}, bf16[1,8,16,128]{3,2,1,0:T(8,128)(2,1)S(1)}, u32[]{:S(2)}, u32[]{:S(2)}) collective-permute-start(bf16[1,8,16,128]{3,2,1,0:T(8,128)(2,1)S(1)} %get-tuple-element.17), channel_id=1, source_target_pairs={{0,64},{16,80},{32,96},{48,112},{64,0},{80,16},{96,32},{112,48},{1... | collective-permute-start | bytes 98312 | tf_op jit(solution)/shard_map/ppermute | solution.py:19
  9.3 0.3 collective-permute-start.2
  9.6 4.5 %collective-permute-start.1 = (bf16[1,8,16,128]{3,2,1,0:T(8,128)(2,1)S(1)}, bf16[1,8,16,128]{3,2,1,0:T(8,128)(2,1)S(1)}, u32[]{:S(2)}, u32[]{:S(2)}) collective-permute-start(bf16[1,8,16,128]{3,2,1,0:T(8,128)(2,1)S(1)} %get-tuple-element.19), channel_id=1, source_target_pairs={{0,96},{16,112},{32,0},{48,16},{64,32},{80,48},{96,64},{112,80},{1... | collective-permute-start | bytes 98312 | tf_op jit(solution)/shard_map/ppermute | solution.py:19
  14.1 0.7 copy.8
  14.8 0.1 reduce-window.9
  14.9 0.1 reduce
  15.0 0.0 collective-permute-done
  15.0 0.0 copy-start.7
  15.0 0.6 copy-done.7
  15.6 0.0 collective-permute-done.1
  15.6 0.6 copy-done.11
  16.2 0.0 collective-permute-done.2
  16.2 0.6 copy-done.9
  16.8 0.0 collective-permute-done.3
  16.8 0.8 constant_dynamic-slice_fusion
  17.6 2.5 %collective-permute-start.4 = (bf16[4,8,16,128]{3,2,1,0:T(8,128)(2,1)}, bf16[4,8,16,128]{3,2,1,0:T(8,128)(2,1)S(1)}, u32[]{:S(2)}, u32[]{:S(2)}) collective-permute-start(bf16[4,8,16,128]{3,2,1,0:T(8,128)(2,1)} %get-tuple-element.16), channel_id=1, source_target_pairs={{0,12},{4,0},{8,4},{12,8},{1,13},{5,1},{9,5},{13,9},{2,14},{6,2},{... | collective-permute-start | bytes 393224 | tf_op jit(solution)/shard_map/ppermute | solution.py:19
  20.1 0.7 fusion
  23.9 0.1 collective-permute-start.8
  24.0 1.7 %collective-permute-start.6 = (bf16[4,8,16,128]{3,2,1,0:T(8,128)(2,1)}, bf16[4,8,16,128]{3,2,1,0:T(8,128)(2,1)S(1)}, u32[]{:S(2)}, u32[]{:S(2)}) collective-permute-start(bf16[4,8,16,128]{3,2,1,0:T(8,128)(2,1)} %get-tuple-element.15), channel_id=1, source_target_pairs={{0,8},{4,12},{8,0},{12,4},{1,9},{5,13},{9,1},{13,5},{2,10},{6,14},... | collective-permute-start | bytes 393224 | tf_op jit(solution)/shard_map/ppermute | solution.py:19
  25.7 0.1 pad_add_fusion.1.live_ref
  25.8 0.0 copy-done.1
  25.8 0.1 copy.12
  25.9 1.1 %copy-done.2 = bf16[2048,2,128]{2,1,0:T(2,128)(2,1)S(1)} copy-done((bf16[2048,2,128]{2,1,0:T(2,128)(2,1)S(1)}, bf16[2048,2,128]{2,1,0:T(2,128)(2,1)}, u32[]{:S(2)}) %copy-start.2) | copy-done | bytes 1048600
  27.0 0.8 copy.10
  27.8 0.0 collective-permute-done.4.q_ref
  27.8 0.6 attend_1.1
  28.4 5.7 %collective-permute-start.5 = (f32[4,136,128]{2,1,0:T(8,128)S(1)}, f32[4,136,128]{2,1,0:T(8,128)S(1)}, u32[]{:S(2)}, u32[]{:S(2)}) collective-permute-start(f32[4,136,128]{2,1,0:T(8,128)S(1)} %attend_1.1), channel_id=1, source_target_pairs={{0,4},{4,8},{8,12},{12,0},{1,5},{5,9},{9,13},{13,1},{2,6},{6,10},{... | collective-permute-start | bytes 835592 | tf_op jit(solution)/shard_map/ppermute | solution.py:19
  34.1 0.0 collective-permute-done.6.q_ref
  34.1 0.6 attend_2.1
  34.6 0.0 copy-start.8
  34.6 0.0 copy-start.10
  34.7 0.0 copy-start.12
  34.7 0.0 copy-start.13
  34.7 0.7 collective-permute-start.7
  35.4 0.0 collective-permute-done.8.q_ref
  35.4 0.6 attend_3.1
  35.9 7.1 %collective-permute-start.9 = (f32[4,136,128]{2,1,0:T(8,128)S(1)}, f32[4,136,128]{2,1,0:T(8,128)S(1)}, u32[]{:S(2)}, u32[]{:S(2)}) collective-permute-start(f32[4,136,128]{2,1,0:T(8,128)S(1)} %attend_3.1), channel_id=1, source_target_pairs={{0,12},{4,0},{8,4},{12,8},{1,13},{5,1},{9,5},{13,9},{2,14},{6,2},{... | collective-permute-start | bytes 835592 | tf_op jit(solution)/shard_map/ppermute | solution.py:19
  43.0 0.0 copy-done.8
  43.1 4.6 %attend_0.1.refs_0_ = f32[4,136,128]{2,1,0:T(8,128)S(1)} custom-call(s32[2]{0:T(128)S(1)} %pad_add_fusion.1.live_ref, bf16[4,8,16,128]{3,2,1,0:T(8,128)(2,1)S(1)} %pad_maximum_fusion.q_ref, bf16[2,2048,128]{2,1,0:T(8,128)(2,1)S(1)} %bitcast.14, bf16[2,128,2048]{2,1,0:T(8,128)(2,1)S(1)} %bitcast.18), custom_call_target="tpu_custom_call" | custom-call | flops 536870912 | bytes 2097152 | tf_op jit(solution)/shard_map/attend_0/pallas_call | solution.py:265
  47.7 0.7 copy-done
  48.4 0.0 collective-permute-done.5.refs_1_
  48.4 0.0 collective-permute-done.7.refs_2_
  48.4 2.1 %collective-permute-done.9.refs_3_ = f32[4,136,128]{2,1,0:T(8,128)S(1)} collective-permute-done((f32[4,136,128]{2,1,0:T(8,128)S(1)}, f32[4,136,128]{2,1,0:T(8,128)S(1)}, u32[]{:S(2)}, u32[]{:S(2)}) %collective-permute-start.9) | collective-permute-done | bytes 278560 | tf_op jit(solution)/shard_map/ppermute | solution.py:19
  50.5 0.7 copy-done.5
  51.2 2.1 %merge_columns.1 = f32[5,136,128]{2,1,0:T(8,128)} custom-call(s32[1]{0:T(128)} %bitcast.2.x_ref, f32[4,136,128]{2,1,0:T(8,128)} %copy-done, f32[4,136,128]{2,1,0:T(8,128)} %copy-done.3, f32[4,136,128]{2,1,0:T(8,128)} %copy-done.4, f32[4,136,128]{2,1,0:T(8,128)} %copy-done.5), custom_call_target="tpu_custom_call" | custom-call | tf_op jit(solution)/shard_map/merge_columns/pallas_call | solution.py:281
  53.3 1.7 %fusion.2 = (f32[1,136,128]{2,1,0:T(8,128)S(1)}, f32[1,136,128]{2,1,0:T(8,128)S(1)}, f32[1,136,128]{2,1,0:T(8,128)S(1)}, f32[1,136,128]{2,1,0:T(8,128)S(1)}, f32[1,136,128]{2,1,0:T(8,128)}) fusion(f32[5,136,128]{2,1,0:T(8,128)} %merge_columns.1), kind=kLoop, calls=%fused_computation.21 | loop fusion | bytes 696320 | tf_op jit(solution)/shard_map/slice | solution.py:288
  55.0 0.4 collective-permute-start.13
  55.4 6.9 %collective-permute-start.12 = (f32[1,136,128]{2,1,0:T(8,128)S(1)}, f32[1,136,128]{2,1,0:T(8,128)S(1)}, u32[]{:S(2)}, u32[]{:S(2)}) collective-permute-start(f32[1,136,128]{2,1,0:T(8,128)S(1)} %get-tuple-element.10), channel_id=1, source_target_pairs={{0,48},{16,64},{32,80},{48,96},{64,112},{80,0},{96,16},{112,32},{1... | collective-permute-start | bytes 208904 | tf_op jit(solution)/shard_map/ppermute | solution.py:19
  62.3 0.0 collective-permute-start.11
  62.3 3.0 %collective-permute-start.10 = (f32[1,136,128]{2,1,0:T(8,128)S(1)}, f32[1,136,128]{2,1,0:T(8,128)S(1)}, u32[]{:S(2)}, u32[]{:S(2)}) collective-permute-start(f32[1,136,128]{2,1,0:T(8,128)S(1)} %get-tuple-element.12), channel_id=1, source_target_pairs={{0,16},{16,32},{32,48},{48,64},{64,80},{80,96},{96,112},{112,0},{1... | collective-permute-start | bytes 208904 | tf_op jit(solution)/shard_map/ppermute | solution.py:19
  65.3 0.6 pad_add_fusion.place_ref
  65.8 0.0 collective-permute-done.13.refs_4_
  65.8 1.1 %collective-permute-done.12.refs_3_ = f32[1,136,128]{2,1,0:T(8,128)S(1)} collective-permute-done((f32[1,136,128]{2,1,0:T(8,128)S(1)}, f32[1,136,128]{2,1,0:T(8,128)S(1)}, u32[]{:S(2)}, u32[]{:S(2)}) %collective-permute-start.12) | collective-permute-done | bytes 69664 | tf_op jit(solution)/shard_map/ppermute | solution.py:19
  66.9 3.1 %collective-permute-done.11.refs_2_ = f32[1,136,128]{2,1,0:T(8,128)S(1)} collective-permute-done((f32[1,136,128]{2,1,0:T(8,128)S(1)}, f32[1,136,128]{2,1,0:T(8,128)S(1)}, u32[]{:S(2)}, u32[]{:S(2)}) %collective-permute-start.11) | collective-permute-done | bytes 69664 | tf_op jit(solution)/shard_map/ppermute | solution.py:19
  70.1 2.7 %collective-permute-done.10.refs_1_ = f32[1,136,128]{2,1,0:T(8,128)S(1)} collective-permute-done((f32[1,136,128]{2,1,0:T(8,128)S(1)}, f32[1,136,128]{2,1,0:T(8,128)S(1)}, u32[]{:S(2)}, u32[]{:S(2)}) %collective-permute-start.10) | collective-permute-done | bytes 69664 | tf_op jit(solution)/shard_map/ppermute | solution.py:19
  72.8 0.0 copy-done.14
  72.8 0.6 copy-done.17
  73.4 1.8 %merge_rows.1.a_ref = f32[2,136,128]{2,1,0:T(8,128)} custom-call(s32[2]{0:T(128)} %pad_add_fusion.place_ref, f32[1,136,128]{2,1,0:T(8,128)} %get-tuple-element.13.refs_0_, f32[1,136,128]{2,1,0:T(8,128)} %copy-done.17, f32[1,136,128]{2,1,0:T(8,128)} %copy-done.16, f32[1,136,128]{2,1,0:T(8,128)} %copy-done.15, f32[1,136,128]{2,1,0:T(8,128)} %copy-done.14), custom_call_target="tpu_custom_call" | custom-call | tf_op jit(solution)/shard_map/merge_rows/pallas_call | solution.py:289
  75.2 1.8 %collective-permute-start.14 = (f32[2,136,128]{2,1,0:T(8,128)}, f32[2,136,128]{2,1,0:T(8,128)S(1)}, u32[]{:S(2)}, u32[]{:S(2)}) collective-permute-start(f32[2,136,128]{2,1,0:T(8,128)} %merge_rows.1.a_ref), channel_id=1, source_target_pairs={{0,128},{128,0},{1,129},{129,1},{2,130},{130,2},{3,131},{131,3},{4... | collective-permute-start | bytes 417800 | tf_op jit(solution)/shard_map/ppermute | solution.py:19
  77.0 1.2 %collective-permute-done.14.b_ref = f32[2,136,128]{2,1,0:T(8,128)S(1)} collective-permute-done((f32[2,136,128]{2,1,0:T(8,128)}, f32[2,136,128]{2,1,0:T(8,128)S(1)}, u32[]{:S(2)}, u32[]{:S(2)}) %collective-permute-start.14) | collective-permute-done | bytes 139296 | tf_op jit(solution)/shard_map/ppermute | solution.py:19
  78.2 0.6 copy-done.6
  78.9 1.7 %finish.1 = bf16[16,16,128]{2,1,0:T(8,128)(2,1)} custom-call(f32[2,136,128]{2,1,0:T(8,128)} %merge_rows.1.a_ref, f32[2,136,128]{2,1,0:T(8,128)} %copy-done.6), custom_call_target="tpu_custom_call" | custom-call | tf_op jit(solution)/shard_map/finish/pallas_call | solution.py:297
  (25 shorter events, 0.1 us)
Async XLA Ops:
  0.0 25.8 %copy-start.1 = (bf16[2048,2,128]{2,1,0:T(2,128)(2,1)S(1)}, bf16[2048,2,128]{2,1,0:T(2,128)(2,1)}, u32[]{:S(2)}) copy-start(bf16[2048,2,128]{2,1,0:T(2,128)(2,1)} %param.5) | copy-start | bytes 3145732
  1.6 13.4 %collective-permute-start = (bf16[1,8,16,128]{3,2,1,0:T(8,128)(2,1)S(1)}, bf16[1,8,16,128]{3,2,1,0:T(8,128)(2,1)S(1)}, u32[]{:S(2)}, u32[]{:S(2)}) collective-permute-start(bf16[1,8,16,128]{3,2,1,0:T(8,128)(2,1)S(1)} %get-tuple-element.20), channel_id=1, source_target_pairs={{0,112},{16,0},{32,16},{48,32},{64,48},{80,64},{96,80},{112,96},{1... | collective-permute-start | bytes 98312 | tf_op jit(solution)/shard_map/ppermute | solution.py:19
  8.0 8.8 %collective-permute-start.3 = (bf16[1,8,16,128]{3,2,1,0:T(8,128)(2,1)S(1)}, bf16[1,8,16,128]{3,2,1,0:T(8,128)(2,1)S(1)}, u32[]{:S(2)}, u32[]{:S(2)}) collective-permute-start(bf16[1,8,16,128]{3,2,1,0:T(8,128)(2,1)S(1)} %get-tuple-element.17), channel_id=1, source_target_pairs={{0,64},{16,80},{32,96},{48,112},{64,0},{80,16},{96,32},{112,48},{1... | collective-permute-start | bytes 98312 | tf_op jit(solution)/shard_map/ppermute | solution.py:19
  9.3 6.9 %collective-permute-start.2 = (bf16[1,8,16,128]{3,2,1,0:T(8,128)(2,1)S(1)}, bf16[1,8,16,128]{3,2,1,0:T(8,128)(2,1)S(1)}, u32[]{:S(2)}, u32[]{:S(2)}) collective-permute-start(bf16[1,8,16,128]{3,2,1,0:T(8,128)(2,1)S(1)} %get-tuple-element.18), channel_id=1, source_target_pairs={{0,80},{16,96},{32,112},{48,0},{64,16},{80,32},{96,48},{112,64},{1... | collective-permute-start | bytes 98312 | tf_op jit(solution)/shard_map/ppermute | solution.py:19
  9.6 6.0 %collective-permute-start.1 = (bf16[1,8,16,128]{3,2,1,0:T(8,128)(2,1)S(1)}, bf16[1,8,16,128]{3,2,1,0:T(8,128)(2,1)S(1)}, u32[]{:S(2)}, u32[]{:S(2)}) collective-permute-start(bf16[1,8,16,128]{3,2,1,0:T(8,128)(2,1)S(1)} %get-tuple-element.19), channel_id=1, source_target_pairs={{0,96},{16,112},{32,0},{48,16},{64,32},{80,48},{96,64},{112,80},{1... | collective-permute-start | bytes 98312 | tf_op jit(solution)/shard_map/ppermute | solution.py:19
  15.0 0.6 copy-start.7
  15.6 0.6 copy-start.11
  16.2 0.6 copy-start.9
  17.6 10.2 %collective-permute-start.4 = (bf16[4,8,16,128]{3,2,1,0:T(8,128)(2,1)}, bf16[4,8,16,128]{3,2,1,0:T(8,128)(2,1)S(1)}, u32[]{:S(2)}, u32[]{:S(2)}) collective-permute-start(bf16[4,8,16,128]{3,2,1,0:T(8,128)(2,1)} %get-tuple-element.16), channel_id=1, source_target_pairs={{0,12},{4,0},{8,4},{12,8},{1,13},{5,1},{9,5},{13,9},{2,14},{6,2},{... | collective-permute-start | bytes 393224 | tf_op jit(solution)/shard_map/ppermute | solution.py:19
  23.9 11.5 %collective-permute-start.8 = (bf16[4,8,16,128]{3,2,1,0:T(8,128)(2,1)}, bf16[4,8,16,128]{3,2,1,0:T(8,128)(2,1)S(1)}, u32[]{:S(2)}, u32[]{:S(2)}) collective-permute-start(bf16[4,8,16,128]{3,2,1,0:T(8,128)(2,1)} %get-tuple-element.14), channel_id=1, source_target_pairs={{0,4},{4,8},{8,12},{12,0},{1,5},{5,9},{9,13},{13,1},{2,6},{6,10},{... | collective-permute-start | bytes 393224 | tf_op jit(solution)/shard_map/ppermute | solution.py:19
  24.0 10.1 %collective-permute-start.6 = (bf16[4,8,16,128]{3,2,1,0:T(8,128)(2,1)}, bf16[4,8,16,128]{3,2,1,0:T(8,128)(2,1)S(1)}, u32[]{:S(2)}, u32[]{:S(2)}) collective-permute-start(bf16[4,8,16,128]{3,2,1,0:T(8,128)(2,1)} %get-tuple-element.15), channel_id=1, source_target_pairs={{0,8},{4,12},{8,0},{12,4},{1,9},{5,13},{9,1},{13,5},{2,10},{6,14},... | collective-permute-start | bytes 393224 | tf_op jit(solution)/shard_map/ppermute | solution.py:19
  25.8 1.2 %copy-start.2 = (bf16[2048,2,128]{2,1,0:T(2,128)(2,1)S(1)}, bf16[2048,2,128]{2,1,0:T(2,128)(2,1)}, u32[]{:S(2)}) copy-start(bf16[2048,2,128]{2,1,0:T(2,128)(2,1)} %param.6) | copy-start | bytes 3145732
  28.4 20.0 %collective-permute-start.5 = (f32[4,136,128]{2,1,0:T(8,128)S(1)}, f32[4,136,128]{2,1,0:T(8,128)S(1)}, u32[]{:S(2)}, u32[]{:S(2)}) collective-permute-start(f32[4,136,128]{2,1,0:T(8,128)S(1)} %attend_1.1), channel_id=1, source_target_pairs={{0,4},{4,8},{8,12},{12,0},{1,5},{5,9},{9,13},{13,1},{2,6},{6,10},{... | collective-permute-start | bytes 835592 | tf_op jit(solution)/shard_map/ppermute | solution.py:19
  34.6 8.4 %copy-start.8 = (bf16[1,8,16,128]{3,2,1,0:T(8,128)(2,1)S(1)}, bf16[1,8,16,128]{3,2,1,0:T(8,128)(2,1)}, u32[]{:S(2)}) copy-start(bf16[1,8,16,128]{3,2,1,0:T(8,128)(2,1)} %copy-done.7) | copy-start | bytes 98308
  34.6 8.4 %copy-start.10 = (bf16[1,8,16,128]{3,2,1,0:T(8,128)(2,1)S(1)}, bf16[1,8,16,128]{3,2,1,0:T(8,128)(2,1)}, u32[]{:S(2)}) copy-start(bf16[1,8,16,128]{3,2,1,0:T(8,128)(2,1)} %copy-done.9) | copy-start | bytes 98308
  34.7 8.4 %copy-start.12 = (bf16[1,8,16,128]{3,2,1,0:T(8,128)(2,1)S(1)}, bf16[1,8,16,128]{3,2,1,0:T(8,128)(2,1)}, u32[]{:S(2)}) copy-start(bf16[1,8,16,128]{3,2,1,0:T(8,128)(2,1)} %copy-done.11) | copy-start | bytes 98308
  34.7 8.4 %copy-start.13 = (bf16[1,8,16,128]{3,2,1,0:T(8,128)(2,1)S(1)}, bf16[1,8,16,128]{3,2,1,0:T(8,128)(2,1)}, u32[]{:S(2)}) copy-start(bf16[1,8,16,128]{3,2,1,0:T(8,128)(2,1)} %get-tuple-element.22) | copy-start | bytes 98308
  34.7 13.7 %collective-permute-start.7 = (f32[4,136,128]{2,1,0:T(8,128)S(1)}, f32[4,136,128]{2,1,0:T(8,128)S(1)}, u32[]{:S(2)}, u32[]{:S(2)}) collective-permute-start(f32[4,136,128]{2,1,0:T(8,128)S(1)} %attend_2.1), channel_id=1, source_target_pairs={{0,8},{4,12},{8,0},{12,4},{1,9},{5,13},{9,1},{13,5},{2,10},{6,14},... | collective-permute-start | bytes 835592 | tf_op jit(solution)/shard_map/ppermute | solution.py:19
  35.9 14.6 %collective-permute-start.9 = (f32[4,136,128]{2,1,0:T(8,128)S(1)}, f32[4,136,128]{2,1,0:T(8,128)S(1)}, u32[]{:S(2)}, u32[]{:S(2)}) collective-permute-start(f32[4,136,128]{2,1,0:T(8,128)S(1)} %attend_3.1), channel_id=1, source_target_pairs={{0,12},{4,0},{8,4},{12,8},{1,13},{5,1},{9,5},{13,9},{2,14},{6,2},{... | collective-permute-start | bytes 835592 | tf_op jit(solution)/shard_map/ppermute | solution.py:19
  47.7 0.7 copy-start
  48.4 2.1 %copy-start.3 = (f32[4,136,128]{2,1,0:T(8,128)}, f32[4,136,128]{2,1,0:T(8,128)S(1)}, u32[]{:S(2)}) copy-start(f32[4,136,128]{2,1,0:T(8,128)S(1)} %collective-permute-done.5.refs_1_) | copy-start | bytes 835588
  48.4 2.1 %copy-start.4 = (f32[4,136,128]{2,1,0:T(8,128)}, f32[4,136,128]{2,1,0:T(8,128)S(1)}, u32[]{:S(2)}) copy-start(f32[4,136,128]{2,1,0:T(8,128)S(1)} %collective-permute-done.7.refs_2_) | copy-start | bytes 835588
  50.5 0.7 copy-start.5
  55.0 10.9 %collective-permute-start.13 = (f32[1,136,128]{2,1,0:T(8,128)S(1)}, f32[1,136,128]{2,1,0:T(8,128)S(1)}, u32[]{:S(2)}, u32[]{:S(2)}) collective-permute-start(f32[1,136,128]{2,1,0:T(8,128)S(1)} %get-tuple-element.9), channel_id=1, source_target_pairs={{0,64},{16,80},{32,96},{48,112},{64,0},{80,16},{96,32},{112,48},{1... | collective-permute-start | bytes 208904 | tf_op jit(solution)/shard_map/ppermute | solution.py:19
  55.4 11.5 %collective-permute-start.12 = (f32[1,136,128]{2,1,0:T(8,128)S(1)}, f32[1,136,128]{2,1,0:T(8,128)S(1)}, u32[]{:S(2)}, u32[]{:S(2)}) collective-permute-start(f32[1,136,128]{2,1,0:T(8,128)S(1)} %get-tuple-element.10), channel_id=1, source_target_pairs={{0,48},{16,64},{32,80},{48,96},{64,112},{80,0},{96,16},{112,32},{1... | collective-permute-start | bytes 208904 | tf_op jit(solution)/shard_map/ppermute | solution.py:19
  62.3 7.8 %collective-permute-start.11 = (f32[1,136,128]{2,1,0:T(8,128)S(1)}, f32[1,136,128]{2,1,0:T(8,128)S(1)}, u32[]{:S(2)}, u32[]{:S(2)}) collective-permute-start(f32[1,136,128]{2,1,0:T(8,128)S(1)} %get-tuple-element.11), channel_id=1, source_target_pairs={{0,32},{16,48},{32,64},{48,80},{64,96},{80,112},{96,0},{112,16},{1... | collective-permute-start | bytes 208904 | tf_op jit(solution)/shard_map/ppermute | solution.py:19
  62.3 10.5 %collective-permute-start.10 = (f32[1,136,128]{2,1,0:T(8,128)S(1)}, f32[1,136,128]{2,1,0:T(8,128)S(1)}, u32[]{:S(2)}, u32[]{:S(2)}) collective-permute-start(f32[1,136,128]{2,1,0:T(8,128)S(1)} %get-tuple-element.12), channel_id=1, source_target_pairs={{0,16},{16,32},{32,48},{48,64},{64,80},{80,96},{96,112},{112,0},{1... | collective-permute-start | bytes 208904 | tf_op jit(solution)/shard_map/ppermute | solution.py:19
  65.8 7.0 %copy-start.14 = (f32[1,136,128]{2,1,0:T(8,128)}, f32[1,136,128]{2,1,0:T(8,128)S(1)}, u32[]{:S(2)}) copy-start(f32[1,136,128]{2,1,0:T(8,128)S(1)} %collective-permute-done.13.refs_4_) | copy-start | bytes 208900
  66.9 5.9 %copy-start.15 = (f32[1,136,128]{2,1,0:T(8,128)}, f32[1,136,128]{2,1,0:T(8,128)S(1)}, u32[]{:S(2)}) copy-start(f32[1,136,128]{2,1,0:T(8,128)S(1)} %collective-permute-done.12.refs_3_) | copy-start | bytes 208900
  70.1 2.7 %copy-start.16 = (f32[1,136,128]{2,1,0:T(8,128)}, f32[1,136,128]{2,1,0:T(8,128)S(1)}, u32[]{:S(2)}) copy-start(f32[1,136,128]{2,1,0:T(8,128)S(1)} %collective-permute-done.11.refs_2_) | copy-start | bytes 208900
  72.8 0.6 copy-start.17
  75.2 3.0 %collective-permute-start.14 = (f32[2,136,128]{2,1,0:T(8,128)}, f32[2,136,128]{2,1,0:T(8,128)S(1)}, u32[]{:S(2)}, u32[]{:S(2)}) collective-permute-start(f32[2,136,128]{2,1,0:T(8,128)} %merge_rows.1.a_ref), channel_id=1, source_target_pairs={{0,128},{128,0},{1,129},{129,1},{2,130},{130,2},{3,131},{131,3},{4... | collective-permute-start | bytes 417800 | tf_op jit(solution)/shard_map/ppermute | solution.py:19
  78.2 0.7 copy-start.6

commit v2 on v0

v2 whole, which is shorter than its diff:
```python
import functools
import math

import jax
import jax.numpy as jnp
from jax import lax
from jax.experimental import pallas as pl
from jax.experimental.pallas import tpu as pltpu
from jax.sharding import Mesh, PartitionSpec as P

BLOCK = 128
NEGATIVE = -1e30
TAIL = 8
EXTRA = 8
COLUMNS = 4
REACH = 4


def shifted(part, axes, by):
    size = lax.axis_size(axes)
    return lax.ppermute(part, axes, [(i, (i + by) % size) for i in range(size)])


def own_kernel(kv_count, o_ref, q_ref, out_ref):
    tail = TAIL
    sharing = q_ref.shape[1] // kv_count
    mine = q_ref[pl.ds(o_ref[0] * tail, tail)].astype(jnp.float32)
    rows = [
        mine[:, h * sharing : (h + 1) * sharing, :].reshape(tail * sharing, -1)
        for h in range(kv_count)
    ]
    out_ref[...] = jnp.transpose(jnp.concatenate(rows, axis=0)).astype(out_ref.dtype)


def stack_kernel(*refs):
    blocks, out_ref = refs[:-1], refs[-1]
    kv_count = out_ref.shape[0]
    wide = out_ref.shape[2] // len(blocks)
    for h in range(kv_count):
        out_ref[h] = jnp.concatenate(
            [b[:, h * wide : (h + 1) * wide] for b in blocks], axis=1
        )


def attend_kernel(own, factor, live_ref, q_ref, k_ref, v_ref, out_ref, s_ref):
    kv_count, key_rows, dim = k_ref.shape
    width = q_ref.shape[2]
    blocks = out_ref.shape[0]
    wide = width // blocks
    sharing = wide // TAIL
    n_live = live_ref[0]
    first = live_ref[1]
    count = key_rows // BLOCK

    @pl.when(own >= n_live)
    def _():
        out_ref[:, :dim, :] = jnp.zeros((blocks, dim, kv_count * wide), jnp.float32)
        row = lax.broadcasted_iota(jnp.int32, (blocks, EXTRA, kv_count * wide), 1)
        out_ref[:, dim:, :] = jnp.where(row == 0, NEGATIVE, 0.0)

    @pl.when(own < n_live)
    def _():
        tops, totals, outputs = [], [], []
        for h in range(kv_count):
            s = jnp.dot(k_ref[h], q_ref[h], preferred_element_type=jnp.float32)
            s_ref[h] = s
            peak = jnp.full((8, width), NEGATIVE, jnp.float32)
            for b in range(count):
                rows = s[b * BLOCK : (b + 1) * BLOCK]
                if own == 0 and b == count - 1:
                    lane = lax.broadcasted_iota(jnp.int32, (8, width), 1)
                    late = lax.broadcasted_iota(jnp.int32, (8, width), 0)
                    ahead = (lane < wide) & (late > lane // sharing)
                    corner = jnp.where(ahead, NEGATIVE, rows[BLOCK - 8 :])
                    s_ref[h, key_rows - 8 :, :] = corner
                    peak = jnp.maximum(peak, corner)
                    rows = rows[: BLOCK - 8]
                top = jnp.max(rows.reshape(-1, 8, width), axis=0)
                peak = jnp.maximum(peak, jnp.where(b >= first, top, NEGATIVE))
            tops.append(jnp.max(peak, axis=0, keepdims=True))
        for h in range(kv_count):
            total = jnp.zeros((8, width), jnp.float32)
            parts = []
            for b in range(count):
                s = s_ref[h, b * BLOCK : (b + 1) * BLOCK, :]
                level = jnp.where(b >= first, tops[h], -NEGATIVE)
                w = jnp.exp2((s - level) * factor)
                total = total + jnp.sum(w.reshape(-1, 8, width), axis=0)
                parts.append(w.astype(jnp.bfloat16))
            totals.append(jnp.sum(total, axis=0, keepdims=True))
            outputs.append(
                jnp.dot(v_ref[h], jnp.concatenate(parts, axis=0), preferred_element_type=jnp.float32)
            )
        row = lax.broadcasted_iota(jnp.int32, (EXTRA, kv_count * wide), 0)
        for j in range(blocks):
            lanes = slice(j * wide, (j + 1) * wide)
            keep = own + blocks * j < n_live
            o = jnp.concatenate([a[:, lanes] for a in outputs], axis=1)
            m = jnp.concatenate([a[:, lanes] for a in tops], axis=1)
            l = jnp.concatenate([a[:, lanes] for a in totals], axis=1)
            out_ref[j, :dim, :] = jnp.where(keep, o, 0.0)
            out_ref[j, dim:, :] = jnp.where(
                row == 0,
                jnp.where(keep, m, NEGATIVE),
                jnp.where((row == 1) & keep, l, 0.0),
            )


def merge(parts, factor):
    top = functools.reduce(jnp.maximum, [m for _, m, _ in parts])
    o = l = None
    for po, pm, pt in parts:
        f = jnp.exp2((pm - top) * factor)
        o = po * f if o is None else o + po * f
        l = pt * f if l is None else l + pt * f
    return o, top, l


def column_kernel(factor, *refs):
    parts, outs = refs[:COLUMNS], refs[COLUMNS:]
    dim = outs[0].shape[0] - EXTRA
    for j, out in enumerate(outs):
        found = [(p[j, :dim], p[j, dim : dim + 1], p[j, dim + 1 : dim + 2]) for p in parts]
        o, m, l = merge(found, factor)
        row = lax.broadcasted_iota(jnp.int32, (EXTRA, m.shape[1]), 0)
        out[:dim] = o
        out[dim:] = jnp.where(row == 0, m, jnp.where(row == 1, l, 0.0))


def finish_kernel(factor, kv_count, *refs):
    parts, out_ref = refs[:-1], refs[-1]
    dim = out_ref.shape[2]
    found = [(p[:dim], p[dim : dim + 1], p[dim + 1 : dim + 2]) for p in parts]
    o, _, l = merge(found, factor)
    res = jnp.transpose(o / l).reshape(kv_count, TAIL, -1, dim)
    out_ref[...] = jnp.concatenate([res[h] for h in range(kv_count)], axis=1).astype(out_ref.dtype)


def on_chip(count):
    return [pl.BlockSpec(memory_space=pltpu.VMEM)] * count


def room(mebibytes):
    return pltpu.CompilerParams(vmem_limit_bytes=mebibytes << 20)


def scalars():
    return [pl.BlockSpec(memory_space=pltpu.SMEM)]


def body(queries, keys, values, doc_lengths):
    rows, columns, groups = lax.axis_size("z"), lax.axis_size("x"), lax.axis_size("outer")
    o, z, x = lax.axis_index("outer"), lax.axis_index("z"), lax.axis_index("x")
    key_rows, kv_count, dim = keys.shape
    heads = queries.shape[1]
    sharing = heads // kv_count
    lanes = kv_count * TAIL * sharing
    width = REACH * TAIL * sharing
    factor = math.log2(math.e) / math.sqrt(dim)

    own = pl.pallas_call(
        functools.partial(own_kernel, kv_count),
        out_shape=jax.ShapeDtypeStruct((dim, lanes), queries.dtype),
        in_specs=scalars() + on_chip(1),
        out_specs=on_chip(1)[0],
        compiler_params=room(4),
        name="own_tails",
    )(o.reshape(1).astype(jnp.int32), queries)
    held = [own] + [shifted(own, ("outer", "z"), -j) for j in range(1, REACH)]

    segment = (o * rows + z) * columns + x
    blocks = key_rows // BLOCK
    ends = jnp.cumsum(doc_lengths)
    last = segment * blocks + blocks - 1
    start = jnp.max(jnp.where(ends <= last, ends, 0))
    end = jnp.min(jnp.where(ends > last, ends, rows * columns * groups * blocks))
    live = jnp.stack([end // blocks - segment, jnp.maximum(start - segment * blocks, 0)])
    live = live.astype(jnp.int32)
    k_heads = jnp.transpose(keys, (1, 0, 2))
    v_heads = jnp.transpose(values, (1, 2, 0))
    held, live, k_heads, v_heads = lax.optimization_barrier((held, live, k_heads, v_heads))

    stack = pl.pallas_call(
        stack_kernel,
        out_shape=jax.ShapeDtypeStruct((kv_count, dim, width), queries.dtype),
        in_specs=on_chip(REACH),
        out_specs=on_chip(1)[0],
        compiler_params=room(4),
        name="stack_tails",
    )(*held)
    everywhere = ("outer", "z", "x")
    asked = [stack] + [shifted(stack, everywhere, -u) for u in range(1, columns)]

    partial = []
    for u in range(columns):
        block = asked[u]
        if u == 1:
            block, _ = lax.optimization_barrier((block, partial[0]))
        partial.append(
            pl.pallas_call(
                functools.partial(attend_kernel, u, factor),
                out_shape=jax.ShapeDtypeStruct((REACH, dim + EXTRA, lanes), jnp.float32),
                in_specs=scalars() + on_chip(3),
                out_specs=on_chip(1)[0],
                scratch_shapes=[pltpu.VMEM((kv_count, key_rows, width), jnp.float32)],
                cost_estimate=pl.CostEstimate(
                    flops=4 * kv_count * key_rows * width * dim,
                    bytes_accessed=4 * kv_count * key_rows * dim,
                    transcendentals=kv_count * key_rows * width,
                ),
                compiler_params=room(16),
                name=f"attend_{u}",
            )(live, block, k_heads, v_heads)
        )
    arrived = [partial[0]] + [shifted(partial[u], everywhere, u) for u in range(1, columns)]
    column = pl.pallas_call(
        functools.partial(column_kernel, factor),
        out_shape=[jax.ShapeDtypeStruct((dim + EXTRA, lanes), jnp.float32)] * REACH,
        in_specs=on_chip(columns),
        out_specs=on_chip(REACH),
        compiler_params=room(4),
        name="merge_columns",
    )(*arrived)
    arrived = [column[0]] + [shifted(column[j], ("outer", "z"), j) for j in range(1, REACH)]
    mine = pl.pallas_call(
        functools.partial(finish_kernel, factor, kv_count),
        out_shape=jax.ShapeDtypeStruct((TAIL, heads, dim), queries.dtype),
        in_specs=on_chip(REACH),
        out_specs=on_chip(1)[0],
        compiler_params=room(4),
        name="finish",
    )(*arrived)
    other = shifted(mine, "outer", 1)
    first = jnp.where(o == 0, mine, other)
    second = jnp.where(o == 0, other, mine)
    return jnp.concatenate([first, second], axis=0)


def solution(mesh):
    outer, inner, head = (mesh.shape[a] for a in ("outer", "inner", "head"))
    grid = Mesh(
        mesh.devices.reshape(outer, inner // COLUMNS, COLUMNS, head),
        ("outer", "z", "x", "head"),
    )
    tails = P(("z", "x"), "head", None)
    rows = P(("outer", "z", "x"), "head", None)
    return jax.shard_map(
        body, mesh=grid, in_specs=(tails, rows, rows, P()), out_specs=tails, check_vma=False
    )
```

time: 448 us -> 64.2 us (0.14)
  the two profiles are of different devices: /device:TPU:1 before, /device:TPU:51 now
where the time goes in v2:
time: 64.2 us; the launch traced here: 63.8 us
  waiting for transfers between devices  24.5 us (38%)
  starting transfers between devices  20.8 us (32%)
  Pallas kernels  9.92 us (15%)
  local copies, waits for them, and re-layouts  3.91 us (6%)
  between operations  3.09 us (5%)
  other arithmetic  1.6 us (2%)
    ppermute x13, waiting for transfers between devices, shifted(): return lax.ppermute(part, axes, [(i, (i + by) % size) for i in range(size)])  24.5 us
    ppermute x13, starting transfers between devices, shifted(): return lax.ppermute(part, axes, [(i, (i + by) % size) for i in range(size)])  20.8 us
    pallas_call x4, Pallas kernels, body(): pl.pallas_call(functools.partial(attend_kernel, u, factor), out_shape=jax...  9.51 us
    unnamed x8, local copies, waits for them, and re-layouts  3.83 us
  transfers between devices with their start and end apart: 13, of which 6 were waited for; matrix products, arithmetic and copies ran while one was open for 5% of the time, Pallas kernels for 15%

profile of v2, /device:TPU:51, one launch (start us, length us, event | category | flops | bytes accessed | tf_op | source)
XLA Modules:
  0.0 63.8 jit_solution(1416580446558924573)
XLA Ops:
  0.0 0.0 copy-start
  0.0 0.8 %copy-done = bf16[16,16,128]{2,1,0:T(8,128)(2,1)S(1)} copy-done((bf16[16,16,128]{2,1,0:T(8,128)(2,1)S(1)}, bf16[16,16,128]{2,1,0:T(8,128)(2,1)}, u32[]{:S(2)}) %copy-start) | copy-done | bytes 65560
  0.8 0.1 own_tails.1.refs_0_
  0.9 6.2 %collective-permute-start.2 = (bf16[128,128]{1,0:T(8,128)(2,1)S(1)}, bf16[128,128]{1,0:T(8,128)(2,1)S(1)}, u32[]{:S(2)}, u32[]{:S(2)}) collective-permute-start(bf16[128,128]{1,0:T(8,128)(2,1)S(1)} %own_tails.1.refs_0_), channel_id=1, source_target_pairs={{0,208},{16,224},{32,240},{48,0},{64,16},{80,32},{96,48},{112,64},... | collective-permute-start | bytes 98312 | tf_op jit(solution)/shard_map/ppermute | solution.py:21
  7.2 1.4 %collective-permute-start.1 = (bf16[128,128]{1,0:T(8,128)(2,1)S(1)}, bf16[128,128]{1,0:T(8,128)(2,1)S(1)}, u32[]{:S(2)}, u32[]{:S(2)}) collective-permute-start(bf16[128,128]{1,0:T(8,128)(2,1)S(1)} %own_tails.1.refs_0_), channel_id=1, source_target_pairs={{0,224},{16,240},{32,0},{48,16},{64,32},{80,48},{96,64},{112,80},{... | collective-permute-start | bytes 98312 | tf_op jit(solution)/shard_map/ppermute | solution.py:21
  8.6 0.0 collective-permute-start
  8.6 0.0 copy-start.2
  8.6 0.7 %copy-done.2 = s32[32]{0:T(128)S(1)} copy-done((s32[32]{0:T(128)S(1)}, s32[32]{0:T(128)}, u32[]{:S(2)}) %copy-start.2) | copy-done | bytes 152
  9.3 0.1 copy.8
  9.3 0.1 reduce-window.9
  9.4 0.1 reduce
  9.5 0.7 %fusion = (s32[]{:T(128)}, s32[]{:T(128)}) fusion(s32[32]{0:T(128)S(1)} %reduce, s32[]{:T(128)S(6)} %sub.13), kind=kLoop, calls=%fused_computation.6 | loop fusion | flops 190 | bytes 140 | tf_op jit(solution)/shard_map/reduce_min | solution.py:176
  13.2 0.1 pad_add_fusion.live_ref
  13.2 0.0 copy-start.1
  13.2 1.4 %copy.12 = bf16[2048,2,128]{2,0,1:T(8,128)(2,1)S(1)} copy(bf16[2048,2,128]{2,1,0:T(2,128)(2,1)} %param.5) | data formatting | bytes 2097152 | tf_op args[1]
  14.7 0.1 copy-done.1
  14.8 0.8 %copy.10 = bf16[2048,2,128]{0,2,1:T(8,128)(2,1)S(1)} copy(bf16[2048,2,128]{2,1,0:T(2,128)(2,1)S(1)} %copy-done.1) | data formatting | bytes 2097152 | tf_op args[2]
  15.6 0.0 collective-permute-done.2.refs_3_
  15.6 0.0 collective-permute-done.1.refs_2_
  15.6 0.0 collective-permute-done.refs_1_
  15.6 0.1 stack_tails.1.q_ref
  15.7 0.3 collective-permute-start.3
  16.1 1.2 %collective-permute-start.7 = (bf16[2,128,256]{2,1,0:T(8,128)(2,1)S(1)}, bf16[2,128,256]{2,1,0:T(8,128)(2,1)S(1)}, u32[]{:S(2)}, u32[]{:S(2)}) collective-permute-start(bf16[2,128,256]{2,1,0:T(8,128)(2,1)S(1)} %stack_tails.1.q_ref), channel_id=1, source_target_pairs={{0,244},{4,248},{8,252},{12,0},{16,4},{20,8},{24,12},{28,16},{32,2... | collective-permute-start | bytes 393224 | tf_op jit(solution)/shard_map/ppermute | solution.py:21
  17.3 3.4 %collective-permute-start.5 = (bf16[2,128,256]{2,1,0:T(8,128)(2,1)S(1)}, bf16[2,128,256]{2,1,0:T(8,128)(2,1)S(1)}, u32[]{:S(2)}, u32[]{:S(2)}) collective-permute-start(bf16[2,128,256]{2,1,0:T(8,128)(2,1)S(1)} %stack_tails.1.q_ref), channel_id=1, source_target_pairs={{0,248},{4,252},{8,0},{12,4},{16,8},{20,12},{24,16},{28,20},{32,24... | collective-permute-start | bytes 393224 | tf_op jit(solution)/shard_map/ppermute | solution.py:21
  20.7 2.4 %attend_0.1.refs_0_ = f32[4,136,128]{2,1,0:T(8,128)S(1)} custom-call(s32[2]{0:T(128)S(1)} %pad_add_fusion.live_ref, bf16[2,128,256]{2,1,0:T(8,128)(2,1)S(1)} %stack_tails.1.q_ref, bf16[2,2048,128]{2,1,0:T(8,128)(2,1)S(1)} %bitcast.8, bf16[2,128,2048]{2,1,0:T(8,128)(2,1)S(1)} %bitcast.12), custom_call_target="tpu_custom_call" | custom-call | flops 536870912 | bytes 2097152 | tf_op jit(solution)/shard_map/attend_0/pallas_call | solution.py:200
  23.1 0.0 collective-permute-done.3.q_ref
  23.1 2.3 %attend_1.1 = f32[4,136,128]{2,1,0:T(8,128)S(1)} custom-call(s32[2]{0:T(128)S(1)} %pad_add_fusion.live_ref, bf16[2,128,256]{2,1,0:T(8,128)(2,1)S(1)} %collective-permute-done.3.q_ref, bf16[2,2048,128]{2,1,0:T(8,128)(2,1)S(1)} %bitcast.9, bf16[2,128,2048]{2,1,0:T(8,128)(2,1)S(1)} %bitcast.13), custom_call_target="tpu_custom_call" | custom-call | flops 536870912 | bytes 2097152 | tf_op jit(solution)/shard_map/attend_1/pallas_call | solution.py:200
  25.4 0.1 collective-permute-start.4
  25.5 0.7 %collective-permute-done.7.q_ref = bf16[2,128,256]{2,1,0:T(8,128)(2,1)S(1)} collective-permute-done((bf16[2,128,256]{2,1,0:T(8,128)(2,1)S(1)}, bf16[2,128,256]{2,1,0:T(8,128)(2,1)S(1)}, u32[]{:S(2)}, u32[]{:S(2)}) %collective-permute-start.7) | collective-permute-done | bytes 131104 | tf_op jit(solution)/shard_map/ppermute | solution.py:21
  26.2 2.3 %attend_3.1 = f32[4,136,128]{2,1,0:T(8,128)S(1)} custom-call(s32[2]{0:T(128)S(1)} %pad_add_fusion.live_ref, bf16[2,128,256]{2,1,0:T(8,128)(2,1)S(1)} %collective-permute-done.7.q_ref, bf16[2,2048,128]{2,1,0:T(8,128)(2,1)S(1)} %bitcast.10, bf16[2,128,2048]{2,1,0:T(8,128)(2,1)S(1)} %bitcast.14), custom_call_target="tpu_custom_call" | custom-call | flops 536870912 | bytes 2097152 | tf_op jit(solution)/shard_map/attend_3/pallas_call | solution.py:200
  28.5 1.4 %collective-permute-start.8 = (f32[4,136,128]{2,1,0:T(8,128)S(1)}, f32[4,136,128]{2,1,0:T(8,128)S(1)}, u32[]{:S(2)}, u32[]{:S(2)}) collective-permute-start(f32[4,136,128]{2,1,0:T(8,128)S(1)} %attend_3.1), channel_id=1, source_target_pairs={{0,12},{4,16},{8,20},{12,24},{16,28},{20,32},{24,36},{28,40},{32,4... | collective-permute-start | bytes 835592 | tf_op jit(solution)/shard_map/ppermute | solution.py:21
  29.9 0.0 collective-permute-done.5.q_ref
  29.9 2.5 %attend_2.1 = f32[4,136,128]{2,1,0:T(8,128)S(1)} custom-call(s32[2]{0:T(128)S(1)} %pad_add_fusion.live_ref, bf16[2,128,256]{2,1,0:T(8,128)(2,1)S(1)} %collective-permute-done.5.q_ref, bf16[2,2048,128]{2,1,0:T(8,128)(2,1)S(1)} %bitcast.11, bf16[2,128,2048]{2,1,0:T(8,128)(2,1)S(1)} %bitcast.15), custom_call_target="tpu_custom_call" | custom-call | flops 536870912 | bytes 2097152 | tf_op jit(solution)/shard_map/attend_2/pallas_call | solution.py:200
  32.4 2.6 %collective-permute-start.6 = (f32[4,136,128]{2,1,0:T(8,128)S(1)}, f32[4,136,128]{2,1,0:T(8,128)S(1)}, u32[]{:S(2)}, u32[]{:S(2)}) collective-permute-start(f32[4,136,128]{2,1,0:T(8,128)S(1)} %attend_2.1), channel_id=1, source_target_pairs={{0,8},{4,12},{8,16},{12,20},{16,24},{20,28},{24,32},{28,36},{32,40... | collective-permute-start | bytes 835592 | tf_op jit(solution)/shard_map/ppermute | solution.py:21
  35.0 0.0 collective-permute-done.4.refs_1_
  35.1 2.7 %collective-permute-done.8.refs_3_ = f32[4,136,128]{2,1,0:T(8,128)S(1)} collective-permute-done((f32[4,136,128]{2,1,0:T(8,128)S(1)}, f32[4,136,128]{2,1,0:T(8,128)S(1)}, u32[]{:S(2)}, u32[]{:S(2)}) %collective-permute-start.8) | collective-permute-done | bytes 278560 | tf_op jit(solution)/shard_map/ppermute | solution.py:21
  37.8 9.5 %collective-permute-done.6.refs_2_ = f32[4,136,128]{2,1,0:T(8,128)S(1)} collective-permute-done((f32[4,136,128]{2,1,0:T(8,128)S(1)}, f32[4,136,128]{2,1,0:T(8,128)S(1)}, u32[]{:S(2)}, u32[]{:S(2)}) %collective-permute-start.6) | collective-permute-done | bytes 278560 | tf_op jit(solution)/shard_map/ppermute | solution.py:21
  47.3 0.1 merge_columns.1
  47.4 0.1 collective-permute-start.9
  47.5 0.9 %collective-permute-start.10 = (f32[136,128]{1,0:T(8,128)S(1)}, f32[136,128]{1,0:T(8,128)S(1)}, u32[]{:S(2)}, u32[]{:S(2)}) collective-permute-start(f32[136,128]{1,0:T(8,128)S(1)} %get-tuple-element.27), channel_id=1, source_target_pairs={{0,32},{16,48},{32,64},{48,80},{64,96},{80,112},{96,128},{112,144}... | collective-permute-start | bytes 208904 | tf_op jit(solution)/shard_map/ppermute | solution.py:21
  48.4 2.5 %collective-permute-start.11 = (f32[136,128]{1,0:T(8,128)S(1)}, f32[136,128]{1,0:T(8,128)S(1)}, u32[]{:S(2)}, u32[]{:S(2)}) collective-permute-start(f32[136,128]{1,0:T(8,128)S(1)} %get-tuple-element.28), channel_id=1, source_target_pairs={{0,48},{16,64},{32,80},{48,96},{64,112},{80,128},{96,144},{112,160... | collective-permute-start | bytes 208904 | tf_op jit(solution)/shard_map/ppermute | solution.py:21
  50.9 0.0 collective-permute-done.9.refs_1_
  50.9 3.1 %collective-permute-done.10.refs_2_ = f32[136,128]{1,0:T(8,128)S(1)} collective-permute-done((f32[136,128]{1,0:T(8,128)S(1)}, f32[136,128]{1,0:T(8,128)S(1)}, u32[]{:S(2)}, u32[]{:S(2)}) %collective-permute-start.10) | collective-permute-done | bytes 69664 | tf_op jit(solution)/shard_map/ppermute | solution.py:21
  54.0 7.5 %collective-permute-done.11.refs_3_ = f32[136,128]{1,0:T(8,128)S(1)} collective-permute-done((f32[136,128]{1,0:T(8,128)S(1)}, f32[136,128]{1,0:T(8,128)S(1)}, u32[]{:S(2)}, u32[]{:S(2)}) %collective-permute-start.11) | collective-permute-done | bytes 69664 | tf_op jit(solution)/shard_map/ppermute | solution.py:21
  61.5 0.1 finish.1
  61.7 0.7 %collective-permute-start.12 = (bf16[8,16,128]{2,1,0:T(8,128)(2,1)S(1)}, bf16[8,16,128]{2,1,0:T(8,128)(2,1)S(1)}, u32[]{:S(2)}, u32[]{:S(2)}) collective-permute-start(bf16[8,16,128]{2,1,0:T(8,128)(2,1)S(1)} %finish.1), channel_id=1, source_target_pairs={{0,128},{128,0},{1,129},{129,1},{2,130},{130,2},{3,131},{131,3},{4... | collective-permute-start | bytes 98312 | tf_op jit(solution)/shard_map/ppermute | solution.py:21
  62.3 0.9 %collective-permute-done.12 = bf16[8,16,128]{2,1,0:T(8,128)(2,1)S(1)} collective-permute-done((bf16[8,16,128]{2,1,0:T(8,128)(2,1)S(1)}, bf16[8,16,128]{2,1,0:T(8,128)(2,1)S(1)}, u32[]{:S(2)}, u32[]{:S(2)}) %collective-permute-start.12) | collective-permute-done | bytes 32800 | tf_op jit(solution)/shard_map/ppermute | solution.py:21
  63.2 0.6 pad_maximum_fusion
  (1 shorter events, 0.0 us)
Async XLA Ops:
  0.0 0.8 %copy-start = (bf16[16,16,128]{2,1,0:T(8,128)(2,1)S(1)}, bf16[16,16,128]{2,1,0:T(8,128)(2,1)}, u32[]{:S(2)}) copy-start(bf16[16,16,128]{2,1,0:T(8,128)(2,1)} %q_ref.1) | copy-start | bytes 196612
  0.9 14.6 %collective-permute-start.2 = (bf16[128,128]{1,0:T(8,128)(2,1)S(1)}, bf16[128,128]{1,0:T(8,128)(2,1)S(1)}, u32[]{:S(2)}, u32[]{:S(2)}) collective-permute-start(bf16[128,128]{1,0:T(8,128)(2,1)S(1)} %own_tails.1.refs_0_), channel_id=1, source_target_pairs={{0,208},{16,224},{32,240},{48,0},{64,16},{80,32},{96,48},{112,64},... | collective-permute-start | bytes 98312 | tf_op jit(solution)/shard_map/ppermute | solution.py:21
  7.2 8.4 %collective-permute-start.1 = (bf16[128,128]{1,0:T(8,128)(2,1)S(1)}, bf16[128,128]{1,0:T(8,128)(2,1)S(1)}, u32[]{:S(2)}, u32[]{:S(2)}) collective-permute-start(bf16[128,128]{1,0:T(8,128)(2,1)S(1)} %own_tails.1.refs_0_), channel_id=1, source_target_pairs={{0,224},{16,240},{32,0},{48,16},{64,32},{80,48},{96,64},{112,80},{... | collective-permute-start | bytes 98312 | tf_op jit(solution)/shard_map/ppermute | solution.py:21
  8.6 7.0 %collective-permute-start = (bf16[128,128]{1,0:T(8,128)(2,1)S(1)}, bf16[128,128]{1,0:T(8,128)(2,1)S(1)}, u32[]{:S(2)}, u32[]{:S(2)}) collective-permute-start(bf16[128,128]{1,0:T(8,128)(2,1)S(1)} %own_tails.1.refs_0_), channel_id=1, source_target_pairs={{0,240},{16,0},{32,16},{48,32},{64,48},{80,64},{96,80},{112,96},{1... | collective-permute-start | bytes 98312 | tf_op jit(solution)/shard_map/ppermute | solution.py:21
  8.6 0.7 %copy-start.2 = (s32[32]{0:T(128)S(1)}, s32[32]{0:T(128)}, u32[]{:S(2)}) copy-start(s32[32]{0:T(128)} %param.7) | copy-start | bytes 388
  13.2 1.5 %copy-start.1 = (bf16[2048,2,128]{2,1,0:T(2,128)(2,1)S(1)}, bf16[2048,2,128]{2,1,0:T(2,128)(2,1)}, u32[]{:S(2)}) copy-start(bf16[2048,2,128]{2,1,0:T(2,128)(2,1)} %param.6) | copy-start | bytes 3145732
  15.7 7.3 %collective-permute-start.3 = (bf16[2,128,256]{2,1,0:T(8,128)(2,1)S(1)}, bf16[2,128,256]{2,1,0:T(8,128)(2,1)S(1)}, u32[]{:S(2)}, u32[]{:S(2)}) collective-permute-start(bf16[2,128,256]{2,1,0:T(8,128)(2,1)S(1)} %stack_tails.1.q_ref), channel_id=1, source_target_pairs={{0,252},{4,0},{8,4},{12,8},{16,12},{20,16},{24,20},{28,24},{32,28}... | collective-permute-start | bytes 393224 | tf_op jit(solution)/shard_map/ppermute | solution.py:21
  16.1 10.1 %collective-permute-start.7 = (bf16[2,128,256]{2,1,0:T(8,128)(2,1)S(1)}, bf16[2,128,256]{2,1,0:T(8,128)(2,1)S(1)}, u32[]{:S(2)}, u32[]{:S(2)}) collective-permute-start(bf16[2,128,256]{2,1,0:T(8,128)(2,1)S(1)} %stack_tails.1.q_ref), channel_id=1, source_target_pairs={{0,244},{4,248},{8,252},{12,0},{16,4},{20,8},{24,12},{28,16},{32,2... | collective-permute-start | bytes 393224 | tf_op jit(solution)/shard_map/ppermute | solution.py:21
  17.3 12.7 %collective-permute-start.5 = (bf16[2,128,256]{2,1,0:T(8,128)(2,1)S(1)}, bf16[2,128,256]{2,1,0:T(8,128)(2,1)S(1)}, u32[]{:S(2)}, u32[]{:S(2)}) collective-permute-start(bf16[2,128,256]{2,1,0:T(8,128)(2,1)S(1)} %stack_tails.1.q_ref), channel_id=1, source_target_pairs={{0,248},{4,252},{8,0},{12,4},{16,8},{20,12},{24,16},{28,20},{32,24... | collective-permute-start | bytes 393224 | tf_op jit(solution)/shard_map/ppermute | solution.py:21
  25.4 9.7 %collective-permute-start.4 = (f32[4,136,128]{2,1,0:T(8,128)S(1)}, f32[4,136,128]{2,1,0:T(8,128)S(1)}, u32[]{:S(2)}, u32[]{:S(2)}) collective-permute-start(f32[4,136,128]{2,1,0:T(8,128)S(1)} %attend_1.1), channel_id=1, source_target_pairs={{0,4},{4,8},{8,12},{12,16},{16,20},{20,24},{24,28},{28,32},{32,36}... | collective-permute-start | bytes 835592 | tf_op jit(solution)/shard_map/ppermute | solution.py:21
  28.5 9.3 %collective-permute-start.8 = (f32[4,136,128]{2,1,0:T(8,128)S(1)}, f32[4,136,128]{2,1,0:T(8,128)S(1)}, u32[]{:S(2)}, u32[]{:S(2)}) collective-permute-start(f32[4,136,128]{2,1,0:T(8,128)S(1)} %attend_3.1), channel_id=1, source_target_pairs={{0,12},{4,16},{8,20},{12,24},{16,28},{20,32},{24,36},{28,40},{32,4... | collective-permute-start | bytes 835592 | tf_op jit(solution)/shard_map/ppermute | solution.py:21
  32.4 14.9 %collective-permute-start.6 = (f32[4,136,128]{2,1,0:T(8,128)S(1)}, f32[4,136,128]{2,1,0:T(8,128)S(1)}, u32[]{:S(2)}, u32[]{:S(2)}) collective-permute-start(f32[4,136,128]{2,1,0:T(8,128)S(1)} %attend_2.1), channel_id=1, source_target_pairs={{0,8},{4,12},{8,16},{12,20},{16,24},{20,28},{24,32},{28,36},{32,40... | collective-permute-start | bytes 835592 | tf_op jit(solution)/shard_map/ppermute | solution.py:21
  47.4 3.4 %collective-permute-start.9 = (f32[136,128]{1,0:T(8,128)S(1)}, f32[136,128]{1,0:T(8,128)S(1)}, u32[]{:S(2)}, u32[]{:S(2)}) collective-permute-start(f32[136,128]{1,0:T(8,128)S(1)} %get-tuple-element.26), channel_id=1, source_target_pairs={{0,16},{16,32},{32,48},{48,64},{64,80},{80,96},{96,112},{112,128},... | collective-permute-start | bytes 208904 | tf_op jit(solution)/shard_map/ppermute | solution.py:21
  47.5 6.5 %collective-permute-start.10 = (f32[136,128]{1,0:T(8,128)S(1)}, f32[136,128]{1,0:T(8,128)S(1)}, u32[]{:S(2)}, u32[]{:S(2)}) collective-permute-start(f32[136,128]{1,0:T(8,128)S(1)} %get-tuple-element.27), channel_id=1, source_target_pairs={{0,32},{16,48},{32,64},{48,80},{64,96},{80,112},{96,128},{112,144}... | collective-permute-start | bytes 208904 | tf_op jit(solution)/shard_map/ppermute | solution.py:21
  48.4 13.1 %collective-permute-start.11 = (f32[136,128]{1,0:T(8,128)S(1)}, f32[136,128]{1,0:T(8,128)S(1)}, u32[]{:S(2)}, u32[]{:S(2)}) collective-permute-start(f32[136,128]{1,0:T(8,128)S(1)} %get-tuple-element.28), channel_id=1, source_target_pairs={{0,48},{16,64},{32,80},{48,96},{64,112},{80,128},{96,144},{112,160... | collective-permute-start | bytes 208904 | tf_op jit(solution)/shard_map/ppermute | solution.py:21
  61.7 1.5 %collective-permute-start.12 = (bf16[8,16,128]{2,1,0:T(8,128)(2,1)S(1)}, bf16[8,16,128]{2,1,0:T(8,128)(2,1)S(1)}, u32[]{:S(2)}, u32[]{:S(2)}) collective-permute-start(bf16[8,16,128]{2,1,0:T(8,128)(2,1)S(1)} %finish.1), channel_id=1, source_target_pairs={{0,128},{128,0},{1,129},{129,1},{2,130},{130,2},{3,131},{131,3},{4... | collective-permute-start | bytes 98312 | tf_op jit(solution)/shard_map/ppermute | solution.py:21

commit v3 on v2

--- a/solution.py
+++ b/solution.py
@@ -11,7 +11,9 @@
 BLOCK = 128
 NEGATIVE = -1e30
 TAIL = 8
+NOTHING = -32768.0
 EXTRA = 8
+CODED = 16
 COLUMNS = 4
 REACH = 4
 
@@ -42,21 +44,64 @@
         )
 
 
-def attend_kernel(own, factor, live_ref, q_ref, k_ref, v_ref, out_ref, s_ref):
+def place_of(blocks, segment_ref, lengths_ref):
+    segment = segment_ref[0]
+    last = segment * blocks + (blocks - 1)
+    edge, start, end = jnp.int32(0), jnp.int32(0), jnp.int32(1 << 24)
+    for k in range(lengths_ref.shape[0]):
+        edge = edge + lengths_ref[k]
+        start = jnp.where(edge <= last, edge, start)
+        end = jnp.where(edge > last, jnp.minimum(end, edge), end)
+    return lax.div(end, jnp.int32(blocks)) - segment, start - segment * blocks
+
+
+def write_exact(ref, o, m, l):
+    dim = o.shape[0]
+    row = lax.broadcasted_iota(jnp.int32, (EXTRA, o.shape[1]), 0)
+    ref[:dim] = o
+    ref[dim:] = jnp.where(row == 0, m, jnp.where(row == 1, l, 0.0))
+
+
+def read_exact(ref, dim):
+    return ref[:dim], ref[dim : dim + 1], ref[dim + 1 : dim + 2]
+
+
+def write_coded(ref, o, m, l):
+    dim = o.shape[0]
+    most = jnp.maximum(jnp.max(jnp.abs(o), axis=0, keepdims=True), 1e-30)
+    power = jnp.floor(jnp.log2(most) + 1e-3) + 1.0
+    code = jnp.clip(jnp.floor(o * jnp.exp2(15.0 - power) + 0.5), -32767.0, 32767.0)
+    high = jnp.floor(l * 2.0)
+    low = jnp.floor((l * 2.0 - high) * 32768.0)
+    row = lax.broadcasted_iota(jnp.int32, (CODED, o.shape[1]), 0)
+    tail = jnp.where(row == 0, m, jnp.where(row == 1, high, jnp.where(row == 2, low, power)))
+    ref[:dim] = code.astype(jnp.int32).astype(jnp.int16)
+    ref[dim:] = tail.astype(jnp.int32).astype(jnp.int16)
+
+
+def read_coded(ref, dim):
+    tail = ref[dim:].astype(jnp.int32).astype(jnp.float32)
+    m, high, low, power = (tail[k : k + 1] for k in range(4))
+    o = ref[:dim].astype(jnp.int32).astype(jnp.float32) * jnp.exp2(power - 15.0)
+    return o, m, (high + low * (1.0 / 32768.0)) * 0.5
+
+
+def attend_kernel(own, factor, segment_ref, lengths_ref, q_ref, k_ref, v_ref, out_ref, s_ref):
     kv_count, key_rows, dim = k_ref.shape
     width = q_ref.shape[2]
     blocks = out_ref.shape[0]
     wide = width // blocks
     sharing = wide // TAIL
-    n_live = live_ref[0]
-    first = live_ref[1]
+    lanes = kv_count * wide
     count = key_rows // BLOCK
+    n_live, first = place_of(count, segment_ref, lengths_ref)
+    write = write_exact if own == 0 else write_coded
 
     @pl.when(own >= n_live)
     def _():
-        out_ref[:, :dim, :] = jnp.zeros((blocks, dim, kv_count * wide), jnp.float32)
-        row = lax.broadcasted_iota(jnp.int32, (blocks, EXTRA, kv_count * wide), 1)
-        out_ref[:, dim:, :] = jnp.where(row == 0, NEGATIVE, 0.0)
+        none = jnp.zeros((1, lanes), jnp.float32)
+        for j in range(blocks):
+            write(out_ref.at[j], jnp.zeros((dim, lanes), jnp.float32), none + NOTHING, none)
 
     @pl.when(own < n_live)
     def _():
@@ -91,47 +136,43 @@
             outputs.append(
                 jnp.dot(v_ref[h], jnp.concatenate(parts, axis=0), preferred_element_type=jnp.float32)
             )
-        row = lax.broadcasted_iota(jnp.int32, (EXTRA, kv_count * wide), 0)
         for j in range(blocks):
-            lanes = slice(j * wide, (j + 1) * wide)
+            here = slice(j * wide, (j + 1) * wide)
             keep = own + blocks * j < n_live
-            o = jnp.concatenate([a[:, lanes] for a in outputs], axis=1)
-            m = jnp.concatenate([a[:, lanes] for a in tops], axis=1)
-            l = jnp.concatenate([a[:, lanes] for a in totals], axis=1)
-            out_ref[j, :dim, :] = jnp.where(keep, o, 0.0)
-            out_ref[j, dim:, :] = jnp.where(
-                row == 0,
-                jnp.where(keep, m, NEGATIVE),
-                jnp.where((row == 1) & keep, l, 0.0),
+            o = jnp.concatenate([a[:, here] for a in outputs], axis=1)
+            m = jnp.concatenate([a[:, here] for a in tops], axis=1) * factor
+            l = jnp.concatenate([a[:, here] for a in totals], axis=1)
+            whole = jnp.ceil(m)
+            f = jnp.where(keep, jnp.exp2(m - whole), 0.0)
+            write(
+                out_ref.at[j], jnp.where(keep, o * f, 0.0), jnp.where(keep, whole, NOTHING), l * f
             )
 
 
-def merge(parts, factor):
+def merge(parts):
     top = functools.reduce(jnp.maximum, [m for _, m, _ in parts])
     o = l = None
     for po, pm, pt in parts:
-        f = jnp.exp2((pm - top) * factor)
+        f = jnp.exp2(pm - top)
         o = po * f if o is None else o + po * f
         l = pt * f if l is None else l + pt * f
     return o, top, l
 
 
-def column_kernel(factor, *refs):
+def column_kernel(*refs):
     parts, outs = refs[:COLUMNS], refs[COLUMNS:]
     dim = outs[0].shape[0] - EXTRA
     for j, out in enumerate(outs):
-        found = [(p[j, :dim], p[j, dim : dim + 1], p[j, dim + 1 : dim + 2]) for p in parts]
-        o, m, l = merge(found, factor)
-        row = lax.broadcasted_iota(jnp.int32, (EXTRA, m.shape[1]), 0)
-        out[:dim] = o
-        out[dim:] = jnp.where(row == 0, m, jnp.where(row == 1, l, 0.0))
-
-
-def finish_kernel(factor, kv_count, *refs):
+        found = [read_exact(parts[0].at[j], dim)] + [read_coded(p.at[j], dim) for p in parts[1:]]
+        write = write_exact if j == 0 else write_coded
+        write(out, *merge(found))
+
+
+def finish_kernel(kv_count, *refs):
     parts, out_ref = refs[:-1], refs[-1]
     dim = out_ref.shape[2]
-    found = [(p[:dim], p[dim : dim + 1], p[dim + 1 : dim + 2]) for p in parts]
-    o, _, l = merge(found, factor)
+    found = [read_exact(parts[0], dim)] + [read_coded(p, dim) for p in parts[1:]]
+    o, _, l = merge(found)
     res = jnp.transpose(o / l).reshape(kv_count, TAIL, -1, dim)
     out_ref[...] = jnp.concatenate([res[h] for h in range(kv_count)], axis=1).astype(out_ref.dtype)
 
@@ -149,7 +190,7 @@
 
 
 def body(queries, keys, values, doc_lengths):
-    rows, columns, groups = lax.axis_size("z"), lax.axis_size("x"), lax.axis_size("outer")
+    rows, columns = lax.axis_size("z"), lax.axis_size("x")
     o, z, x = lax.axis_index("outer"), lax.axis_index("z"), lax.axis_index("x")
     key_rows, kv_count, dim = keys.shape
     heads = queries.shape[1]
@@ -168,17 +209,10 @@
     )(o.reshape(1).astype(jnp.int32), queries)
     held = [own] + [shifted(own, ("outer", "z"), -j) for j in range(1, REACH)]
 
-    segment = (o * rows + z) * columns + x
-    blocks = key_rows // BLOCK
-    ends = jnp.cumsum(doc_lengths)
-    last = segment * blocks + blocks - 1
-    start = jnp.max(jnp.where(ends <= last, ends, 0))
-    end = jnp.min(jnp.where(ends > last, ends, rows * columns * groups * blocks))
-    live = jnp.stack([end // blocks - segment, jnp.maximum(start - segment * blocks, 0)])
-    live = live.astype(jnp.int32)
+    segment = ((o * rows + z) * columns + x).reshape(1).astype(jnp.int32)
     k_heads = jnp.transpose(keys, (1, 0, 2))
+    held, k_heads, values = lax.optimization_barrier((held, k_heads, values))
     v_heads = jnp.transpose(values, (1, 2, 0))
-    held, live, k_heads, v_heads = lax.optimization_barrier((held, live, k_heads, v_heads))
 
     stack = pl.pallas_call(
         stack_kernel,
@@ -191,6 +225,8 @@
     everywhere = ("outer", "z", "x")
     asked = [stack] + [shifted(stack, everywhere, -u) for u in range(1, columns)]
 
+    exact = jax.ShapeDtypeStruct((REACH, dim + EXTRA, lanes), jnp.float32)
+    coded = jax.ShapeDtypeStruct((REACH, dim + CODED, lanes), jnp.int16)
     partial = []
     for u in range(columns):
         block = asked[u]
@@ -199,8 +235,8 @@
         partial.append(
             pl.pallas_call(
                 functools.partial(attend_kernel, u, factor),
-                out_shape=jax.ShapeDtypeStruct((REACH, dim + EXTRA, lanes), jnp.float32),
-                in_specs=scalars() + on_chip(3),
+                out_shape=exact if u == 0 else coded,
+                in_specs=scalars() * 2 + on_chip(3),
                 out_specs=on_chip(1)[0],
                 scratch_shapes=[pltpu.VMEM((kv_count, key_rows, width), jnp.float32)],
                 cost_estimate=pl.CostEstimate(
@@ -210,12 +246,13 @@
                 ),
                 compiler_params=room(16),
                 name=f"attend_{u}",
-            )(live, block, k_heads, v_heads)
+            )(segment, doc_lengths, block, k_heads, v_heads)
         )
     arrived = [partial[0]] + [shifted(partial[u], everywhere, u) for u in range(1, columns)]
     column = pl.pallas_call(
-        functools.partial(column_kernel, factor),
-        out_shape=[jax.ShapeDtypeStruct((dim + EXTRA, lanes), jnp.float32)] * REACH,
+        column_kernel,
+        out_shape=[jax.ShapeDtypeStruct((dim + EXTRA, lanes), jnp.float32)]
+        + [jax.ShapeDtypeStruct((dim + CODED, lanes), jnp.int16)] * (REACH - 1),
         in_specs=on_chip(columns),
         out_specs=on_chip(REACH),
         compiler_params=room(4),
@@ -223,7 +260,7 @@
     )(*arrived)
     arrived = [column[0]] + [shifted(column[j], ("outer", "z"), j) for j in range(1, REACH)]
     mine = pl.pallas_call(
-        functools.partial(finish_kernel, factor, kv_count),
+        functools.partial(finish_kernel, kv_count),
         out_shape=jax.ShapeDtypeStruct((TAIL, heads, dim), queries.dtype),
         in_specs=on_chip(REACH),
         out_specs=on_chip(1)[0],

time: 64.2 us -> 55.5 us (0.86)
  the two profiles are of different devices: /device:TPU:51 before, /device:TPU:1 now
where the time goes in v3:
time: 55.5 us; the launch traced here: 55.6 us
  starting transfers between devices  21.4 us (39%)
  waiting for transfers between devices  18 us (32%)
  Pallas kernels  10.2 us (18%)
  local copies, waits for them, and re-layouts  5.29 us (10%)
  other arithmetic  0.65 us (1%)
    ppermute x13, starting transfers between devices, shifted(): return lax.ppermute(part, axes, [(i, (i + by) % size) for i in range(size)])  21.4 us
    ppermute x13, waiting for transfers between devices, shifted(): return lax.ppermute(part, axes, [(i, (i + by) % size) for i in range(size)])  18 us
    pallas_call x4, Pallas kernels, body(): pl.pallas_call(functools.partial(attend_kernel, u, factor), out_shape=exa...  9.64 us
    unnamed x5, local copies, waits for them, and re-layouts  2.85 us
    optimization_barrier x1, local copies, waits for them, and re-layouts, body(): held, k_heads, values = lax.optimization_barrier((held, k_heads, values))  2.44 us
  transfers between devices with their start and end apart: 13, of which 9 were waited for; matrix products, arithmetic and copies ran while one was open for 7% of the time, Pallas kernels for 17%

profile of v3, /device:TPU:1, one launch (start us, length us, event | category | flops | bytes accessed | tf_op | source)
XLA Modules:
  0.0 55.6 jit_solution(14752224329782145244)
XLA Ops:
  0.0 0.0 copy-start
  0.0 0.8 %copy-done = bf16[16,16,128]{2,1,0:T(8,128)(2,1)S(1)} copy-done((bf16[16,16,128]{2,1,0:T(8,128)(2,1)S(1)}, bf16[16,16,128]{2,1,0:T(8,128)(2,1)}, u32[]{:S(2)}) %copy-start) | copy-done | bytes 65560
  0.8 0.1 own_tails.1.refs_0_
  0.9 7.9 %collective-permute-start.2 = (bf16[128,128]{1,0:T(8,128)(2,1)S(1)}, bf16[128,128]{1,0:T(8,128)(2,1)S(1)}, u32[]{:S(2)}, u32[]{:S(2)}) collective-permute-start(bf16[128,128]{1,0:T(8,128)(2,1)S(1)} %own_tails.1.refs_0_), channel_id=1, source_target_pairs={{0,208},{16,224},{32,240},{48,0},{64,16},{80,32},{96,48},{112,64},... | collective-permute-start | bytes 98312 | tf_op jit(solution)/shard_map/ppermute | solution.py:23
  8.9 0.5 collective-permute-start.1
  9.4 0.5 collective-permute-start
  9.9 1.4 %copy.8 = bf16[2048,2,128]{2,0,1:T(8,128)(2,1)S(1)} copy(bf16[2048,2,128]{2,1,0:T(2,128)(2,1)} %param.5) | data formatting | bytes 2097152 | tf_op args[1]
  11.2 0.0 collective-permute-done.2.refs_3_
  11.3 1.6 %collective-permute-done.1.refs_2_ = bf16[128,128]{1,0:T(8,128)(2,1)S(1)} collective-permute-done((bf16[128,128]{1,0:T(8,128)(2,1)S(1)}, bf16[128,128]{1,0:T(8,128)(2,1)S(1)}, u32[]{:S(2)}, u32[]{:S(2)}) %collective-permute-start.1) | collective-permute-done | bytes 32800 | tf_op jit(solution)/shard_map/ppermute | solution.py:23
  12.9 1.5 %collective-permute-done.refs_1_ = bf16[128,128]{1,0:T(8,128)(2,1)S(1)} collective-permute-done((bf16[128,128]{1,0:T(8,128)(2,1)S(1)}, bf16[128,128]{1,0:T(8,128)(2,1)S(1)}, u32[]{:S(2)}, u32[]{:S(2)}) %collective-permute-start) | collective-permute-done | bytes 32800 | tf_op jit(solution)/shard_map/ppermute | solution.py:23
  14.4 0.1 stack_tails.1.q_ref
  14.5 5.2 %collective-permute-start.3 = (bf16[2,128,256]{2,1,0:T(8,128)(2,1)S(1)}, bf16[2,128,256]{2,1,0:T(8,128)(2,1)S(1)}, u32[]{:S(2)}, u32[]{:S(2)}) collective-permute-start(bf16[2,128,256]{2,1,0:T(8,128)(2,1)S(1)} %stack_tails.1.q_ref), channel_id=1, source_target_pairs={{0,252},{4,0},{8,4},{12,8},{16,12},{20,16},{24,20},{28,24},{32,28}... | collective-permute-start | bytes 393224 | tf_op jit(solution)/shard_map/ppermute | solution.py:23
  19.7 0.8 %collective-permute-start.5 = (bf16[2,128,256]{2,1,0:T(8,128)(2,1)S(1)}, bf16[2,128,256]{2,1,0:T(8,128)(2,1)S(1)}, u32[]{:S(2)}, u32[]{:S(2)}) collective-permute-start(bf16[2,128,256]{2,1,0:T(8,128)(2,1)S(1)} %stack_tails.1.q_ref), channel_id=1, source_target_pairs={{0,248},{4,252},{8,0},{12,4},{16,8},{20,12},{24,16},{28,20},{32,24... | collective-permute-start | bytes 393224 | tf_op jit(solution)/shard_map/ppermute | solution.py:23
  20.5 1.1 %collective-permute-start.7 = (bf16[2,128,256]{2,1,0:T(8,128)(2,1)S(1)}, bf16[2,128,256]{2,1,0:T(8,128)(2,1)S(1)}, u32[]{:S(2)}, u32[]{:S(2)}) collective-permute-start(bf16[2,128,256]{2,1,0:T(8,128)(2,1)S(1)} %stack_tails.1.q_ref), channel_id=1, source_target_pairs={{0,244},{4,248},{8,252},{12,0},{16,4},{20,8},{24,12},{28,16},{32,2... | collective-permute-start | bytes 393224 | tf_op jit(solution)/shard_map/ppermute | solution.py:23
  21.5 2.4 %copy.6 = bf16[2048,2,128]{0,2,1:T(8,128)(2,1)S(1)} copy(bf16[2048,2,128]{2,1,0:T(2,128)(2,1)} %param.6) | data formatting | bytes 2097152 | tf_op jit(solution)/shard_map/optimization_barrier | solution.py:214
  24.0 0.0 copy-start.1
  24.0 0.6 %copy-done.1 = s32[32]{0:T(128)S(1)} copy-done((s32[32]{0:T(128)S(1)}, s32[32]{0:T(128)}, u32[]{:S(2)}) %copy-start.1) | copy-done | bytes 152
  24.6 2.4 %attend_0.1.refs_0_ = f32[4,136,128]{2,1,0:T(8,128)S(1)} custom-call(s32[1]{0:T(128)} %bitcast.segment_ref, s32[32]{0:T(128)S(1)} %copy-done.1, bf16[2,128,256]{2,1,0:T(8,128)(2,1)S(1)} %stack_tails.1.q_ref, bf16[2,2048,128]{2,1,0:T(8,128)(2,1)S(1)} %bitcast.6, bf16[2,128,2048]{2,1,0:T(8,128)(2,1)S(1)} %bitcast.10), custom_call_target="tpu_custom_call" | custom-call | flops 536870912 | bytes 2097152 | tf_op jit(solution)/shard_map/attend_0/pallas_call | solution.py:236
  27.1 0.0 collective-permute-done.3.q_ref
  27.1 2.3 %attend_1.1 = s16[4,144,128]{2,1,0:T(8,128)(2,1)S(1)} custom-call(s32[1]{0:T(128)} %bitcast.segment_ref, s32[32]{0:T(128)S(1)} %copy-done.1, bf16[2,128,256]{2,1,0:T(8,128)(2,1)S(1)} %collective-permute-done.3.q_ref, bf16[2,2048,128]{2,1,0:T(8,128)(2,1)S(1)} %bitcast.7, bf16[2,128,2048]{2,1,0:T(8,128)(2,1)S(1)} %bitcast.11), custom_call_target="tpu_custom_call" | custom-call | flops 536870912 | bytes 2097152 | tf_op jit(solution)/shard_map/attend_1/pallas_call | solution.py:236
  29.5 1.6 %collective-permute-start.4 = (s16[4,144,128]{2,1,0:T(8,128)(2,1)S(1)}, s16[4,144,128]{2,1,0:T(8,128)(2,1)S(1)}, u32[]{:S(2)}, u32[]{:S(2)}) collective-permute-start(s16[4,144,128]{2,1,0:T(8,128)(2,1)S(1)} %attend_1.1), channel_id=1, source_target_pairs={{0,4},{4,8},{8,12},{12,16},{16,20},{20,24},{24,28},{28,32},{32,36}... | collective-permute-start | bytes 442376 | tf_op jit(solution)/shard_map/ppermute | solution.py:23
  31.1 0.0 collective-permute-done.5.q_ref
  31.1 2.3 %attend_2.1 = s16[4,144,128]{2,1,0:T(8,128)(2,1)S(1)} custom-call(s32[1]{0:T(128)} %bitcast.segment_ref, s32[32]{0:T(128)S(1)} %copy-done.1, bf16[2,128,256]{2,1,0:T(8,128)(2,1)S(1)} %collective-permute-done.5.q_ref, bf16[2,2048,128]{2,1,0:T(8,128)(2,1)S(1)} %bitcast.8, bf16[2,128,2048]{2,1,0:T(8,128)(2,1)S(1)} %bitcast.12), custom_call_target="tpu_custom_call" | custom-call | flops 536870912 | bytes 2097152 | tf_op jit(solution)/shard_map/attend_2/pallas_call | solution.py:236
  33.4 1.3 %collective-permute-start.6 = (s16[4,144,128]{2,1,0:T(8,128)(2,1)S(1)}, s16[4,144,128]{2,1,0:T(8,128)(2,1)S(1)}, u32[]{:S(2)}, u32[]{:S(2)}) collective-permute-start(s16[4,144,128]{2,1,0:T(8,128)(2,1)S(1)} %attend_2.1), channel_id=1, source_target_pairs={{0,8},{4,12},{8,16},{12,20},{16,24},{20,28},{24,32},{28,36},{32,40... | collective-permute-start | bytes 442376 | tf_op jit(solution)/shard_map/ppermute | solution.py:23
  34.7 0.0 collective-permute-done.7.q_ref
  34.7 2.5 %attend_3.1 = s16[4,144,128]{2,1,0:T(8,128)(2,1)S(1)} custom-call(s32[1]{0:T(128)} %bitcast.segment_ref, s32[32]{0:T(128)S(1)} %copy-done.1, bf16[2,128,256]{2,1,0:T(8,128)(2,1)S(1)} %collective-permute-done.7.q_ref, bf16[2,2048,128]{2,1,0:T(8,128)(2,1)S(1)} %bitcast.9, bf16[2,128,2048]{2,1,0:T(8,128)(2,1)S(1)} %bitcast.13), custom_call_target="tpu_custom_call" | custom-call | flops 536870912 | bytes 2097152 | tf_op jit(solution)/shard_map/attend_3/pallas_call | solution.py:236
  37.3 1.4 %collective-permute-start.8 = (s16[4,144,128]{2,1,0:T(8,128)(2,1)S(1)}, s16[4,144,128]{2,1,0:T(8,128)(2,1)S(1)}, u32[]{:S(2)}, u32[]{:S(2)}) collective-permute-start(s16[4,144,128]{2,1,0:T(8,128)(2,1)S(1)} %attend_3.1), channel_id=1, source_target_pairs={{0,12},{4,16},{8,20},{12,24},{16,28},{20,32},{24,36},{28,40},{32,4... | collective-permute-start | bytes 442376 | tf_op jit(solution)/shard_map/ppermute | solution.py:23
  38.7 0.8 %collective-permute-done.4.refs_1_ = s16[4,144,128]{2,1,0:T(8,128)(2,1)S(1)} collective-permute-done((s16[4,144,128]{2,1,0:T(8,128)(2,1)S(1)}, s16[4,144,128]{2,1,0:T(8,128)(2,1)S(1)}, u32[]{:S(2)}, u32[]{:S(2)}) %collective-permute-start.4) | collective-permute-done | bytes 147488 | tf_op jit(solution)/shard_map/ppermute | solution.py:23
  39.5 2.2 %collective-permute-done.6.refs_2_ = s16[4,144,128]{2,1,0:T(8,128)(2,1)S(1)} collective-permute-done((s16[4,144,128]{2,1,0:T(8,128)(2,1)S(1)}, s16[4,144,128]{2,1,0:T(8,128)(2,1)S(1)}, u32[]{:S(2)}, u32[]{:S(2)}) %collective-permute-start.6) | collective-permute-done | bytes 147488 | tf_op jit(solution)/shard_map/ppermute | solution.py:23
  41.7 2.4 %collective-permute-done.8.refs_3_ = s16[4,144,128]{2,1,0:T(8,128)(2,1)S(1)} collective-permute-done((s16[4,144,128]{2,1,0:T(8,128)(2,1)S(1)}, s16[4,144,128]{2,1,0:T(8,128)(2,1)S(1)}, u32[]{:S(2)}, u32[]{:S(2)}) %collective-permute-start.8) | collective-permute-done | bytes 147488 | tf_op jit(solution)/shard_map/ppermute | solution.py:23
  44.0 0.2 merge_columns.1
  44.3 0.1 collective-permute-start.9
  44.4 0.1 collective-permute-start.10
  44.5 0.1 collective-permute-start.11
  44.6 4.4 %collective-permute-done.9.refs_1_ = s16[144,128]{1,0:T(8,128)(2,1)S(1)} collective-permute-done((s16[144,128]{1,0:T(8,128)(2,1)S(1)}, s16[144,128]{1,0:T(8,128)(2,1)S(1)}, u32[]{:S(2)}, u32[]{:S(2)}) %collective-permute-start.9) | collective-permute-done | bytes 36896 | tf_op jit(solution)/shard_map/ppermute | solution.py:23
  49.0 1.0 %collective-permute-done.10.refs_2_ = s16[144,128]{1,0:T(8,128)(2,1)S(1)} collective-permute-done((s16[144,128]{1,0:T(8,128)(2,1)S(1)}, s16[144,128]{1,0:T(8,128)(2,1)S(1)}, u32[]{:S(2)}, u32[]{:S(2)}) %collective-permute-start.10) | collective-permute-done | bytes 36896 | tf_op jit(solution)/shard_map/ppermute | solution.py:23
  50.0 3.3 %collective-permute-done.11.refs_3_ = s16[144,128]{1,0:T(8,128)(2,1)S(1)} collective-permute-done((s16[144,128]{1,0:T(8,128)(2,1)S(1)}, s16[144,128]{1,0:T(8,128)(2,1)S(1)}, u32[]{:S(2)}, u32[]{:S(2)}) %collective-permute-start.11) | collective-permute-done | bytes 36896 | tf_op jit(solution)/shard_map/ppermute | solution.py:23
  53.2 0.1 finish.1
  53.4 0.7 %collective-permute-start.12 = (bf16[8,16,128]{2,1,0:T(8,128)(2,1)S(1)}, bf16[8,16,128]{2,1,0:T(8,128)(2,1)S(1)}, u32[]{:S(2)}, u32[]{:S(2)}) collective-permute-start(bf16[8,16,128]{2,1,0:T(8,128)(2,1)S(1)} %finish.1), channel_id=1, source_target_pairs={{0,128},{128,0},{1,129},{129,1},{2,130},{130,2},{3,131},{131,3},{4... | collective-permute-start | bytes 98312 | tf_op jit(solution)/shard_map/ppermute | solution.py:23
  54.1 0.9 %collective-permute-done.12 = bf16[8,16,128]{2,1,0:T(8,128)(2,1)S(1)} collective-permute-done((bf16[8,16,128]{2,1,0:T(8,128)(2,1)S(1)}, bf16[8,16,128]{2,1,0:T(8,128)(2,1)S(1)}, u32[]{:S(2)}, u32[]{:S(2)}) %collective-permute-start.12) | collective-permute-done | bytes 32800 | tf_op jit(solution)/shard_map/ppermute | solution.py:23
  54.9 0.6 %pad_maximum_fusion = bf16[16,16,128]{2,1,0:T(8,128)(2,1)} fusion(bf16[8,16,128]{2,1,0:T(8,128)(2,1)S(1)} %get-tuple-element.28, bf16[8,16,128]{2,1,0:T(8,128)(2,1)S(1)} %get-tuple-element.27), kind=kLoop, calls=%fused_computation.1 | loop fusion | flops 32768 | bytes 131072 | tf_op jit(solution)/shard_map/concatenate | solution.py:273
  (1 shorter events, 0.0 us)
Async XLA Ops:
  0.0 0.8 %copy-start = (bf16[16,16,128]{2,1,0:T(8,128)(2,1)S(1)}, bf16[16,16,128]{2,1,0:T(8,128)(2,1)}, u32[]{:S(2)}) copy-start(bf16[16,16,128]{2,1,0:T(8,128)(2,1)} %q_ref.1) | copy-start | bytes 196612
  0.9 10.3 %collective-permute-start.2 = (bf16[128,128]{1,0:T(8,128)(2,1)S(1)}, bf16[128,128]{1,0:T(8,128)(2,1)S(1)}, u32[]{:S(2)}, u32[]{:S(2)}) collective-permute-start(bf16[128,128]{1,0:T(8,128)(2,1)S(1)} %own_tails.1.refs_0_), channel_id=1, source_target_pairs={{0,208},{16,224},{32,240},{48,0},{64,16},{80,32},{96,48},{112,64},... | collective-permute-start | bytes 98312 | tf_op jit(solution)/shard_map/ppermute | solution.py:23
  8.9 4.0 %collective-permute-start.1 = (bf16[128,128]{1,0:T(8,128)(2,1)S(1)}, bf16[128,128]{1,0:T(8,128)(2,1)S(1)}, u32[]{:S(2)}, u32[]{:S(2)}) collective-permute-start(bf16[128,128]{1,0:T(8,128)(2,1)S(1)} %own_tails.1.refs_0_), channel_id=1, source_target_pairs={{0,224},{16,240},{32,0},{48,16},{64,32},{80,48},{96,64},{112,80},{... | collective-permute-start | bytes 98312 | tf_op jit(solution)/shard_map/ppermute | solution.py:23
  9.4 4.9 %collective-permute-start = (bf16[128,128]{1,0:T(8,128)(2,1)S(1)}, bf16[128,128]{1,0:T(8,128)(2,1)S(1)}, u32[]{:S(2)}, u32[]{:S(2)}) collective-permute-start(bf16[128,128]{1,0:T(8,128)(2,1)S(1)} %own_tails.1.refs_0_), channel_id=1, source_target_pairs={{0,240},{16,0},{32,16},{48,32},{64,48},{80,64},{96,80},{112,96},{1... | collective-permute-start | bytes 98312 | tf_op jit(solution)/shard_map/ppermute | solution.py:23
  14.5 12.6 %collective-permute-start.3 = (bf16[2,128,256]{2,1,0:T(8,128)(2,1)S(1)}, bf16[2,128,256]{2,1,0:T(8,128)(2,1)S(1)}, u32[]{:S(2)}, u32[]{:S(2)}) collective-permute-start(bf16[2,128,256]{2,1,0:T(8,128)(2,1)S(1)} %stack_tails.1.q_ref), channel_id=1, source_target_pairs={{0,252},{4,0},{8,4},{12,8},{16,12},{20,16},{24,20},{28,24},{32,28}... | collective-permute-start | bytes 393224 | tf_op jit(solution)/shard_map/ppermute | solution.py:23
  19.7 11.4 %collective-permute-start.5 = (bf16[2,128,256]{2,1,0:T(8,128)(2,1)S(1)}, bf16[2,128,256]{2,1,0:T(8,128)(2,1)S(1)}, u32[]{:S(2)}, u32[]{:S(2)}) collective-permute-start(bf16[2,128,256]{2,1,0:T(8,128)(2,1)S(1)} %stack_tails.1.q_ref), channel_id=1, source_target_pairs={{0,248},{4,252},{8,0},{12,4},{16,8},{20,12},{24,16},{28,20},{32,24... | collective-permute-start | bytes 393224 | tf_op jit(solution)/shard_map/ppermute | solution.py:23
  20.5 14.3 %collective-permute-start.7 = (bf16[2,128,256]{2,1,0:T(8,128)(2,1)S(1)}, bf16[2,128,256]{2,1,0:T(8,128)(2,1)S(1)}, u32[]{:S(2)}, u32[]{:S(2)}) collective-permute-start(bf16[2,128,256]{2,1,0:T(8,128)(2,1)S(1)} %stack_tails.1.q_ref), channel_id=1, source_target_pairs={{0,244},{4,248},{8,252},{12,0},{16,4},{20,8},{24,12},{28,16},{32,2... | collective-permute-start | bytes 393224 | tf_op jit(solution)/shard_map/ppermute | solution.py:23
  24.0 0.7 %copy-start.1 = (s32[32]{0:T(128)S(1)}, s32[32]{0:T(128)}, u32[]{:S(2)}) copy-start(s32[32]{0:T(128)} %lengths_ref.7) | copy-start | bytes 388
  29.5 10.0 %collective-permute-start.4 = (s16[4,144,128]{2,1,0:T(8,128)(2,1)S(1)}, s16[4,144,128]{2,1,0:T(8,128)(2,1)S(1)}, u32[]{:S(2)}, u32[]{:S(2)}) collective-permute-start(s16[4,144,128]{2,1,0:T(8,128)(2,1)S(1)} %attend_1.1), channel_id=1, source_target_pairs={{0,4},{4,8},{8,12},{12,16},{16,20},{20,24},{24,28},{28,32},{32,36}... | collective-permute-start | bytes 442376 | tf_op jit(solution)/shard_map/ppermute | solution.py:23
  33.4 8.3 %collective-permute-start.6 = (s16[4,144,128]{2,1,0:T(8,128)(2,1)S(1)}, s16[4,144,128]{2,1,0:T(8,128)(2,1)S(1)}, u32[]{:S(2)}, u32[]{:S(2)}) collective-permute-start(s16[4,144,128]{2,1,0:T(8,128)(2,1)S(1)} %attend_2.1), channel_id=1, source_target_pairs={{0,8},{4,12},{8,16},{12,20},{16,24},{20,28},{24,32},{28,36},{32,40... | collective-permute-start | bytes 442376 | tf_op jit(solution)/shard_map/ppermute | solution.py:23
  37.3 6.8 %collective-permute-start.8 = (s16[4,144,128]{2,1,0:T(8,128)(2,1)S(1)}, s16[4,144,128]{2,1,0:T(8,128)(2,1)S(1)}, u32[]{:S(2)}, u32[]{:S(2)}) collective-permute-start(s16[4,144,128]{2,1,0:T(8,128)(2,1)S(1)} %attend_3.1), channel_id=1, source_target_pairs={{0,12},{4,16},{8,20},{12,24},{16,28},{20,32},{24,36},{28,40},{32,4... | collective-permute-start | bytes 442376 | tf_op jit(solution)/shard_map/ppermute | solution.py:23
  44.3 4.7 %collective-permute-start.9 = (s16[144,128]{1,0:T(8,128)(2,1)S(1)}, s16[144,128]{1,0:T(8,128)(2,1)S(1)}, u32[]{:S(2)}, u32[]{:S(2)}) collective-permute-start(s16[144,128]{1,0:T(8,128)(2,1)S(1)} %get-tuple-element.24), channel_id=1, source_target_pairs={{0,16},{16,32},{32,48},{48,64},{64,80},{80,96},{96,112},{112,128},... | collective-permute-start | bytes 110600 | tf_op jit(solution)/shard_map/ppermute | solution.py:23
  44.4 5.6 %collective-permute-start.10 = (s16[144,128]{1,0:T(8,128)(2,1)S(1)}, s16[144,128]{1,0:T(8,128)(2,1)S(1)}, u32[]{:S(2)}, u32[]{:S(2)}) collective-permute-start(s16[144,128]{1,0:T(8,128)(2,1)S(1)} %get-tuple-element.25), channel_id=1, source_target_pairs={{0,32},{16,48},{32,64},{48,80},{64,96},{80,112},{96,128},{112,144}... | collective-permute-start | bytes 110600 | tf_op jit(solution)/shard_map/ppermute | solution.py:23
  44.5 8.8 %collective-permute-start.11 = (s16[144,128]{1,0:T(8,128)(2,1)S(1)}, s16[144,128]{1,0:T(8,128)(2,1)S(1)}, u32[]{:S(2)}, u32[]{:S(2)}) collective-permute-start(s16[144,128]{1,0:T(8,128)(2,1)S(1)} %get-tuple-element.26), channel_id=1, source_target_pairs={{0,48},{16,64},{32,80},{48,96},{64,112},{80,128},{96,144},{112,160... | collective-permute-start | bytes 110600 | tf_op jit(solution)/shard_map/ppermute | solution.py:23
  53.4 1.6 %collective-permute-start.12 = (bf16[8,16,128]{2,1,0:T(8,128)(2,1)S(1)}, bf16[8,16,128]{2,1,0:T(8,128)(2,1)S(1)}, u32[]{:S(2)}, u32[]{:S(2)}) collective-permute-start(bf16[8,16,128]{2,1,0:T(8,128)(2,1)S(1)} %finish.1), channel_id=1, source_target_pairs={{0,128},{128,0},{1,129},{129,1},{2,130},{130,2},{3,131},{131,3},{4... | collective-permute-start | bytes 98312 | tf_op jit(solution)/shard_map/ppermute | solution.py:23

commit v4 on v3

--- a/solution.py
+++ b/solution.py
@@ -9,6 +9,7 @@
 from jax.sharding import Mesh, PartitionSpec as P
 
 BLOCK = 128
+STEP = 512
 NEGATIVE = -1e30
 TAIL = 8
 NOTHING = -32768.0
@@ -21,6 +22,23 @@
 def shifted(part, axes, by):
     size = lax.axis_size(axes)
     return lax.ppermute(part, axes, [(i, (i + by) % size) for i in range(size)])
+
+
+def mask_kernel(blocks, lengths_ref, live_ref):
+    rows, columns = lax.axis_size("z"), lax.axis_size("x")
+    segment = (lax.axis_index("outer") * rows + lax.axis_index("z")) * columns + lax.axis_index("x")
+    count = lengths_ref.shape[1]
+    lengths = jnp.broadcast_to(lengths_ref[...].astype(jnp.float32), (count, count))
+    upto = lax.broadcasted_iota(jnp.int32, (count, count), 0)
+    which = lax.broadcasted_iota(jnp.int32, (count, count), 1)
+    edges = jnp.sum(jnp.where(which <= upto, lengths, 0.0), axis=1, keepdims=True)
+    here = (segment * blocks).astype(jnp.float32)
+    last = here + (blocks - 1.0)
+    start = jnp.max(jnp.where(edges <= last, edges, 0.0), axis=0, keepdims=True)
+    end = jnp.min(jnp.where(edges > last, edges, 1e9), axis=0, keepdims=True)
+    n_live = jnp.floor(end * (1.0 / blocks)) - segment.astype(jnp.float32)
+    row = lax.broadcasted_iota(jnp.int32, live_ref.shape, 0)
+    live_ref[...] = jnp.where(row == 0, n_live, start - here)
 
 
 def own_kernel(kv_count, o_ref, q_ref, out_ref):
@@ -42,17 +60,6 @@
         out_ref[h] = jnp.concatenate(
             [b[:, h * wide : (h + 1) * wide] for b in blocks], axis=1
         )
-
-
-def place_of(blocks, segment_ref, lengths_ref):
-    segment = segment_ref[0]
-    last = segment * blocks + (blocks - 1)
-    edge, start, end = jnp.int32(0), jnp.int32(0), jnp.int32(1 << 24)
-    for k in range(lengths_ref.shape[0]):
-        edge = edge + lengths_ref[k]
-        start = jnp.where(edge <= last, edge, start)
-        end = jnp.where(edge > last, jnp.minimum(end, edge), end)
-    return lax.div(end, jnp.int32(blocks)) - segment, start - segment * blocks
 
 
 def write_exact(ref, o, m, l):
@@ -86,7 +93,7 @@
     return o, m, (high + low * (1.0 / 32768.0)) * 0.5
 
 
-def attend_kernel(own, factor, segment_ref, lengths_ref, q_ref, k_ref, v_ref, out_ref, s_ref):
+def attend_kernel(own, factor, live_ref, q_ref, k_ref, v_ref, out_ref, s_ref):
     kv_count, key_rows, dim = k_ref.shape
     width = q_ref.shape[2]
     blocks = out_ref.shape[0]
@@ -94,25 +101,30 @@
     sharing = wide // TAIL
     lanes = kv_count * wide
     count = key_rows // BLOCK
-    n_live, first = place_of(count, segment_ref, lengths_ref)
+    n_live, first = live_ref[0:1, 0:1], live_ref[1:2, 0:1]
+    some = jnp.max(live_ref[0:1, :])
     write = write_exact if own == 0 else write_coded
 
-    @pl.when(own >= n_live)
+    @pl.when(own >= some)
     def _():
         none = jnp.zeros((1, lanes), jnp.float32)
         for j in range(blocks):
             write(out_ref.at[j], jnp.zeros((dim, lanes), jnp.float32), none + NOTHING, none)
 
-    @pl.when(own < n_live)
+    @pl.when(own < some)
     def _():
-        tops, totals, outputs = [], [], []
-        for h in range(kv_count):
-            s = jnp.dot(k_ref[h], q_ref[h], preferred_element_type=jnp.float32)
-            s_ref[h] = s
+        per = STEP // BLOCK
+        steps = key_rows // STEP
+
+        def score(h, c):
+            s = jnp.dot(
+                k_ref[h, c * STEP : (c + 1) * STEP, :], q_ref[h], preferred_element_type=jnp.float32
+            )
+            s_ref[h, c * STEP : (c + 1) * STEP, :] = s
             peak = jnp.full((8, width), NEGATIVE, jnp.float32)
-            for b in range(count):
+            for b in range(per):
                 rows = s[b * BLOCK : (b + 1) * BLOCK]
-                if own == 0 and b == count - 1:
+                if own == 0 and c * per + b == count - 1:
                     lane = lax.broadcasted_iota(jnp.int32, (8, width), 1)
                     late = lax.broadcasted_iota(jnp.int32, (8, width), 0)
                     ahead = (lane < wide) & (late > lane // sharing)
@@ -121,17 +133,28 @@
                     peak = jnp.maximum(peak, corner)
                     rows = rows[: BLOCK - 8]
                 top = jnp.max(rows.reshape(-1, 8, width), axis=0)
-                peak = jnp.maximum(peak, jnp.where(b >= first, top, NEGATIVE))
-            tops.append(jnp.max(peak, axis=0, keepdims=True))
-        for h in range(kv_count):
-            total = jnp.zeros((8, width), jnp.float32)
+                peak = jnp.maximum(peak, jnp.where(c * per + b >= first, top, NEGATIVE))
+            return peak
+
+        def weigh(h, c, top, total):
             parts = []
-            for b in range(count):
+            for b in range(c * per, (c + 1) * per):
                 s = s_ref[h, b * BLOCK : (b + 1) * BLOCK, :]
-                level = jnp.where(b >= first, tops[h], -NEGATIVE)
-                w = jnp.exp2((s - level) * factor)
+                w = jnp.exp2((s - jnp.where(b >= first, top, -NEGATIVE)) * factor)
                 total = total + jnp.sum(w.reshape(-1, 8, width), axis=0)
                 parts.append(w.astype(jnp.bfloat16))
+            return parts, total
+
+        tops, totals, outputs = [], [], []
+        peaks = [score(0, c) for c in range(steps)]
+        for h in range(kv_count):
+            tops.append(jnp.max(functools.reduce(jnp.maximum, peaks), axis=0, keepdims=True))
+            peaks, parts, total = [], [], jnp.zeros((8, width), jnp.float32)
+            for c in range(steps):
+                more, total = weigh(h, c, tops[h], total)
+                parts += more
+                if h + 1 < kv_count:
+                    peaks.append(score(h + 1, c))
             totals.append(jnp.sum(total, axis=0, keepdims=True))
             outputs.append(
                 jnp.dot(v_ref[h], jnp.concatenate(parts, axis=0), preferred_element_type=jnp.float32)
@@ -190,8 +213,8 @@
 
 
 def body(queries, keys, values, doc_lengths):
-    rows, columns = lax.axis_size("z"), lax.axis_size("x")
-    o, z, x = lax.axis_index("outer"), lax.axis_index("z"), lax.axis_index("x")
+    columns = lax.axis_size("x")
+    o = lax.axis_index("outer")
     key_rows, kv_count, dim = keys.shape
     heads = queries.shape[1]
     sharing = heads // kv_count
@@ -209,10 +232,17 @@
     )(o.reshape(1).astype(jnp.int32), queries)
     held = [own] + [shifted(own, ("outer", "z"), -j) for j in range(1, REACH)]
 
-    segment = ((o * rows + z) * columns + x).reshape(1).astype(jnp.int32)
+    live = pl.pallas_call(
+        functools.partial(mask_kernel, key_rows // BLOCK),
+        out_shape=jax.ShapeDtypeStruct((8, 128), jnp.float32),
+        in_specs=on_chip(1),
+        out_specs=on_chip(1)[0],
+        compiler_params=room(4),
+        name="mask",
+    )(doc_lengths.reshape(1, -1))
     k_heads = jnp.transpose(keys, (1, 0, 2))
-    held, k_heads, values = lax.optimization_barrier((held, k_heads, values))
     v_heads = jnp.transpose(values, (1, 2, 0))
+    held, live, k_heads, v_heads = lax.optimization_barrier((held, live, k_heads, v_heads))
 
     stack = pl.pallas_call(
         stack_kernel,
@@ -236,7 +266,7 @@
             pl.pallas_call(
                 functools.partial(attend_kernel, u, factor),
                 out_shape=exact if u == 0 else coded,
-                in_specs=scalars() * 2 + on_chip(3),
+                in_specs=on_chip(4),
                 out_specs=on_chip(1)[0],
                 scratch_shapes=[pltpu.VMEM((kv_count, key_rows, width), jnp.float32)],
                 cost_estimate=pl.CostEstimate(
@@ -246,7 +276,7 @@
                 ),
                 compiler_params=room(16),
                 name=f"attend_{u}",
-            )(segment, doc_lengths, block, k_heads, v_heads)
+            )(live, block, k_heads, v_heads)
         )
     arrived = [partial[0]] + [shifted(partial[u], everywhere, u) for u in range(1, columns)]
     column = pl.pallas_call(

time: 55.5 us -> 54.7 us (0.986)
  Pallas kernels: 10.2 us -> 3.18 us
  waiting for transfers between devices: 18 us -> 23.6 us
  starting transfers between devices: 21.4 us -> 23.8 us
  local copies, waits for them, and re-layouts: 5.29 us -> 3.17 us
    pallas_call x4, Pallas kernels: 9.64 us -> 2.52 us  [body(): pl.pallas_call(functools.partial(attend_kernel, u, factor), out_shape=exa...]
    ppermute x13, waiting for transfers between devices: 18 us -> 23.6 us  [shifted(): return lax.ppermute(part, axes, [(i, (i + by) % size) for i in range(size)])]
    ppermute x13, starting transfers between devices: 21.4 us -> 23.8 us  [shifted(): return lax.ppermute(part, axes, [(i, (i + by) % size) for i in range(size)])]
    optimization_barrier x1 -> x0, local copies, waits for them, and re-layouts: 2.44 us -> none  [body(): held, k_heads, values = lax.optimization_barrier((held, k_heads, values))]
    unnamed x5 -> x8, local copies, waits for them, and re-layouts: 2.85 us -> 3.17 us
  transfers between devices with their start and end apart: 13 -> 13, of which waited for: 9 -> 9; matrix products, arithmetic and copies ran while one was open for 7% -> 4% of each run, Pallas kernels for 17% -> 5%
where the time goes in v4:
time: 54.7 us; the launch traced here: 54.6 us
  starting transfers between devices  23.8 us (44%)
  waiting for transfers between devices  23.6 us (43%)
  Pallas kernels  3.18 us (6%)
  local copies, waits for them, and re-layouts  3.17 us (6%)
  other arithmetic  0.65 us (1%)
    ppermute x13, starting transfers between devices, shifted(): return lax.ppermute(part, axes, [(i, (i + by) % size) for i in range(size)])  23.8 us
    ppermute x13, waiting for transfers between devices, shifted(): return lax.ppermute(part, axes, [(i, (i + by) % size) for i in range(size)])  23.6 us
    unnamed x8, local copies, waits for them, and re-layouts  3.17 us
    pallas_call x4, Pallas kernels, body(): pl.pallas_call(functools.partial(attend_kernel, u, factor), out_shape=exa...  2.52 us
  transfers between devices with their start and end apart: 13, of which 9 were waited for; matrix products, arithmetic and copies ran while one was open for 4% of the time, Pallas kernels for 5%

profile of v4, /device:TPU:1, one launch (start us, length us, event | category | flops | bytes accessed | tf_op | source)
XLA Modules:
  0.0 54.6 jit_solution(5705202249679572923)
XLA Ops:
  0.0 0.0 copy-start
  0.0 0.8 %copy-done = bf16[16,16,128]{2,1,0:T(8,128)(2,1)S(1)} copy-done((bf16[16,16,128]{2,1,0:T(8,128)(2,1)S(1)}, bf16[16,16,128]{2,1,0:T(8,128)(2,1)}, u32[]{:S(2)}) %copy-start) | copy-done | bytes 65560
  0.8 0.1 own_tails.1.refs_0_
  0.9 0.0 copy-start.1
  0.9 7.9 %collective-permute-start.2 = (bf16[128,128]{1,0:T(8,128)(2,1)S(1)}, bf16[128,128]{1,0:T(8,128)(2,1)S(1)}, u32[]{:S(2)}, u32[]{:S(2)}) collective-permute-start(bf16[128,128]{1,0:T(8,128)(2,1)S(1)} %own_tails.1.refs_0_), channel_id=1, source_target_pairs={{0,208},{16,224},{32,240},{48,0},{64,16},{80,32},{96,48},{112,64},... | collective-permute-start | bytes 98312 | tf_op jit(solution)/shard_map/ppermute | solution.py:24
  8.9 0.5 collective-permute-start.1
  9.4 0.5 collective-permute-start
  9.9 0.0 copy-done.1
  9.9 0.1 mask.1.live_ref
  10.0 0.0 copy-start.2
  10.0 1.5 %copy.8 = bf16[2048,2,128]{2,0,1:T(8,128)(2,1)S(1)} copy(bf16[2048,2,128]{2,1,0:T(2,128)(2,1)} %param.5) | data formatting | bytes 2097152 | tf_op args[1]
  11.5 0.1 copy-done.2
  11.5 0.8 %copy.6 = bf16[2048,2,128]{0,2,1:T(8,128)(2,1)S(1)} copy(bf16[2048,2,128]{2,1,0:T(2,128)(2,1)S(1)} %copy-done.2) | data formatting | bytes 2097152 | tf_op args[2]
  12.3 0.0 collective-permute-done.2.refs_3_
  12.3 0.6 %collective-permute-done.1.refs_2_ = bf16[128,128]{1,0:T(8,128)(2,1)S(1)} collective-permute-done((bf16[128,128]{1,0:T(8,128)(2,1)S(1)}, bf16[128,128]{1,0:T(8,128)(2,1)S(1)}, u32[]{:S(2)}, u32[]{:S(2)}) %collective-permute-start.1) | collective-permute-done | bytes 32800 | tf_op jit(solution)/shard_map/ppermute | solution.py:24
  12.9 1.5 %collective-permute-done.refs_1_ = bf16[128,128]{1,0:T(8,128)(2,1)S(1)} collective-permute-done((bf16[128,128]{1,0:T(8,128)(2,1)S(1)}, bf16[128,128]{1,0:T(8,128)(2,1)S(1)}, u32[]{:S(2)}, u32[]{:S(2)}) %collective-permute-start) | collective-permute-done | bytes 32800 | tf_op jit(solution)/shard_map/ppermute | solution.py:24
  14.4 0.1 stack_tails.1.q_ref
  14.5 5.5 %collective-permute-start.5 = (bf16[2,128,256]{2,1,0:T(8,128)(2,1)S(1)}, bf16[2,128,256]{2,1,0:T(8,128)(2,1)S(1)}, u32[]{:S(2)}, u32[]{:S(2)}) collective-permute-start(bf16[2,128,256]{2,1,0:T(8,128)(2,1)S(1)} %stack_tails.1.q_ref), channel_id=1, source_target_pairs={{0,248},{4,252},{8,0},{12,4},{16,8},{20,12},{24,16},{28,20},{32,24... | collective-permute-start | bytes 393224 | tf_op jit(solution)/shard_map/ppermute | solution.py:24
  19.9 0.8 %collective-permute-start.7 = (bf16[2,128,256]{2,1,0:T(8,128)(2,1)S(1)}, bf16[2,128,256]{2,1,0:T(8,128)(2,1)S(1)}, u32[]{:S(2)}, u32[]{:S(2)}) collective-permute-start(bf16[2,128,256]{2,1,0:T(8,128)(2,1)S(1)} %stack_tails.1.q_ref), channel_id=1, source_target_pairs={{0,244},{4,248},{8,252},{12,0},{16,4},{20,8},{24,12},{28,16},{32,2... | collective-permute-start | bytes 393224 | tf_op jit(solution)/shard_map/ppermute | solution.py:24
  20.7 2.6 %collective-permute-start.3 = (bf16[2,128,256]{2,1,0:T(8,128)(2,1)S(1)}, bf16[2,128,256]{2,1,0:T(8,128)(2,1)S(1)}, u32[]{:S(2)}, u32[]{:S(2)}) collective-permute-start(bf16[2,128,256]{2,1,0:T(8,128)(2,1)S(1)} %stack_tails.1.q_ref), channel_id=1, source_target_pairs={{0,252},{4,0},{8,4},{12,8},{16,12},{20,16},{24,20},{28,24},{32,28}... | collective-permute-start | bytes 393224 | tf_op jit(solution)/shard_map/ppermute | solution.py:24
  23.4 1.9 %attend_0.1.refs_0_ = f32[4,136,128]{2,1,0:T(8,128)S(1)} custom-call(f32[8,128]{1,0:T(8,128)S(1)} %mask.1.live_ref, bf16[2,128,256]{2,1,0:T(8,128)(2,1)S(1)} %stack_tails.1.q_ref, bf16[2,2048,128]{2,1,0:T(8,128)(2,1)S(1)} %bitcast.6, bf16[2,128,2048]{2,1,0:T(8,128)(2,1)S(1)} %bitcast.10), custom_call_target="tpu_custom_call" | custom-call | flops 536870912 | bytes 2097152 | tf_op jit(solution)/shard_map/attend_0/pallas_call | solution.py:266
  25.3 0.0 collective-permute-done.5.q_ref
  25.3 0.1 attend_2.1
  25.4 0.8 %collective-permute-start.6 = (s16[4,144,128]{2,1,0:T(8,128)(2,1)S(1)}, s16[4,144,128]{2,1,0:T(8,128)(2,1)S(1)}, u32[]{:S(2)}, u32[]{:S(2)}) collective-permute-start(s16[4,144,128]{2,1,0:T(8,128)(2,1)S(1)} %attend_2.1), channel_id=1, source_target_pairs={{0,8},{4,12},{8,16},{12,20},{16,24},{20,28},{24,32},{28,36},{32,40... | collective-permute-start | bytes 442376 | tf_op jit(solution)/shard_map/ppermute | solution.py:24
  26.3 0.0 collective-permute-done.7.q_ref
  26.3 0.1 attend_3.1
  26.4 1.0 %collective-permute-start.8 = (s16[4,144,128]{2,1,0:T(8,128)(2,1)S(1)}, s16[4,144,128]{2,1,0:T(8,128)(2,1)S(1)}, u32[]{:S(2)}, u32[]{:S(2)}) collective-permute-start(s16[4,144,128]{2,1,0:T(8,128)(2,1)S(1)} %attend_3.1), channel_id=1, source_target_pairs={{0,12},{4,16},{8,20},{12,24},{16,28},{20,32},{24,36},{28,40},{32,4... | collective-permute-start | bytes 442376 | tf_op jit(solution)/shard_map/ppermute | solution.py:24
  27.4 1.1 %collective-permute-done.3.q_ref = bf16[2,128,256]{2,1,0:T(8,128)(2,1)S(1)} collective-permute-done((bf16[2,128,256]{2,1,0:T(8,128)(2,1)S(1)}, bf16[2,128,256]{2,1,0:T(8,128)(2,1)S(1)}, u32[]{:S(2)}, u32[]{:S(2)}) %collective-permute-start.3) | collective-permute-done | bytes 131104 | tf_op jit(solution)/shard_map/ppermute | solution.py:24
  28.6 0.3 attend_1.1
  28.9 1.1 %collective-permute-start.4 = (s16[4,144,128]{2,1,0:T(8,128)(2,1)S(1)}, s16[4,144,128]{2,1,0:T(8,128)(2,1)S(1)}, u32[]{:S(2)}, u32[]{:S(2)}) collective-permute-start(s16[4,144,128]{2,1,0:T(8,128)(2,1)S(1)} %attend_1.1), channel_id=1, source_target_pairs={{0,4},{4,8},{8,12},{12,16},{16,20},{20,24},{24,28},{28,32},{32,36}... | collective-permute-start | bytes 442376 | tf_op jit(solution)/shard_map/ppermute | solution.py:24
  30.0 5.9 %collective-permute-done.6.refs_2_ = s16[4,144,128]{2,1,0:T(8,128)(2,1)S(1)} collective-permute-done((s16[4,144,128]{2,1,0:T(8,128)(2,1)S(1)}, s16[4,144,128]{2,1,0:T(8,128)(2,1)S(1)}, u32[]{:S(2)}, u32[]{:S(2)}) %collective-permute-start.6) | collective-permute-done | bytes 147488 | tf_op jit(solution)/shard_map/ppermute | solution.py:24
  35.9 0.0 collective-permute-done.8.refs_3_
  35.9 5.1 %collective-permute-done.4.refs_1_ = s16[4,144,128]{2,1,0:T(8,128)(2,1)S(1)} collective-permute-done((s16[4,144,128]{2,1,0:T(8,128)(2,1)S(1)}, s16[4,144,128]{2,1,0:T(8,128)(2,1)S(1)}, u32[]{:S(2)}, u32[]{:S(2)}) %collective-permute-start.4) | collective-permute-done | bytes 147488 | tf_op jit(solution)/shard_map/ppermute | solution.py:24
  41.0 0.3 merge_columns.1
  41.3 0.1 collective-permute-start.9
  41.4 0.1 collective-permute-start.10
  41.5 0.4 collective-permute-start.11
  41.9 4.1 %collective-permute-done.9.refs_1_ = s16[144,128]{1,0:T(8,128)(2,1)S(1)} collective-permute-done((s16[144,128]{1,0:T(8,128)(2,1)S(1)}, s16[144,128]{1,0:T(8,128)(2,1)S(1)}, u32[]{:S(2)}, u32[]{:S(2)}) %collective-permute-start.9) | collective-permute-done | bytes 36896 | tf_op jit(solution)/shard_map/ppermute | solution.py:24
  46.0 1.1 %collective-permute-done.10.refs_2_ = s16[144,128]{1,0:T(8,128)(2,1)S(1)} collective-permute-done((s16[144,128]{1,0:T(8,128)(2,1)S(1)}, s16[144,128]{1,0:T(8,128)(2,1)S(1)}, u32[]{:S(2)}, u32[]{:S(2)}) %collective-permute-start.10) | collective-permute-done | bytes 36896 | tf_op jit(solution)/shard_map/ppermute | solution.py:24
  47.1 3.3 %collective-permute-done.11.refs_3_ = s16[144,128]{1,0:T(8,128)(2,1)S(1)} collective-permute-done((s16[144,128]{1,0:T(8,128)(2,1)S(1)}, s16[144,128]{1,0:T(8,128)(2,1)S(1)}, u32[]{:S(2)}, u32[]{:S(2)}) %collective-permute-start.11) | collective-permute-done | bytes 36896 | tf_op jit(solution)/shard_map/ppermute | solution.py:24
  50.4 0.1 finish.1
  50.5 2.5 %collective-permute-start.12 = (bf16[8,16,128]{2,1,0:T(8,128)(2,1)S(1)}, bf16[8,16,128]{2,1,0:T(8,128)(2,1)S(1)}, u32[]{:S(2)}, u32[]{:S(2)}) collective-permute-start(bf16[8,16,128]{2,1,0:T(8,128)(2,1)S(1)} %finish.1), channel_id=1, source_target_pairs={{0,128},{128,0},{1,129},{129,1},{2,130},{130,2},{3,131},{131,3},{4... | collective-permute-start | bytes 98312 | tf_op jit(solution)/shard_map/ppermute | solution.py:24
  53.0 0.9 %collective-permute-done.12 = bf16[8,16,128]{2,1,0:T(8,128)(2,1)S(1)} collective-permute-done((bf16[8,16,128]{2,1,0:T(8,128)(2,1)S(1)}, bf16[8,16,128]{2,1,0:T(8,128)(2,1)S(1)}, u32[]{:S(2)}, u32[]{:S(2)}) %collective-permute-start.12) | collective-permute-done | bytes 32800 | tf_op jit(solution)/shard_map/ppermute | solution.py:24
  53.9 0.6 %pad_maximum_fusion = bf16[16,16,128]{2,1,0:T(8,128)(2,1)} fusion(bf16[8,16,128]{2,1,0:T(8,128)(2,1)S(1)} %get-tuple-element.30, bf16[8,16,128]{2,1,0:T(8,128)(2,1)S(1)} %get-tuple-element.29), kind=kLoop, calls=%fused_computation.1 | loop fusion | flops 32768 | bytes 131072 | tf_op jit(solution)/shard_map/concatenate | solution.py:303
  (1 shorter events, 0.0 us)
Async XLA Ops:
  0.0 0.8 %copy-start = (bf16[16,16,128]{2,1,0:T(8,128)(2,1)S(1)}, bf16[16,16,128]{2,1,0:T(8,128)(2,1)}, u32[]{:S(2)}) copy-start(bf16[16,16,128]{2,1,0:T(8,128)(2,1)} %q_ref.1) | copy-start | bytes 196612
  0.9 9.0 %copy-start.1 = (s32[32]{0:T(128)S(1)}, s32[32]{0:T(128)}, u32[]{:S(2)}) copy-start(s32[32]{0:T(128)} %param.7) | copy-start | bytes 388
  0.9 11.4 %collective-permute-start.2 = (bf16[128,128]{1,0:T(8,128)(2,1)S(1)}, bf16[128,128]{1,0:T(8,128)(2,1)S(1)}, u32[]{:S(2)}, u32[]{:S(2)}) collective-permute-start(bf16[128,128]{1,0:T(8,128)(2,1)S(1)} %own_tails.1.refs_0_), channel_id=1, source_target_pairs={{0,208},{16,224},{32,240},{48,0},{64,16},{80,32},{96,48},{112,64},... | collective-permute-start | bytes 98312 | tf_op jit(solution)/shard_map/ppermute | solution.py:24
  8.9 4.0 %collective-permute-start.1 = (bf16[128,128]{1,0:T(8,128)(2,1)S(1)}, bf16[128,128]{1,0:T(8,128)(2,1)S(1)}, u32[]{:S(2)}, u32[]{:S(2)}) collective-permute-start(bf16[128,128]{1,0:T(8,128)(2,1)S(1)} %own_tails.1.refs_0_), channel_id=1, source_target_pairs={{0,224},{16,240},{32,0},{48,16},{64,32},{80,48},{96,64},{112,80},{... | collective-permute-start | bytes 98312 | tf_op jit(solution)/shard_map/ppermute | solution.py:24
  9.4 4.9 %collective-permute-start = (bf16[128,128]{1,0:T(8,128)(2,1)S(1)}, bf16[128,128]{1,0:T(8,128)(2,1)S(1)}, u32[]{:S(2)}, u32[]{:S(2)}) collective-permute-start(bf16[128,128]{1,0:T(8,128)(2,1)S(1)} %own_tails.1.refs_0_), channel_id=1, source_target_pairs={{0,240},{16,0},{32,16},{48,32},{64,48},{80,64},{96,80},{112,96},{1... | collective-permute-start | bytes 98312 | tf_op jit(solution)/shard_map/ppermute | solution.py:24
  10.0 1.5 %copy-start.2 = (bf16[2048,2,128]{2,1,0:T(2,128)(2,1)S(1)}, bf16[2048,2,128]{2,1,0:T(2,128)(2,1)}, u32[]{:S(2)}) copy-start(bf16[2048,2,128]{2,1,0:T(2,128)(2,1)} %param.6) | copy-start | bytes 3145732
  14.5 10.8 %collective-permute-start.5 = (bf16[2,128,256]{2,1,0:T(8,128)(2,1)S(1)}, bf16[2,128,256]{2,1,0:T(8,128)(2,1)S(1)}, u32[]{:S(2)}, u32[]{:S(2)}) collective-permute-start(bf16[2,128,256]{2,1,0:T(8,128)(2,1)S(1)} %stack_tails.1.q_ref), channel_id=1, source_target_pairs={{0,248},{4,252},{8,0},{12,4},{16,8},{20,12},{24,16},{28,20},{32,24... | collective-permute-start | bytes 393224 | tf_op jit(solution)/shard_map/ppermute | solution.py:24
  19.9 6.3 %collective-permute-start.7 = (bf16[2,128,256]{2,1,0:T(8,128)(2,1)S(1)}, bf16[2,128,256]{2,1,0:T(8,128)(2,1)S(1)}, u32[]{:S(2)}, u32[]{:S(2)}) collective-permute-start(bf16[2,128,256]{2,1,0:T(8,128)(2,1)S(1)} %stack_tails.1.q_ref), channel_id=1, source_target_pairs={{0,244},{4,248},{8,252},{12,0},{16,4},{20,8},{24,12},{28,16},{32,2... | collective-permute-start | bytes 393224 | tf_op jit(solution)/shard_map/ppermute | solution.py:24
  20.7 7.8 %collective-permute-start.3 = (bf16[2,128,256]{2,1,0:T(8,128)(2,1)S(1)}, bf16[2,128,256]{2,1,0:T(8,128)(2,1)S(1)}, u32[]{:S(2)}, u32[]{:S(2)}) collective-permute-start(bf16[2,128,256]{2,1,0:T(8,128)(2,1)S(1)} %stack_tails.1.q_ref), channel_id=1, source_target_pairs={{0,252},{4,0},{8,4},{12,8},{16,12},{20,16},{24,20},{28,24},{32,28}... | collective-permute-start | bytes 393224 | tf_op jit(solution)/shard_map/ppermute | solution.py:24
  25.4 10.5 %collective-permute-start.6 = (s16[4,144,128]{2,1,0:T(8,128)(2,1)S(1)}, s16[4,144,128]{2,1,0:T(8,128)(2,1)S(1)}, u32[]{:S(2)}, u32[]{:S(2)}) collective-permute-start(s16[4,144,128]{2,1,0:T(8,128)(2,1)S(1)} %attend_2.1), channel_id=1, source_target_pairs={{0,8},{4,12},{8,16},{12,20},{16,24},{20,28},{24,32},{28,36},{32,40... | collective-permute-start | bytes 442376 | tf_op jit(solution)/shard_map/ppermute | solution.py:24
  26.4 9.5 %collective-permute-start.8 = (s16[4,144,128]{2,1,0:T(8,128)(2,1)S(1)}, s16[4,144,128]{2,1,0:T(8,128)(2,1)S(1)}, u32[]{:S(2)}, u32[]{:S(2)}) collective-permute-start(s16[4,144,128]{2,1,0:T(8,128)(2,1)S(1)} %attend_3.1), channel_id=1, source_target_pairs={{0,12},{4,16},{8,20},{12,24},{16,28},{20,32},{24,36},{28,40},{32,4... | collective-permute-start | bytes 442376 | tf_op jit(solution)/shard_map/ppermute | solution.py:24
  28.9 12.1 %collective-permute-start.4 = (s16[4,144,128]{2,1,0:T(8,128)(2,1)S(1)}, s16[4,144,128]{2,1,0:T(8,128)(2,1)S(1)}, u32[]{:S(2)}, u32[]{:S(2)}) collective-permute-start(s16[4,144,128]{2,1,0:T(8,128)(2,1)S(1)} %attend_1.1), channel_id=1, source_target_pairs={{0,4},{4,8},{8,12},{12,16},{16,20},{20,24},{24,28},{28,32},{32,36}... | collective-permute-start | bytes 442376 | tf_op jit(solution)/shard_map/ppermute | solution.py:24
  41.3 4.7 %collective-permute-start.9 = (s16[144,128]{1,0:T(8,128)(2,1)S(1)}, s16[144,128]{1,0:T(8,128)(2,1)S(1)}, u32[]{:S(2)}, u32[]{:S(2)}) collective-permute-start(s16[144,128]{1,0:T(8,128)(2,1)S(1)} %get-tuple-element.26), channel_id=1, source_target_pairs={{0,16},{16,32},{32,48},{48,64},{64,80},{80,96},{96,112},{112,128},... | collective-permute-start | bytes 110600 | tf_op jit(solution)/shard_map/ppermute | solution.py:24
  41.4 5.7 %collective-permute-start.10 = (s16[144,128]{1,0:T(8,128)(2,1)S(1)}, s16[144,128]{1,0:T(8,128)(2,1)S(1)}, u32[]{:S(2)}, u32[]{:S(2)}) collective-permute-start(s16[144,128]{1,0:T(8,128)(2,1)S(1)} %get-tuple-element.27), channel_id=1, source_target_pairs={{0,32},{16,48},{32,64},{48,80},{64,96},{80,112},{96,128},{112,144}... | collective-permute-start | bytes 110600 | tf_op jit(solution)/shard_map/ppermute | solution.py:24
  41.5 8.9 %collective-permute-start.11 = (s16[144,128]{1,0:T(8,128)(2,1)S(1)}, s16[144,128]{1,0:T(8,128)(2,1)S(1)}, u32[]{:S(2)}, u32[]{:S(2)}) collective-permute-start(s16[144,128]{1,0:T(8,128)(2,1)S(1)} %get-tuple-element.28), channel_id=1, source_target_pairs={{0,48},{16,64},{32,80},{48,96},{64,112},{80,128},{96,144},{112,160... | collective-permute-start | bytes 110600 | tf_op jit(solution)/shard_map/ppermute | solution.py:24
  50.5 3.4 %collective-permute-start.12 = (bf16[8,16,128]{2,1,0:T(8,128)(2,1)S(1)}, bf16[8,16,128]{2,1,0:T(8,128)(2,1)S(1)}, u32[]{:S(2)}, u32[]{:S(2)}) collective-permute-start(bf16[8,16,128]{2,1,0:T(8,128)(2,1)S(1)} %finish.1), channel_id=1, source_target_pairs={{0,128},{128,0},{1,129},{129,1},{2,130},{130,2},{3,131},{131,3},{4... | collective-permute-start | bytes 98312 | tf_op jit(solution)/shard_map/ppermute | solution.py:24

commit v5 on v4

--- a/solution.py
+++ b/solution.py
@@ -14,7 +14,7 @@
 TAIL = 8
 NOTHING = -32768.0
 EXTRA = 8
-CODED = 16
+CODED = 8
 COLUMNS = 4
 REACH = 4
 
@@ -111,16 +111,15 @@
         for j in range(blocks):
             write(out_ref.at[j], jnp.zeros((dim, lanes), jnp.float32), none + NOTHING, none)
 
-    @pl.when(own < some)
-    def _():
+    def run(width, live_blocks):
         per = STEP // BLOCK
         steps = key_rows // STEP
 
         def score(h, c):
             s = jnp.dot(
-                k_ref[h, c * STEP : (c + 1) * STEP, :], q_ref[h], preferred_element_type=jnp.float32
+                k_ref[h, c * STEP : (c + 1) * STEP, :], q_ref[h, :, :width], preferred_element_type=jnp.float32
             )
-            s_ref[h, c * STEP : (c + 1) * STEP, :] = s
+            s_ref[h, c * STEP : (c + 1) * STEP, :width] = s
             peak = jnp.full((8, width), NEGATIVE, jnp.float32)
             for b in range(per):
                 rows = s[b * BLOCK : (b + 1) * BLOCK]
@@ -129,7 +128,7 @@
                     late = lax.broadcasted_iota(jnp.int32, (8, width), 0)
                     ahead = (lane < wide) & (late > lane // sharing)
                     corner = jnp.where(ahead, NEGATIVE, rows[BLOCK - 8 :])
-                    s_ref[h, key_rows - 8 :, :] = corner
+                    s_ref[h, key_rows - 8 :, :width] = corner
                     peak = jnp.maximum(peak, corner)
                     rows = rows[: BLOCK - 8]
                 top = jnp.max(rows.reshape(-1, 8, width), axis=0)
@@ -139,7 +138,7 @@
         def weigh(h, c, top, total):
             parts = []
             for b in range(c * per, (c + 1) * per):
-                s = s_ref[h, b * BLOCK : (b + 1) * BLOCK, :]
+                s = s_ref[h, b * BLOCK : (b + 1) * BLOCK, :width]
                 w = jnp.exp2((s - jnp.where(b >= first, top, -NEGATIVE)) * factor)
                 total = total + jnp.sum(w.reshape(-1, 8, width), axis=0)
                 parts.append(w.astype(jnp.bfloat16))
@@ -159,7 +158,10 @@
             outputs.append(
                 jnp.dot(v_ref[h], jnp.concatenate(parts, axis=0), preferred_element_type=jnp.float32)
             )
-        for j in range(blocks):
+        none = jnp.zeros((1, lanes), jnp.float32)
+        for j in range(live_blocks, blocks):
+            write(out_ref.at[j], jnp.zeros((dim, lanes), jnp.float32), none + NOTHING, none)
+        for j in range(live_blocks):
             here = slice(j * wide, (j + 1) * wide)
             keep = own + blocks * j < n_live
             o = jnp.concatenate([a[:, here] for a in outputs], axis=1)
@@ -170,6 +172,16 @@
             write(
                 out_ref.at[j], jnp.where(keep, o * f, 0.0), jnp.where(keep, whole, NOTHING), l * f
             )
+
+    half = blocks // 2
+
+    @pl.when((own < some) & (own + COLUMNS * half >= some))
+    def _():
+        run(half * wide, half)
+
+    @pl.when(own + COLUMNS * half < some)
+    def _():
+        run(width, blocks)
 
 
 def merge(parts):

time: 54.7 us -> 52.9 us (0.967); the launches traced: 54.6 us -> 53.6 us
  waiting for transfers between devices: 23.6 us -> 22.5 us
  starting transfers between devices: 23.8 us -> 24.7 us
  Pallas kernels: 3.18 us -> 2.51 us
    ppermute x13, waiting for transfers between devices: 23.6 us -> 22.5 us  [shifted(): return lax.ppermute(part, axes, [(i, (i + by) % size) for i in range(size)])]
    ppermute x13, starting transfers between devices: 23.8 us -> 24.7 us  [shifted(): return lax.ppermute(part, axes, [(i, (i + by) % size) for i in range(size)])]
    pallas_call x4, Pallas kernels: 2.52 us -> 1.86 us  [body(): pl.pallas_call(functools.partial(attend_kernel, u, factor), out_shape=exa...]
  transfers between devices with their start and end apart: 13 -> 13, of which waited for: 9 -> 11; matrix products, arithmetic and copies ran while one was open for 4% -> 4% of each run, Pallas kernels for 5% -> 4%
where the time goes in v5:
time: 52.9 us; the launch traced here: 53.6 us
  starting transfers between devices  24.7 us (47%)
  waiting for transfers between devices  22.5 us (43%)
  local copies, waits for them, and re-layouts  3.17 us (6%)
  Pallas kernels  2.51 us (5%)
  other arithmetic  0.65 us (1%)
    ppermute x13, starting transfers between devices, shifted(): return lax.ppermute(part, axes, [(i, (i + by) % size) for i in range(size)])  24.7 us
    ppermute x13, waiting for transfers between devices, shifted(): return lax.ppermute(part, axes, [(i, (i + by) % size) for i in range(size)])  22.5 us
    unnamed x8, local copies, waits for them, and re-layouts  3.17 us
    pallas_call x4, Pallas kernels, body(): pl.pallas_call(functools.partial(attend_kernel, u, factor), out_shape=exa...  1.86 us
  transfers between devices with their start and end apart: 13, of which 11 were waited for; matrix products, arithmetic and copies ran while one was open for 4% of the time, Pallas kernels for 4%

profile of v5, /device:TPU:1, one launch (start us, length us, event | category | flops | bytes accessed | tf_op | source)
XLA Modules:
  0.0 53.6 jit_solution(4092695264673839367)
XLA Ops:
  0.0 0.0 copy-start
  0.0 0.8 %copy-done = bf16[16,16,128]{2,1,0:T(8,128)(2,1)S(1)} copy-done((bf16[16,16,128]{2,1,0:T(8,128)(2,1)S(1)}, bf16[16,16,128]{2,1,0:T(8,128)(2,1)}, u32[]{:S(2)}) %copy-start) | copy-done | bytes 65560
  0.8 0.1 own_tails.1.refs_0_
  0.9 0.0 copy-start.1
  0.9 7.9 %collective-permute-start.2 = (bf16[128,128]{1,0:T(8,128)(2,1)S(1)}, bf16[128,128]{1,0:T(8,128)(2,1)S(1)}, u32[]{:S(2)}, u32[]{:S(2)}) collective-permute-start(bf16[128,128]{1,0:T(8,128)(2,1)S(1)} %own_tails.1.refs_0_), channel_id=1, source_target_pairs={{0,208},{16,224},{32,240},{48,0},{64,16},{80,32},{96,48},{112,64},... | collective-permute-start | bytes 98312 | tf_op jit(solution)/shard_map/ppermute | solution.py:24
  8.9 0.5 %collective-permute-start.1 = (bf16[128,128]{1,0:T(8,128)(2,1)S(1)}, bf16[128,128]{1,0:T(8,128)(2,1)S(1)}, u32[]{:S(2)}, u32[]{:S(2)}) collective-permute-start(bf16[128,128]{1,0:T(8,128)(2,1)S(1)} %own_tails.1.refs_0_), channel_id=1, source_target_pairs={{0,224},{16,240},{32,0},{48,16},{64,32},{80,48},{96,64},{112,80},{... | collective-permute-start | bytes 98312 | tf_op jit(solution)/shard_map/ppermute | solution.py:24
  9.4 0.5 collective-permute-start
  9.9 0.0 copy-done.1
  9.9 0.1 mask.1.live_ref
  10.0 0.0 copy-start.2
  10.0 1.5 %copy.8 = bf16[2048,2,128]{2,0,1:T(8,128)(2,1)S(1)} copy(bf16[2048,2,128]{2,1,0:T(2,128)(2,1)} %param.5) | data formatting | bytes 2097152 | tf_op args[1]
  11.5 0.1 copy-done.2
  11.5 0.8 %copy.6 = bf16[2048,2,128]{0,2,1:T(8,128)(2,1)S(1)} copy(bf16[2048,2,128]{2,1,0:T(2,128)(2,1)S(1)} %copy-done.2) | data formatting | bytes 2097152 | tf_op args[2]
  12.3 0.0 collective-permute-done.2.refs_3_
  12.3 0.6 %collective-permute-done.1.refs_2_ = bf16[128,128]{1,0:T(8,128)(2,1)S(1)} collective-permute-done((bf16[128,128]{1,0:T(8,128)(2,1)S(1)}, bf16[128,128]{1,0:T(8,128)(2,1)S(1)}, u32[]{:S(2)}, u32[]{:S(2)}) %collective-permute-start.1) | collective-permute-done | bytes 32800 | tf_op jit(solution)/shard_map/ppermute | solution.py:24
  12.9 1.5 %collective-permute-done.refs_1_ = bf16[128,128]{1,0:T(8,128)(2,1)S(1)} collective-permute-done((bf16[128,128]{1,0:T(8,128)(2,1)S(1)}, bf16[128,128]{1,0:T(8,128)(2,1)S(1)}, u32[]{:S(2)}, u32[]{:S(2)}) %collective-permute-start) | collective-permute-done | bytes 32800 | tf_op jit(solution)/shard_map/ppermute | solution.py:24
  14.4 0.1 stack_tails.1.q_ref
  14.5 5.5 %collective-permute-start.5 = (bf16[2,128,256]{2,1,0:T(8,128)(2,1)S(1)}, bf16[2,128,256]{2,1,0:T(8,128)(2,1)S(1)}, u32[]{:S(2)}, u32[]{:S(2)}) collective-permute-start(bf16[2,128,256]{2,1,0:T(8,128)(2,1)S(1)} %stack_tails.1.q_ref), channel_id=1, source_target_pairs={{0,248},{4,252},{8,0},{12,4},{16,8},{20,12},{24,16},{28,20},{32,24... | collective-permute-start | bytes 393224 | tf_op jit(solution)/shard_map/ppermute | solution.py:24
  19.9 0.8 %collective-permute-start.7 = (bf16[2,128,256]{2,1,0:T(8,128)(2,1)S(1)}, bf16[2,128,256]{2,1,0:T(8,128)(2,1)S(1)}, u32[]{:S(2)}, u32[]{:S(2)}) collective-permute-start(bf16[2,128,256]{2,1,0:T(8,128)(2,1)S(1)} %stack_tails.1.q_ref), channel_id=1, source_target_pairs={{0,244},{4,248},{8,252},{12,0},{16,4},{20,8},{24,12},{28,16},{32,2... | collective-permute-start | bytes 393224 | tf_op jit(solution)/shard_map/ppermute | solution.py:24
  20.7 2.6 %collective-permute-start.3 = (bf16[2,128,256]{2,1,0:T(8,128)(2,1)S(1)}, bf16[2,128,256]{2,1,0:T(8,128)(2,1)S(1)}, u32[]{:S(2)}, u32[]{:S(2)}) collective-permute-start(bf16[2,128,256]{2,1,0:T(8,128)(2,1)S(1)} %stack_tails.1.q_ref), channel_id=1, source_target_pairs={{0,252},{4,0},{8,4},{12,8},{16,12},{20,16},{24,20},{28,24},{32,28}... | collective-permute-start | bytes 393224 | tf_op jit(solution)/shard_map/ppermute | solution.py:24
  23.4 1.2 %attend_0.1.refs_0_ = f32[4,136,128]{2,1,0:T(8,128)S(1)} custom-call(f32[8,128]{1,0:T(8,128)S(1)} %mask.1.live_ref, bf16[2,128,256]{2,1,0:T(8,128)(2,1)S(1)} %stack_tails.1.q_ref, bf16[2,2048,128]{2,1,0:T(8,128)(2,1)S(1)} %bitcast.6, bf16[2,128,2048]{2,1,0:T(8,128)(2,1)S(1)} %bitcast.10), custom_call_target="tpu_custom_call" | custom-call | flops 536870912 | bytes 2097152 | tf_op jit(solution)/shard_map/attend_0/pallas_call | solution.py:278
  24.6 0.0 collective-permute-done.5.q_ref
  24.6 0.1 attend_2.1
  24.8 0.1 collective-permute-start.6
  24.9 1.3 %collective-permute-done.7.q_ref = bf16[2,128,256]{2,1,0:T(8,128)(2,1)S(1)} collective-permute-done((bf16[2,128,256]{2,1,0:T(8,128)(2,1)S(1)}, bf16[2,128,256]{2,1,0:T(8,128)(2,1)S(1)}, u32[]{:S(2)}, u32[]{:S(2)}) %collective-permute-start.7) | collective-permute-done | bytes 131104 | tf_op jit(solution)/shard_map/ppermute | solution.py:24
  26.2 0.3 attend_3.1
  26.6 0.4 collective-permute-start.8
  27.0 1.6 %collective-permute-done.3.q_ref = bf16[2,128,256]{2,1,0:T(8,128)(2,1)S(1)} collective-permute-done((bf16[2,128,256]{2,1,0:T(8,128)(2,1)S(1)}, bf16[2,128,256]{2,1,0:T(8,128)(2,1)S(1)}, u32[]{:S(2)}, u32[]{:S(2)}) %collective-permute-start.3) | collective-permute-done | bytes 131104 | tf_op jit(solution)/shard_map/ppermute | solution.py:24
  28.6 0.1 attend_1.1
  28.7 0.1 collective-permute-start.4
  28.8 5.7 %collective-permute-done.6.refs_2_ = s16[4,136,128]{2,1,0:T(8,128)(2,1)S(1)} collective-permute-done((s16[4,136,128]{2,1,0:T(8,128)(2,1)S(1)}, s16[4,136,128]{2,1,0:T(8,128)(2,1)S(1)}, u32[]{:S(2)}, u32[]{:S(2)}) %collective-permute-start.6) | collective-permute-done | bytes 139296 | tf_op jit(solution)/shard_map/ppermute | solution.py:24
  34.6 0.7 %collective-permute-done.8.refs_3_ = s16[4,136,128]{2,1,0:T(8,128)(2,1)S(1)} collective-permute-done((s16[4,136,128]{2,1,0:T(8,128)(2,1)S(1)}, s16[4,136,128]{2,1,0:T(8,128)(2,1)S(1)}, u32[]{:S(2)}, u32[]{:S(2)}) %collective-permute-start.8) | collective-permute-done | bytes 139296 | tf_op jit(solution)/shard_map/ppermute | solution.py:24
  35.2 4.2 %collective-permute-done.4.refs_1_ = s16[4,136,128]{2,1,0:T(8,128)(2,1)S(1)} collective-permute-done((s16[4,136,128]{2,1,0:T(8,128)(2,1)S(1)}, s16[4,136,128]{2,1,0:T(8,128)(2,1)S(1)}, u32[]{:S(2)}, u32[]{:S(2)}) %collective-permute-start.4) | collective-permute-done | bytes 139296 | tf_op jit(solution)/shard_map/ppermute | solution.py:24
  39.4 0.3 merge_columns.1
  39.7 0.1 collective-permute-start.9
  39.8 0.1 collective-permute-start.10
  39.9 2.3 %collective-permute-start.11 = (s16[136,128]{1,0:T(8,128)(2,1)S(1)}, s16[136,128]{1,0:T(8,128)(2,1)S(1)}, u32[]{:S(2)}, u32[]{:S(2)}) collective-permute-start(s16[136,128]{1,0:T(8,128)(2,1)S(1)} %get-tuple-element.28), channel_id=1, source_target_pairs={{0,48},{16,64},{32,80},{48,96},{64,112},{80,128},{96,144},{112,160... | collective-permute-start | bytes 104456 | tf_op jit(solution)/shard_map/ppermute | solution.py:24
  42.2 2.2 %collective-permute-done.9.refs_1_ = s16[136,128]{1,0:T(8,128)(2,1)S(1)} collective-permute-done((s16[136,128]{1,0:T(8,128)(2,1)S(1)}, s16[136,128]{1,0:T(8,128)(2,1)S(1)}, u32[]{:S(2)}, u32[]{:S(2)}) %collective-permute-start.9) | collective-permute-done | bytes 34848 | tf_op jit(solution)/shard_map/ppermute | solution.py:24
  44.4 1.1 %collective-permute-done.10.refs_2_ = s16[136,128]{1,0:T(8,128)(2,1)S(1)} collective-permute-done((s16[136,128]{1,0:T(8,128)(2,1)S(1)}, s16[136,128]{1,0:T(8,128)(2,1)S(1)}, u32[]{:S(2)}, u32[]{:S(2)}) %collective-permute-start.10) | collective-permute-done | bytes 34848 | tf_op jit(solution)/shard_map/ppermute | solution.py:24
  45.5 2.7 %collective-permute-done.11.refs_3_ = s16[136,128]{1,0:T(8,128)(2,1)S(1)} collective-permute-done((s16[136,128]{1,0:T(8,128)(2,1)S(1)}, s16[136,128]{1,0:T(8,128)(2,1)S(1)}, u32[]{:S(2)}, u32[]{:S(2)}) %collective-permute-start.11) | collective-permute-done | bytes 34848 | tf_op jit(solution)/shard_map/ppermute | solution.py:24
  48.2 0.1 finish.1
  48.3 3.8 %collective-permute-start.12 = (bf16[8,16,128]{2,1,0:T(8,128)(2,1)S(1)}, bf16[8,16,128]{2,1,0:T(8,128)(2,1)S(1)}, u32[]{:S(2)}, u32[]{:S(2)}) collective-permute-start(bf16[8,16,128]{2,1,0:T(8,128)(2,1)S(1)} %finish.1), channel_id=1, source_target_pairs={{0,128},{128,0},{1,129},{129,1},{2,130},{130,2},{3,131},{131,3},{4... | collective-permute-start | bytes 98312 | tf_op jit(solution)/shard_map/ppermute | solution.py:24
  52.1 0.9 %collective-permute-done.12 = bf16[8,16,128]{2,1,0:T(8,128)(2,1)S(1)} collective-permute-done((bf16[8,16,128]{2,1,0:T(8,128)(2,1)S(1)}, bf16[8,16,128]{2,1,0:T(8,128)(2,1)S(1)}, u32[]{:S(2)}, u32[]{:S(2)}) %collective-permute-start.12) | collective-permute-done | bytes 32800 | tf_op jit(solution)/shard_map/ppermute | solution.py:24
  53.0 0.6 %pad_maximum_fusion = bf16[16,16,128]{2,1,0:T(8,128)(2,1)} fusion(bf16[8,16,128]{2,1,0:T(8,128)(2,1)S(1)} %get-tuple-element.30, bf16[8,16,128]{2,1,0:T(8,128)(2,1)S(1)} %get-tuple-element.29), kind=kLoop, calls=%fused_computation.1 | loop fusion | flops 32768 | bytes 131072 | tf_op jit(solution)/shard_map/concatenate | solution.py:315
  (1 shorter events, 0.0 us)
Async XLA Ops:
  0.0 0.8 %copy-start = (bf16[16,16,128]{2,1,0:T(8,128)(2,1)S(1)}, bf16[16,16,128]{2,1,0:T(8,128)(2,1)}, u32[]{:S(2)}) copy-start(bf16[16,16,128]{2,1,0:T(8,128)(2,1)} %q_ref.1) | copy-start | bytes 196612
  0.9 9.0 %copy-start.1 = (s32[32]{0:T(128)S(1)}, s32[32]{0:T(128)}, u32[]{:S(2)}) copy-start(s32[32]{0:T(128)} %param.7) | copy-start | bytes 388
  0.9 11.4 %collective-permute-start.2 = (bf16[128,128]{1,0:T(8,128)(2,1)S(1)}, bf16[128,128]{1,0:T(8,128)(2,1)S(1)}, u32[]{:S(2)}, u32[]{:S(2)}) collective-permute-start(bf16[128,128]{1,0:T(8,128)(2,1)S(1)} %own_tails.1.refs_0_), channel_id=1, source_target_pairs={{0,208},{16,224},{32,240},{48,0},{64,16},{80,32},{96,48},{112,64},... | collective-permute-start | bytes 98312 | tf_op jit(solution)/shard_map/ppermute | solution.py:24
  8.9 4.0 %collective-permute-start.1 = (bf16[128,128]{1,0:T(8,128)(2,1)S(1)}, bf16[128,128]{1,0:T(8,128)(2,1)S(1)}, u32[]{:S(2)}, u32[]{:S(2)}) collective-permute-start(bf16[128,128]{1,0:T(8,128)(2,1)S(1)} %own_tails.1.refs_0_), channel_id=1, source_target_pairs={{0,224},{16,240},{32,0},{48,16},{64,32},{80,48},{96,64},{112,80},{... | collective-permute-start | bytes 98312 | tf_op jit(solution)/shard_map/ppermute | solution.py:24
  9.4 4.9 %collective-permute-start = (bf16[128,128]{1,0:T(8,128)(2,1)S(1)}, bf16[128,128]{1,0:T(8,128)(2,1)S(1)}, u32[]{:S(2)}, u32[]{:S(2)}) collective-permute-start(bf16[128,128]{1,0:T(8,128)(2,1)S(1)} %own_tails.1.refs_0_), channel_id=1, source_target_pairs={{0,240},{16,0},{32,16},{48,32},{64,48},{80,64},{96,80},{112,96},{1... | collective-permute-start | bytes 98312 | tf_op jit(solution)/shard_map/ppermute | solution.py:24
  10.0 1.5 %copy-start.2 = (bf16[2048,2,128]{2,1,0:T(2,128)(2,1)S(1)}, bf16[2048,2,128]{2,1,0:T(2,128)(2,1)}, u32[]{:S(2)}) copy-start(bf16[2048,2,128]{2,1,0:T(2,128)(2,1)} %param.6) | copy-start | bytes 3145732
  14.5 10.1 %collective-permute-start.5 = (bf16[2,128,256]{2,1,0:T(8,128)(2,1)S(1)}, bf16[2,128,256]{2,1,0:T(8,128)(2,1)S(1)}, u32[]{:S(2)}, u32[]{:S(2)}) collective-permute-start(bf16[2,128,256]{2,1,0:T(8,128)(2,1)S(1)} %stack_tails.1.q_ref), channel_id=1, source_target_pairs={{0,248},{4,252},{8,0},{12,4},{16,8},{20,12},{24,16},{28,20},{32,24... | collective-permute-start | bytes 393224 | tf_op jit(solution)/shard_map/ppermute | solution.py:24
  19.9 6.3 %collective-permute-start.7 = (bf16[2,128,256]{2,1,0:T(8,128)(2,1)S(1)}, bf16[2,128,256]{2,1,0:T(8,128)(2,1)S(1)}, u32[]{:S(2)}, u32[]{:S(2)}) collective-permute-start(bf16[2,128,256]{2,1,0:T(8,128)(2,1)S(1)} %stack_tails.1.q_ref), channel_id=1, source_target_pairs={{0,244},{4,248},{8,252},{12,0},{16,4},{20,8},{24,12},{28,16},{32,2... | collective-permute-start | bytes 393224 | tf_op jit(solution)/shard_map/ppermute | solution.py:24
  20.7 7.8 %collective-permute-start.3 = (bf16[2,128,256]{2,1,0:T(8,128)(2,1)S(1)}, bf16[2,128,256]{2,1,0:T(8,128)(2,1)S(1)}, u32[]{:S(2)}, u32[]{:S(2)}) collective-permute-start(bf16[2,128,256]{2,1,0:T(8,128)(2,1)S(1)} %stack_tails.1.q_ref), channel_id=1, source_target_pairs={{0,252},{4,0},{8,4},{12,8},{16,12},{20,16},{24,20},{28,24},{32,28}... | collective-permute-start | bytes 393224 | tf_op jit(solution)/shard_map/ppermute | solution.py:24
  24.8 9.8 %collective-permute-start.6 = (s16[4,136,128]{2,1,0:T(8,128)(2,1)S(1)}, s16[4,136,128]{2,1,0:T(8,128)(2,1)S(1)}, u32[]{:S(2)}, u32[]{:S(2)}) collective-permute-start(s16[4,136,128]{2,1,0:T(8,128)(2,1)S(1)} %attend_2.1), channel_id=1, source_target_pairs={{0,8},{4,12},{8,16},{12,20},{16,24},{20,28},{24,32},{28,36},{32,40... | collective-permute-start | bytes 417800 | tf_op jit(solution)/shard_map/ppermute | solution.py:24
  26.6 8.7 %collective-permute-start.8 = (s16[4,136,128]{2,1,0:T(8,128)(2,1)S(1)}, s16[4,136,128]{2,1,0:T(8,128)(2,1)S(1)}, u32[]{:S(2)}, u32[]{:S(2)}) collective-permute-start(s16[4,136,128]{2,1,0:T(8,128)(2,1)S(1)} %attend_3.1), channel_id=1, source_target_pairs={{0,12},{4,16},{8,20},{12,24},{16,28},{20,32},{24,36},{28,40},{32,4... | collective-permute-start | bytes 417800 | tf_op jit(solution)/shard_map/ppermute | solution.py:24
  28.7 10.7 %collective-permute-start.4 = (s16[4,136,128]{2,1,0:T(8,128)(2,1)S(1)}, s16[4,136,128]{2,1,0:T(8,128)(2,1)S(1)}, u32[]{:S(2)}, u32[]{:S(2)}) collective-permute-start(s16[4,136,128]{2,1,0:T(8,128)(2,1)S(1)} %attend_1.1), channel_id=1, source_target_pairs={{0,4},{4,8},{8,12},{12,16},{16,20},{20,24},{24,28},{28,32},{32,36}... | collective-permute-start | bytes 417800 | tf_op jit(solution)/shard_map/ppermute | solution.py:24
  39.7 4.7 %collective-permute-start.9 = (s16[136,128]{1,0:T(8,128)(2,1)S(1)}, s16[136,128]{1,0:T(8,128)(2,1)S(1)}, u32[]{:S(2)}, u32[]{:S(2)}) collective-permute-start(s16[136,128]{1,0:T(8,128)(2,1)S(1)} %get-tuple-element.26), channel_id=1, source_target_pairs={{0,16},{16,32},{32,48},{48,64},{64,80},{80,96},{96,112},{112,128},... | collective-permute-start | bytes 104456 | tf_op jit(solution)/shard_map/ppermute | solution.py:24
  39.8 5.7 %collective-permute-start.10 = (s16[136,128]{1,0:T(8,128)(2,1)S(1)}, s16[136,128]{1,0:T(8,128)(2,1)S(1)}, u32[]{:S(2)}, u32[]{:S(2)}) collective-permute-start(s16[136,128]{1,0:T(8,128)(2,1)S(1)} %get-tuple-element.27), channel_id=1, source_target_pairs={{0,32},{16,48},{32,64},{48,80},{64,96},{80,112},{96,128},{112,144}... | collective-permute-start | bytes 104456 | tf_op jit(solution)/shard_map/ppermute | solution.py:24
  39.9 8.3 %collective-permute-start.11 = (s16[136,128]{1,0:T(8,128)(2,1)S(1)}, s16[136,128]{1,0:T(8,128)(2,1)S(1)}, u32[]{:S(2)}, u32[]{:S(2)}) collective-permute-start(s16[136,128]{1,0:T(8,128)(2,1)S(1)} %get-tuple-element.28), channel_id=1, source_target_pairs={{0,48},{16,64},{32,80},{48,96},{64,112},{80,128},{96,144},{112,160... | collective-permute-start | bytes 104456 | tf_op jit(solution)/shard_map/ppermute | solution.py:24
  48.3 4.6 %collective-permute-start.12 = (bf16[8,16,128]{2,1,0:T(8,128)(2,1)S(1)}, bf16[8,16,128]{2,1,0:T(8,128)(2,1)S(1)}, u32[]{:S(2)}, u32[]{:S(2)}) collective-permute-start(bf16[8,16,128]{2,1,0:T(8,128)(2,1)S(1)} %finish.1), channel_id=1, source_target_pairs={{0,128},{128,0},{1,129},{129,1},{2,130},{130,2},{3,131},{131,3},{4... | collective-permute-start | bytes 98312 | tf_op jit(solution)/shard_map/ppermute | solution.py:24

commit v6 on v5

--- a/solution.py
+++ b/solution.py
@@ -41,25 +41,17 @@
     live_ref[...] = jnp.where(row == 0, n_live, start - here)
 
 
-def own_kernel(kv_count, o_ref, q_ref, out_ref):
-    tail = TAIL
-    sharing = q_ref.shape[1] // kv_count
-    mine = q_ref[pl.ds(o_ref[0] * tail, tail)].astype(jnp.float32)
-    rows = [
-        mine[:, h * sharing : (h + 1) * sharing, :].reshape(tail * sharing, -1)
-        for h in range(kv_count)
-    ]
-    out_ref[...] = jnp.transpose(jnp.concatenate(rows, axis=0)).astype(out_ref.dtype)
-
-
 def stack_kernel(*refs):
     blocks, out_ref = refs[:-1], refs[-1]
-    kv_count = out_ref.shape[0]
-    wide = out_ref.shape[2] // len(blocks)
+    kv_count, dim, width = out_ref.shape
+    tail, heads, _ = blocks[0].shape
+    sharing = heads // kv_count
+    whole = [b[...].astype(jnp.float32) for b in blocks]
     for h in range(kv_count):
-        out_ref[h] = jnp.concatenate(
-            [b[:, h * wide : (h + 1) * wide] for b in blocks], axis=1
-        )
+        rows = [
+            w[:, h * sharing : (h + 1) * sharing, :].reshape(tail * sharing, dim) for w in whole
+        ]
+        out_ref[h] = jnp.transpose(jnp.concatenate(rows, axis=0)).astype(out_ref.dtype)
 
 
 def write_exact(ref, o, m, l):
@@ -234,14 +226,7 @@
     width = REACH * TAIL * sharing
     factor = math.log2(math.e) / math.sqrt(dim)
 
-    own = pl.pallas_call(
-        functools.partial(own_kernel, kv_count),
-        out_shape=jax.ShapeDtypeStruct((dim, lanes), queries.dtype),
-        in_specs=scalars() + on_chip(1),
-        out_specs=on_chip(1)[0],
-        compiler_params=room(4),
-        name="own_tails",
-    )(o.reshape(1).astype(jnp.int32), queries)
+    own = lax.dynamic_slice_in_dim(queries, o * TAIL, TAIL, 0)
     held = [own] + [shifted(own, ("outer", "z"), -j) for j in range(1, REACH)]
 
     live = pl.pallas_call(

time: 52.9 us -> 51.4 us (0.972); the launches traced: 53.6 us -> 51.2 us
  starting transfers between devices: 24.7 us -> 19.6 us
  waiting for transfers between devices: 22.5 us -> 25.3 us
    ppermute x13, starting transfers between devices: 24.7 us -> 19.6 us  [shifted(): return lax.ppermute(part, axes, [(i, (i + by) % size) for i in range(size)])]
    ppermute x13, waiting for transfers between devices: 22.5 us -> 25.3 us  [shifted(): return lax.ppermute(part, axes, [(i, (i + by) % size) for i in range(size)])]
  transfers between devices with their start and end apart: 13 -> 13, of which waited for: 11 -> 10; matrix products, arithmetic and copies ran while one was open for 4% -> 4% of each run, Pallas kernels for 4% -> 4%
where the time goes in v6:
time: 51.4 us; the launch traced here: 51.2 us
  waiting for transfers between devices  25.3 us (49%)
  starting transfers between devices  19.6 us (38%)
  local copies, waits for them, and re-layouts  3.17 us (6%)
  Pallas kernels  2.43 us (5%)
  other arithmetic  0.65 us (1%)
    ppermute x13, waiting for transfers between devices, shifted(): return lax.ppermute(part, axes, [(i, (i + by) % size) for i in range(size)])  25.3 us
    ppermute x13, starting transfers between devices, shifted(): return lax.ppermute(part, axes, [(i, (i + by) % size) for i in range(size)])  19.6 us
    unnamed x8, local copies, waits for them, and re-layouts  3.17 us
    pallas_call x4, Pallas kernels, body(): pl.pallas_call(functools.partial(attend_kernel, u, factor), out_shape=exa...  1.86 us
  transfers between devices with their start and end apart: 13, of which 10 were waited for; matrix products, arithmetic and copies ran while one was open for 4% of the time, Pallas kernels for 4%

profile of v6, /device:TPU:1, one launch (start us, length us, event | category | flops | bytes accessed | tf_op | source)
XLA Modules:
  0.0 51.2 jit_solution(13643187703388156143)
XLA Ops:
  0.0 0.0 copy-start
  0.0 0.8 %copy-done = bf16[16,16,128]{2,1,0:T(8,128)(2,1)S(1)} copy-done((bf16[16,16,128]{2,1,0:T(8,128)(2,1)S(1)}, bf16[16,16,128]{2,1,0:T(8,128)(2,1)}, u32[]{:S(2)}) %copy-start) | copy-done | bytes 65560
  0.8 0.0 copy-start.1
  0.8 7.9 %collective-permute-start.2 = (bf16[8,16,128]{2,1,0:T(8,128)(2,1)S(1)}, bf16[8,16,128]{2,1,0:T(8,128)(2,1)S(1)}, u32[]{:S(2)}, u32[]{:S(2)}) collective-permute-start(bf16[8,16,128]{2,1,0:T(8,128)(2,1)S(1)} %constant_dynamic-slice_fusion.refs_0_), channel_id=1, source_target_pairs={{0,208},{16,224},{32,240},{48,0},{64,16},{80,32},{96,48},{112,64},... | collective-permute-start | bytes 98312 | tf_op jit(solution)/shard_map/ppermute | solution.py:24
  8.7 0.6 %collective-permute-start.1 = (bf16[8,16,128]{2,1,0:T(8,128)(2,1)S(1)}, bf16[8,16,128]{2,1,0:T(8,128)(2,1)S(1)}, u32[]{:S(2)}, u32[]{:S(2)}) collective-permute-start(bf16[8,16,128]{2,1,0:T(8,128)(2,1)S(1)} %constant_dynamic-slice_fusion.refs_0_), channel_id=1, source_target_pairs={{0,224},{16,240},{32,0},{48,16},{64,32},{80,48},{96,64},{112,80},{... | collective-permute-start | bytes 98312 | tf_op jit(solution)/shard_map/ppermute | solution.py:24
  9.3 0.5 collective-permute-start
  9.7 0.0 copy-done.1
  9.7 0.1 mask.1.live_ref
  9.8 0.0 copy-start.2
  9.8 1.5 %copy.8 = bf16[2048,2,128]{2,0,1:T(8,128)(2,1)S(1)} copy(bf16[2048,2,128]{2,1,0:T(2,128)(2,1)} %param.5) | data formatting | bytes 2097152 | tf_op args[1]
  11.3 0.1 copy-done.2
  11.4 0.8 %copy.6 = bf16[2048,2,128]{0,2,1:T(8,128)(2,1)S(1)} copy(bf16[2048,2,128]{2,1,0:T(2,128)(2,1)S(1)} %copy-done.2) | data formatting | bytes 2097152 | tf_op args[2]
  12.2 0.0 collective-permute-done.2.refs_3_
  12.2 0.6 %collective-permute-done.1.refs_2_ = bf16[8,16,128]{2,1,0:T(8,128)(2,1)S(1)} collective-permute-done((bf16[8,16,128]{2,1,0:T(8,128)(2,1)S(1)}, bf16[8,16,128]{2,1,0:T(8,128)(2,1)S(1)}, u32[]{:S(2)}, u32[]{:S(2)}) %collective-permute-start.1) | collective-permute-done | bytes 32800 | tf_op jit(solution)/shard_map/ppermute | solution.py:24
  12.7 1.5 %collective-permute-done.refs_1_ = bf16[8,16,128]{2,1,0:T(8,128)(2,1)S(1)} collective-permute-done((bf16[8,16,128]{2,1,0:T(8,128)(2,1)S(1)}, bf16[8,16,128]{2,1,0:T(8,128)(2,1)S(1)}, u32[]{:S(2)}, u32[]{:S(2)}) %collective-permute-start) | collective-permute-done | bytes 32800 | tf_op jit(solution)/shard_map/ppermute | solution.py:24
  14.2 0.1 stack_tails.1.q_ref
  14.3 5.5 %collective-permute-start.5 = (bf16[2,128,256]{2,1,0:T(8,128)(2,1)S(1)}, bf16[2,128,256]{2,1,0:T(8,128)(2,1)S(1)}, u32[]{:S(2)}, u32[]{:S(2)}) collective-permute-start(bf16[2,128,256]{2,1,0:T(8,128)(2,1)S(1)} %stack_tails.1.q_ref), channel_id=1, source_target_pairs={{0,248},{4,252},{8,0},{12,4},{16,8},{20,12},{24,16},{28,20},{32,24... | collective-permute-start | bytes 393224 | tf_op jit(solution)/shard_map/ppermute | solution.py:24
  19.7 0.8 %collective-permute-start.7 = (bf16[2,128,256]{2,1,0:T(8,128)(2,1)S(1)}, bf16[2,128,256]{2,1,0:T(8,128)(2,1)S(1)}, u32[]{:S(2)}, u32[]{:S(2)}) collective-permute-start(bf16[2,128,256]{2,1,0:T(8,128)(2,1)S(1)} %stack_tails.1.q_ref), channel_id=1, source_target_pairs={{0,244},{4,248},{8,252},{12,0},{16,4},{20,8},{24,12},{28,16},{32,2... | collective-permute-start | bytes 393224 | tf_op jit(solution)/shard_map/ppermute | solution.py:24
  20.5 2.6 %collective-permute-start.3 = (bf16[2,128,256]{2,1,0:T(8,128)(2,1)S(1)}, bf16[2,128,256]{2,1,0:T(8,128)(2,1)S(1)}, u32[]{:S(2)}, u32[]{:S(2)}) collective-permute-start(bf16[2,128,256]{2,1,0:T(8,128)(2,1)S(1)} %stack_tails.1.q_ref), channel_id=1, source_target_pairs={{0,252},{4,0},{8,4},{12,8},{16,12},{20,16},{24,20},{28,24},{32,28}... | collective-permute-start | bytes 393224 | tf_op jit(solution)/shard_map/ppermute | solution.py:24
  23.2 1.2 %attend_0.1.refs_0_ = f32[4,136,128]{2,1,0:T(8,128)S(1)} custom-call(f32[8,128]{1,0:T(8,128)S(1)} %mask.1.live_ref, bf16[2,128,256]{2,1,0:T(8,128)(2,1)S(1)} %stack_tails.1.q_ref, bf16[2,2048,128]{2,1,0:T(8,128)(2,1)S(1)} %bitcast.5, bf16[2,128,2048]{2,1,0:T(8,128)(2,1)S(1)} %bitcast.9), custom_call_target="tpu_custom_call" | custom-call | flops 536870912 | bytes 2097152 | tf_op jit(solution)/shard_map/attend_0/pallas_call | solution.py:263
  24.4 0.0 collective-permute-done.5.q_ref
  24.4 0.1 attend_2.1
  24.6 0.1 collective-permute-start.6
  24.7 1.3 %collective-permute-done.7.q_ref = bf16[2,128,256]{2,1,0:T(8,128)(2,1)S(1)} collective-permute-done((bf16[2,128,256]{2,1,0:T(8,128)(2,1)S(1)}, bf16[2,128,256]{2,1,0:T(8,128)(2,1)S(1)}, u32[]{:S(2)}, u32[]{:S(2)}) %collective-permute-start.7) | collective-permute-done | bytes 131104 | tf_op jit(solution)/shard_map/ppermute | solution.py:24
  26.0 0.3 attend_3.1
  26.4 0.4 collective-permute-start.8
  26.8 1.6 %collective-permute-done.3.q_ref = bf16[2,128,256]{2,1,0:T(8,128)(2,1)S(1)} collective-permute-done((bf16[2,128,256]{2,1,0:T(8,128)(2,1)S(1)}, bf16[2,128,256]{2,1,0:T(8,128)(2,1)S(1)}, u32[]{:S(2)}, u32[]{:S(2)}) %collective-permute-start.3) | collective-permute-done | bytes 131104 | tf_op jit(solution)/shard_map/ppermute | solution.py:24
  28.4 0.1 attend_1.1
  28.5 0.1 collective-permute-start.4
  28.6 5.7 %collective-permute-done.6.refs_2_ = s16[4,136,128]{2,1,0:T(8,128)(2,1)S(1)} collective-permute-done((s16[4,136,128]{2,1,0:T(8,128)(2,1)S(1)}, s16[4,136,128]{2,1,0:T(8,128)(2,1)S(1)}, u32[]{:S(2)}, u32[]{:S(2)}) %collective-permute-start.6) | collective-permute-done | bytes 139296 | tf_op jit(solution)/shard_map/ppermute | solution.py:24
  34.4 0.0 collective-permute-done.8.refs_3_
  34.4 5.0 %collective-permute-done.4.refs_1_ = s16[4,136,128]{2,1,0:T(8,128)(2,1)S(1)} collective-permute-done((s16[4,136,128]{2,1,0:T(8,128)(2,1)S(1)}, s16[4,136,128]{2,1,0:T(8,128)(2,1)S(1)}, u32[]{:S(2)}, u32[]{:S(2)}) %collective-permute-start.4) | collective-permute-done | bytes 139296 | tf_op jit(solution)/shard_map/ppermute | solution.py:24
  39.4 0.3 merge_columns.1
  39.7 0.1 collective-permute-start.9
  39.8 0.1 collective-permute-start.10
  39.9 0.4 collective-permute-start.11
  40.3 4.6 %collective-permute-done.9.refs_1_ = s16[136,128]{1,0:T(8,128)(2,1)S(1)} collective-permute-done((s16[136,128]{1,0:T(8,128)(2,1)S(1)}, s16[136,128]{1,0:T(8,128)(2,1)S(1)}, u32[]{:S(2)}, u32[]{:S(2)}) %collective-permute-start.9) | collective-permute-done | bytes 34848 | tf_op jit(solution)/shard_map/ppermute | solution.py:24
  44.9 1.0 %collective-permute-done.10.refs_2_ = s16[136,128]{1,0:T(8,128)(2,1)S(1)} collective-permute-done((s16[136,128]{1,0:T(8,128)(2,1)S(1)}, s16[136,128]{1,0:T(8,128)(2,1)S(1)}, u32[]{:S(2)}, u32[]{:S(2)}) %collective-permute-start.10) | collective-permute-done | bytes 34848 | tf_op jit(solution)/shard_map/ppermute | solution.py:24
  45.9 3.1 %collective-permute-done.11.refs_3_ = s16[136,128]{1,0:T(8,128)(2,1)S(1)} collective-permute-done((s16[136,128]{1,0:T(8,128)(2,1)S(1)}, s16[136,128]{1,0:T(8,128)(2,1)S(1)}, u32[]{:S(2)}, u32[]{:S(2)}) %collective-permute-start.11) | collective-permute-done | bytes 34848 | tf_op jit(solution)/shard_map/ppermute | solution.py:24
  49.0 0.1 finish.1
  49.1 0.6 %collective-permute-start.12 = (bf16[8,16,128]{2,1,0:T(8,128)(2,1)S(1)}, bf16[8,16,128]{2,1,0:T(8,128)(2,1)S(1)}, u32[]{:S(2)}, u32[]{:S(2)}) collective-permute-start(bf16[8,16,128]{2,1,0:T(8,128)(2,1)S(1)} %finish.1), channel_id=1, source_target_pairs={{0,128},{128,0},{1,129},{129,1},{2,130},{130,2},{3,131},{131,3},{4... | collective-permute-start | bytes 98312 | tf_op jit(solution)/shard_map/ppermute | solution.py:24
  49.7 0.9 %collective-permute-done.12 = bf16[8,16,128]{2,1,0:T(8,128)(2,1)S(1)} collective-permute-done((bf16[8,16,128]{2,1,0:T(8,128)(2,1)S(1)}, bf16[8,16,128]{2,1,0:T(8,128)(2,1)S(1)}, u32[]{:S(2)}, u32[]{:S(2)}) %collective-permute-start.12) | collective-permute-done | bytes 32800 | tf_op jit(solution)/shard_map/ppermute | solution.py:24
  50.6 0.6 %pad_maximum_fusion = bf16[16,16,128]{2,1,0:T(8,128)(2,1)} fusion(bf16[8,16,128]{2,1,0:T(8,128)(2,1)S(1)} %get-tuple-element.30, bf16[8,16,128]{2,1,0:T(8,128)(2,1)S(1)} %get-tuple-element.29), kind=kLoop, calls=%fused_computation.1 | loop fusion | flops 32768 | bytes 131072 | tf_op jit(solution)/shard_map/concatenate | solution.py:300
  (2 shorter events, 0.0 us)
Async XLA Ops:
  0.0 0.8 %copy-start = (bf16[16,16,128]{2,1,0:T(8,128)(2,1)S(1)}, bf16[16,16,128]{2,1,0:T(8,128)(2,1)}, u32[]{:S(2)}) copy-start(bf16[16,16,128]{2,1,0:T(8,128)(2,1)} %param.4) | copy-start | bytes 196612
  0.8 8.9 %copy-start.1 = (s32[32]{0:T(128)S(1)}, s32[32]{0:T(128)}, u32[]{:S(2)}) copy-start(s32[32]{0:T(128)} %param.7) | copy-start | bytes 388
  0.8 11.3 %collective-permute-start.2 = (bf16[8,16,128]{2,1,0:T(8,128)(2,1)S(1)}, bf16[8,16,128]{2,1,0:T(8,128)(2,1)S(1)}, u32[]{:S(2)}, u32[]{:S(2)}) collective-permute-start(bf16[8,16,128]{2,1,0:T(8,128)(2,1)S(1)} %constant_dynamic-slice_fusion.refs_0_), channel_id=1, source_target_pairs={{0,208},{16,224},{32,240},{48,0},{64,16},{80,32},{96,48},{112,64},... | collective-permute-start | bytes 98312 | tf_op jit(solution)/shard_map/ppermute | solution.py:24
  8.7 4.0 %collective-permute-start.1 = (bf16[8,16,128]{2,1,0:T(8,128)(2,1)S(1)}, bf16[8,16,128]{2,1,0:T(8,128)(2,1)S(1)}, u32[]{:S(2)}, u32[]{:S(2)}) collective-permute-start(bf16[8,16,128]{2,1,0:T(8,128)(2,1)S(1)} %constant_dynamic-slice_fusion.refs_0_), channel_id=1, source_target_pairs={{0,224},{16,240},{32,0},{48,16},{64,32},{80,48},{96,64},{112,80},{... | collective-permute-start | bytes 98312 | tf_op jit(solution)/shard_map/ppermute | solution.py:24
  9.3 4.9 %collective-permute-start = (bf16[8,16,128]{2,1,0:T(8,128)(2,1)S(1)}, bf16[8,16,128]{2,1,0:T(8,128)(2,1)S(1)}, u32[]{:S(2)}, u32[]{:S(2)}) collective-permute-start(bf16[8,16,128]{2,1,0:T(8,128)(2,1)S(1)} %constant_dynamic-slice_fusion.refs_0_), channel_id=1, source_target_pairs={{0,240},{16,0},{32,16},{48,32},{64,48},{80,64},{96,80},{112,96},{1... | collective-permute-start | bytes 98312 | tf_op jit(solution)/shard_map/ppermute | solution.py:24
  9.8 1.5 %copy-start.2 = (bf16[2048,2,128]{2,1,0:T(2,128)(2,1)S(1)}, bf16[2048,2,128]{2,1,0:T(2,128)(2,1)}, u32[]{:S(2)}) copy-start(bf16[2048,2,128]{2,1,0:T(2,128)(2,1)} %param.6) | copy-start | bytes 3145732
  14.3 10.1 %collective-permute-start.5 = (bf16[2,128,256]{2,1,0:T(8,128)(2,1)S(1)}, bf16[2,128,256]{2,1,0:T(8,128)(2,1)S(1)}, u32[]{:S(2)}, u32[]{:S(2)}) collective-permute-start(bf16[2,128,256]{2,1,0:T(8,128)(2,1)S(1)} %stack_tails.1.q_ref), channel_id=1, source_target_pairs={{0,248},{4,252},{8,0},{12,4},{16,8},{20,12},{24,16},{28,20},{32,24... | collective-permute-start | bytes 393224 | tf_op jit(solution)/shard_map/ppermute | solution.py:24
  19.7 6.3 %collective-permute-start.7 = (bf16[2,128,256]{2,1,0:T(8,128)(2,1)S(1)}, bf16[2,128,256]{2,1,0:T(8,128)(2,1)S(1)}, u32[]{:S(2)}, u32[]{:S(2)}) collective-permute-start(bf16[2,128,256]{2,1,0:T(8,128)(2,1)S(1)} %stack_tails.1.q_ref), channel_id=1, source_target_pairs={{0,244},{4,248},{8,252},{12,0},{16,4},{20,8},{24,12},{28,16},{32,2... | collective-permute-start | bytes 393224 | tf_op jit(solution)/shard_map/ppermute | solution.py:24
  20.5 7.8 %collective-permute-start.3 = (bf16[2,128,256]{2,1,0:T(8,128)(2,1)S(1)}, bf16[2,128,256]{2,1,0:T(8,128)(2,1)S(1)}, u32[]{:S(2)}, u32[]{:S(2)}) collective-permute-start(bf16[2,128,256]{2,1,0:T(8,128)(2,1)S(1)} %stack_tails.1.q_ref), channel_id=1, source_target_pairs={{0,252},{4,0},{8,4},{12,8},{16,12},{20,16},{24,20},{28,24},{32,28}... | collective-permute-start | bytes 393224 | tf_op jit(solution)/shard_map/ppermute | solution.py:24
  24.6 9.8 %collective-permute-start.6 = (s16[4,136,128]{2,1,0:T(8,128)(2,1)S(1)}, s16[4,136,128]{2,1,0:T(8,128)(2,1)S(1)}, u32[]{:S(2)}, u32[]{:S(2)}) collective-permute-start(s16[4,136,128]{2,1,0:T(8,128)(2,1)S(1)} %attend_2.1), channel_id=1, source_target_pairs={{0,8},{4,12},{8,16},{12,20},{16,24},{20,28},{24,32},{28,36},{32,40... | collective-permute-start | bytes 417800 | tf_op jit(solution)/shard_map/ppermute | solution.py:24
  26.4 8.0 %collective-permute-start.8 = (s16[4,136,128]{2,1,0:T(8,128)(2,1)S(1)}, s16[4,136,128]{2,1,0:T(8,128)(2,1)S(1)}, u32[]{:S(2)}, u32[]{:S(2)}) collective-permute-start(s16[4,136,128]{2,1,0:T(8,128)(2,1)S(1)} %attend_3.1), channel_id=1, source_target_pairs={{0,12},{4,16},{8,20},{12,24},{16,28},{20,32},{24,36},{28,40},{32,4... | collective-permute-start | bytes 417800 | tf_op jit(solution)/shard_map/ppermute | solution.py:24
  28.5 10.9 %collective-permute-start.4 = (s16[4,136,128]{2,1,0:T(8,128)(2,1)S(1)}, s16[4,136,128]{2,1,0:T(8,128)(2,1)S(1)}, u32[]{:S(2)}, u32[]{:S(2)}) collective-permute-start(s16[4,136,128]{2,1,0:T(8,128)(2,1)S(1)} %attend_1.1), channel_id=1, source_target_pairs={{0,4},{4,8},{8,12},{12,16},{16,20},{20,24},{24,28},{28,32},{32,36}... | collective-permute-start | bytes 417800 | tf_op jit(solution)/shard_map/ppermute | solution.py:24
  39.7 5.2 %collective-permute-start.9 = (s16[136,128]{1,0:T(8,128)(2,1)S(1)}, s16[136,128]{1,0:T(8,128)(2,1)S(1)}, u32[]{:S(2)}, u32[]{:S(2)}) collective-permute-start(s16[136,128]{1,0:T(8,128)(2,1)S(1)} %get-tuple-element.26), channel_id=1, source_target_pairs={{0,16},{16,32},{32,48},{48,64},{64,80},{80,96},{96,112},{112,128},... | collective-permute-start | bytes 104456 | tf_op jit(solution)/shard_map/ppermute | solution.py:24
  39.8 6.1 %collective-permute-start.10 = (s16[136,128]{1,0:T(8,128)(2,1)S(1)}, s16[136,128]{1,0:T(8,128)(2,1)S(1)}, u32[]{:S(2)}, u32[]{:S(2)}) collective-permute-start(s16[136,128]{1,0:T(8,128)(2,1)S(1)} %get-tuple-element.27), channel_id=1, source_target_pairs={{0,32},{16,48},{32,64},{48,80},{64,96},{80,112},{96,128},{112,144}... | collective-permute-start | bytes 104456 | tf_op jit(solution)/shard_map/ppermute | solution.py:24
  39.9 9.1 %collective-permute-start.11 = (s16[136,128]{1,0:T(8,128)(2,1)S(1)}, s16[136,128]{1,0:T(8,128)(2,1)S(1)}, u32[]{:S(2)}, u32[]{:S(2)}) collective-permute-start(s16[136,128]{1,0:T(8,128)(2,1)S(1)} %get-tuple-element.28), channel_id=1, source_target_pairs={{0,48},{16,64},{32,80},{48,96},{64,112},{80,128},{96,144},{112,160... | collective-permute-start | bytes 104456 | tf_op jit(solution)/shard_map/ppermute | solution.py:24
  49.1 1.5 %collective-permute-start.12 = (bf16[8,16,128]{2,1,0:T(8,128)(2,1)S(1)}, bf16[8,16,128]{2,1,0:T(8,128)(2,1)S(1)}, u32[]{:S(2)}, u32[]{:S(2)}) collective-permute-start(bf16[8,16,128]{2,1,0:T(8,128)(2,1)S(1)} %finish.1), channel_id=1, source_target_pairs={{0,128},{128,0},{1,129},{129,1},{2,130},{130,2},{3,131},{131,3},{4... | collective-permute-start | bytes 98312 | tf_op jit(solution)/shard_map/ppermute | solution.py:24
